TPU v7x, 128 devices: a whole 4x4x4 slice. The times are simulated.
128 devices in a mesh: sx: 16 (over y, z), sy: 8 (over x, core).
Axes of the slice: x: 4, y: 4, z: 4, core: 2. Of those that a mesh axis runs over, the one named last changes fastest.
Arguments:
- rhs: float32 [12288, 16384], P('sx', 'sy')
- sigma: float32 [12288, 16384], P('sx', 'sy'), may hold values from 0.05 to 2
- tile_list: int32 [262144], P(('sx', 'sy')), may hold values from 0 to 12287, as said below
- tile_owner: int32 [262144, 1], P(('sx', 'sy')), may hold values from 0 to 127, as said below
- schur_blocks: bfloat16 [128, 128, 128], P(('sx', 'sy')), as said below
Outputs:
- corrected: float32 [12288, 16384], P('sx', 'sy')
- iface_residual: float32 [262144, 128], P(('sx', 'sy'))
- iface_direction: float32 [262144, 128], P(('sx', 'sy'))
Inputs may be any that keep to these rules, and one draw needn't show every extreme that they name: `tile_owner`: within the 2048 tiles of one subdomain no owner appears more than 32 times. `tile_list`: every listed run touches its block's rim: it lies in the block's first or last row, or is the first or last run of its row. Runs may repeat. `schur_blocks`: each block is symmetric.
All inputs are finite; a program needn't handle non-finite values.
Results may differ from a plain program's by a relative error of at most 0.012.
Values may be sent and summed in bfloat16 or wider, within the bound.
No kernel may reach another device: no remote copies, remote signals or barrier semaphores. Data moves between devices by JAX's collectives and lax.ppermute only.
A program may use at most 128 MiB of HBM per device.

v0:
```python
import jax
import jax.numpy as jnp
from jax import lax
from jax.sharding import PartitionSpec as P


def padded_2(shard, sides, width):
    for axis, dim in sides:
        devices, length = (lax.axis_size(axis), shard.shape[dim])
        up = [(i, (i + 1) % devices) for i in range(devices - 1)]
        down = [(j, i) for i, j in up]
        last = lax.slice_in_dim(shard, length - width, length, axis=dim)
        initial = lax.slice_in_dim(shard, 0, width, axis=dim)
        before = lax.ppermute(last, axis, up)
        after = lax.ppermute(initial, axis, down)
        shard = jnp.concatenate([before, shard, after], axis=dim)
    return shard


def apply_op(field, sigma):
    padded = padded_2(field, (("sx", 0), ("sy", 1)), 1)
    beside = padded[2:, 1:-1] + padded[:-2, 1:-1] + padded[1:-1, 2:] + padded[1:-1, :-2]
    return (4.0 + sigma) * field - beside


def per_device(rhs, sigma, tile_list, tile_owner, schur_blocks):
    width = schur_blocks.shape[2]
    dinv = 1.0 / (4.0 + sigma)
    first = 0.6111111 * dinv * rhs
    second = first + 2.75 * dinv * (rhs - apply_op(first, sigma))
    field_res = rhs - apply_op(second, sigma)
    r_tiles = field_res.reshape(-1, width)[tile_list]
    p_half = r_tiles.astype(jnp.bfloat16)
    rr_old = lax.psum(jnp.sum(r_tiles * r_tiles), ("sx", "sy"))
    owner = tile_owner[:, 0]
    count_tiles = tile_list.shape[0]
    nsx = lax.axis_size("sx")
    nsy = lax.axis_size("sy")
    devices = nsx * nsy
    capacity = 2 * count_tiles // devices
    onehot = (owner[:, None] == jnp.arange(devices, dtype=jnp.int32)[None, :]).astype(jnp.int32)
    ranks = jnp.cumsum(onehot, axis=0) - onehot
    slot = jnp.sum(ranks * onehot, axis=1)
    target = owner * capacity + slot
    buffer = jnp.zeros((devices * capacity, width), jnp.bfloat16).at[target].set(p_half)
    own_block = schur_blocks[0]
    boxed = buffer.reshape(devices, capacity, width)
    boxes = lax.all_to_all(boxed, ("sx", "sy"), split_axis=0, concat_axis=0, tiled=True)
    flat = boxes.reshape(-1, width)
    prod = jnp.dot(flat, own_block, preferred_element_type=jnp.float32)
    products = prod.astype(jnp.bfloat16).reshape(boxes.shape)
    returned = lax.all_to_all(products, ("sx", "sy"), split_axis=0, concat_axis=0, tiled=True)
    q_tiles = returned.reshape(-1, width)[target].astype(jnp.float32)
    pq_sum = lax.psum(jnp.sum(r_tiles * q_tiles), ("sx", "sy"))
    alpha = rr_old / pq_sum
    iface_residual = r_tiles - alpha * q_tiles
    rr_new = lax.psum(jnp.sum(iface_residual * iface_residual), ("sx", "sy"))
    iface_direction = iface_residual + rr_new / rr_old * r_tiles
    corrected = second.reshape(-1, width).at[tile_list].add(alpha * r_tiles).reshape(second.shape)
    return (corrected, iface_residual, iface_direction)


def solution(mesh):
    in_specs = (
        P("sx", "sy"),
        P("sx", "sy"),
        P(("sx", "sy")),
        P(("sx", "sy"), None),
        P(("sx", "sy"), None, None),
    )
    out_specs = (P("sx", "sy"), P(("sx", "sy"), None), P(("sx", "sy"), None))
    return jax.shard_map(
        per_device, mesh=mesh, in_specs=in_specs, out_specs=out_specs, check_vma=False
    )
```

profile of v0, /device:TPU:1, one launch (start us, length us, event | category | flops | bytes accessed | tf_op | source)
XLA Modules:
  0.0 314.7 jit_solution(15464946492275688065)
XLA Ops:
  0.6 0.0 copy-start
  0.7 6.0 %multiply_multiply_fusion = f32[768,2048]{1,0:T(8,128)S(1)} fusion(f32[768,2048]{1,0:T(8,128)} %param.5, f32[768,2048]{1,0:T(8,128)} %param.6), kind=kLoop, calls=%fused_computation.32 | loop fusion | flops 6291456 | bytes 18874368 | tf_op jit(solution)/shard_map/mul | solution.py:29
  6.6 0.0 copy-start.2
  6.6 2.7 copy-done.2
  9.3 1.3 collective-permute-start
  10.6 5.0 %collective-permute-start.1 = (f32[1,2048]{1,0:T(1,128)S(1)}, f32[1,2048]{1,0:T(1,128)S(1)}, u32[]{:S(2)}, u32[]{:S(2)}) collective-permute-start(f32[1,2048]{1,0:T(1,128)S(1)} %get-tuple-element.15), channel_id=1, source_target_pairs={{0,8},{8,16},{16,24},{24,32},{32,40},{40,48},{48,56},{56,64},{64,7... | collective-permute-start | bytes 24584 | tf_op jit(solution)/shard_map/ppermute | solution.py:14
  15.7 0.1 copy.9
  15.8 0.3 fusion.18
  16.1 0.0 slice-start
  16.2 0.1 broadcast_add_fusion
  16.2 0.3 copy.10
  16.6 0.0 slice-start.1
  16.6 1.5 pad_maximum_fusion.21
  18.1 3.4 %collective-permute-start.2 = (f32[770,1]{1,0:T(8,128)S(1)}, f32[770,1]{1,0:T(8,128)S(1)}, u32[]{:S(2)}, u32[]{:S(2)}) collective-permute-start(f32[770,1]{1,0:T(8,128)S(1)} %get-tuple-element.11), channel_id=1, source_target_pairs={{1,0},{2,1},{3,2},{4,3},{5,4},{6,5},{7,6},{9,8},{10,9},{11,10},{12... | collective-permute-start | bytes 9248 | tf_op jit(solution)/shard_map/ppermute | solution.py:15
  21.5 3.1 collective-permute-start.3
  24.6 0.0 slice-start.2
  24.6 0.6 fusion.15
  25.3 0.0 slice-start.3
  25.3 2.9 collective-permute-done.2
  28.2 1.2 collective-permute-done.3
  29.4 11.9 %fusion.9 = f32[768,2048]{1,0:T(8,128)S(1)} fusion(f32[768,2048]{1,0:T(8,128)S(1)} %bitcast.23, f32[768,2048]{1,0:T(8,128)} %param.5, f32[770,1]{1,0:T(8,128)S(1)} %collective-permute-done.3, f32[1,2048]{1,0:T(1,128)S(1)} %collective-permute-done, f32[1,2048]{1,0:T(1,128)S(1)} %collective-permute-done.1, f32[770,1]{1,0:T(8,128)S(1)} %collective-permute-done.2, ...), kind=kLoop, calls=%fused_computation.22 | loop fusion | flops 29884416 | bytes 25188368 | tf_op jit(solution)/shard_map/add | solution.py:30
  41.3 0.0 copy-start.1
  41.3 0.0 copy-start.5
  41.4 1.3 collective-permute-start.4
  42.7 4.7 %collective-permute-start.5 = (f32[1,2048]{1,0:T(1,128)S(1)}, f32[1,2048]{1,0:T(1,128)S(1)}, u32[]{:S(2)}, u32[]{:S(2)}) collective-permute-start(f32[1,2048]{1,0:T(1,128)S(1)} %get-tuple-element.13), channel_id=1, source_target_pairs={{0,8},{8,16},{16,24},{24,32},{32,40},{40,48},{48,56},{56,64},{64,7... | collective-permute-start | bytes 24584 | tf_op jit(solution)/shard_map/ppermute | solution.py:14
  47.4 0.7 collective-permute-done.5
  48.1 0.2 pad_maximum_fusion.18
  48.3 1.9 collective-permute-start.6
  50.2 5.2 %collective-permute-start.7 = (f32[770,1]{1,0:T(8,128)S(1)}, f32[770,1]{1,0:T(8,128)S(1)}, u32[]{:S(2)}, u32[]{:S(2)}) collective-permute-start(f32[770,1]{1,0:T(8,128)S(1)} %get-tuple-element.10), channel_id=1, source_target_pairs={{0,1},{1,2},{2,3},{3,4},{4,5},{5,6},{6,7},{8,9},{9,10},{10,11},{11... | collective-permute-start | bytes 9248 | tf_op jit(solution)/shard_map/ppermute | solution.py:14
  55.5 3.5 %collective-permute-done.6 = f32[770,1]{1,0:T(8,128)S(1)} collective-permute-done((f32[770,1]{1,0:T(8,128)S(1)}, f32[770,1]{1,0:T(8,128)S(1)}, u32[]{:S(2)}, u32[]{:S(2)}) %collective-permute-start.6) | collective-permute-done | bytes 3112 | tf_op jit(solution)/shard_map/ppermute | solution.py:15
  59.0 1.2 collective-permute-done.7
  60.2 12.7 %fusion.2 = f32[768,2048]{1,0:T(8,128)} fusion(f32[768,2048]{1,0:T(8,128)S(1)} %bitcast.25, f32[770,1]{1,0:T(8,128)S(1)} %collective-permute-done.7, f32[1,2048]{1,0:T(1,128)S(1)} %collective-permute-done.4, f32[768,2048]{1,0:T(8,128)S(1)} %fusion.9, f32[1,2048]{1,0:T(1,128)S(1)} %collective-permute-done.5, f32[770,1]{1,0:T(8,128)S(1)} %collective-permute-done.6, ...), kind=kLoop, calls=%fused_computation.7 | loop fusion | flops 23592960 | bytes 25188368 | tf_op jit(solution)/shard_map/sub | solution.py:31
  72.9 7.1 %reshape.45 = f32[12288,128]{1,0:T(8,128)} reshape(f32[768,2048]{1,0:T(8,128)} %fusion.2) | data formatting | bytes 12582912 | tf_op jit(solution)/shard_map/reshape | solution.py:32
  80.0 8.2 %gather_fusion = f32[2048,128]{1,0:T(8,128)S(1)} fusion(f32[12288,128]{1,0:T(8,128)} %reshape.45, s32[2048]{0:T(1024)S(1)} %get-tuple-element.17), kind=kCustom, calls=%fused_computation | custom fusion | bytes 2105344 | tf_op jit(solution)/shard_map/gather | solution.py:32
  88.2 6.2 %scatter_custom_fusion = bf16[4096,128]{1,0:T(8,128)(2,1)S(1)} fusion(s32[2048]{0:T(1024)S(1)} %bitcast.32, f32[2048,128]{1,0:T(8,128)S(1)} %gather_fusion, bf16[]{:T(256)} %constant.8.clone.1), kind=kCustom, calls=%fused_computation.52 | custom fusion | flops 262144 | bytes 2097154 | tf_op jit(solution)/shard_map/scatter | solution.py:45
  94.5 35.0 %all_to_all.10 = bf16[128,32,128]{2,1,0:T(8,128)(2,1)S(1)} all-to-all(bf16[128,32,128]{2,1,0:T(8,128)(2,1)S(1)} %bitcast.27), channel_id=1, replica_groups=mesh['sx'=16,'sy'=8] {'sx','sy'}, dimensions={0} | all-to-all | bytes 2097152 | tf_op jit(solution)/shard_map/all_to_all | solution.py:48
  129.5 1.4 convolution_convert_fusion
  130.9 4.4 %all-to-all-start.1 = ((bf16[128,32,128]{2,1,0:T(8,128)(2,1)}), bf16[128,32,128]{2,1,0:T(8,128)(2,1)S(1)}, u32[]{:S(2)}, u32[]{:S(2)}) async-start(bf16[128,32,128]{2,1,0:T(8,128)(2,1)} %bitcast.10), calls=%async_computation.1 | async-start | bytes 2097152 | tf_op jit(solution)/shard_map/all_to_all | solution.py:52
  135.3 7.1 %reshape.44 = f32[12288,128]{1,0:T(8,128)} reshape(f32[768,2048]{1,0:T(8,128)} %copy-done.1) | data formatting | bytes 12582912 | tf_op jit(solution)/shard_map/reshape | solution.py:59
  142.4 12.2 %all-to-all-done.1 = bf16[128,32,128]{2,1,0:T(8,128)(2,1)S(1)} async-done(((bf16[128,32,128]{2,1,0:T(8,128)(2,1)}), bf16[128,32,128]{2,1,0:T(8,128)(2,1)S(1)}, u32[]{:S(2)}, u32[]{:S(2)}) %all-to-all-start.1) | async-done | bytes 1048608 | tf_op jit(solution)/shard_map/all_to_all | solution.py:52
  154.7 6.2 %gather_fusion.1 = bf16[2048,128]{1,0:T(8,128)(2,1)S(1)} fusion(bf16[4096,128]{1,0:T(8,128)(2,1)S(1)} %bitcast.26, s32[2048]{0:T(1024)S(1)} %broadcast_clamp_fusion), kind=kCustom, calls=%fused_computation.1 | custom fusion | bytes 1056768 | tf_op jit(solution)/shard_map/gather | solution.py:53
  160.8 0.9 fusion.12
  161.7 62.6 %all-reduce = (f32[]{:T(128)}, f32[]{:T(128)}) all-reduce(f32[]{:T(128)} %get-tuple-element.4, f32[]{:T(128)} %get-tuple-element.3), channel_id=1, replica_groups=mesh['sx'=16,'sy'=8] {'sx','sy'}, use_global_device_ids=true, to_apply=%region_1.0 | all-reduce | flops 2 | bytes 16 | tf_op jit(solution)/shard_map/psum | solution.py:34
  225.7 0.9 multiply_reduce_fusion
  226.6 62.8 %psum.23 = f32[]{:T(128)} all-reduce(f32[]{:T(128)} %get-tuple-element.7), channel_id=1, replica_groups=mesh['sx'=16,'sy'=8] {'sx','sy'}, use_global_device_ids=true, to_apply=%region_10.11 | all-reduce | flops 1 | bytes 8 | tf_op jit(solution)/shard_map/psum | solution.py:57
  290.8 15.8 %scatter_custom_fusion.1 = f32[12288,128]{1,0:T(8,128)} fusion(f32[12288,128]{1,0:T(8,128)} %reshape.44, s32[2048]{0:T(1024)S(1)} %get-tuple-element.18, f32[2048,128]{1,0:T(8,128)S(1)} %gather_fusion, f32[]{:T(128)S(6)} %div.14), kind=kCustom, calls=%fused_computation.44 | custom fusion | flops 524288 | bytes 7340036 | tf_op jit(solution)/shard_map/scatter-add | solution.py:59
  306.5 7.1 %reshape.51 = f32[768,2048]{1,0:T(8,128)} reshape(f32[12288,128]{1,0:T(8,128)} %scatter_custom_fusion.1) | data formatting | bytes 12582912 | tf_op jit(solution)/shard_map/reshape | solution.py:59
  313.6 1.1 multiply_add_fusion
  (24 shorter events, 0.1 us)
Async XLA Ops:
  0.6 128.9 %copy-start = (bf16[1,128,128]{2,1,0:T(8,128)(2,1)S(1)}, bf16[1,128,128]{2,1,0:T(8,128)(2,1)}, u32[]{:S(2)}) copy-start(bf16[1,128,128]{2,1,0:T(8,128)(2,1)} %param.9) | copy-start | bytes 98308
  0.6 15.0 %copy-start.4 = (s32[2048,1]{0,1:T(1,128)S(1)}, s32[2048,1]{0,1:T(1,128)}, u32[]{:S(2)}) copy-start(s32[2048,1]{0,1:T(1,128)} %param.8) | copy-start | bytes 24580
  6.6 2.7 copy-start.2
  9.3 7.3 %collective-permute-start = (f32[1,2048]{1,0:T(1,128)S(1)}, f32[1,2048]{1,0:T(1,128)S(1)}, u32[]{:S(2)}, u32[]{:S(2)}) collective-permute-start(f32[1,2048]{1,0:T(1,128)S(1)} %get-tuple-element.16), channel_id=1, source_target_pairs={{8,0},{16,8},{24,16},{32,24},{40,32},{48,40},{56,48},{64,56},{72,6... | collective-permute-start | bytes 24584 | tf_op jit(solution)/shard_map/ppermute | solution.py:15
  10.6 6.0 %collective-permute-start.1 = (f32[1,2048]{1,0:T(1,128)S(1)}, f32[1,2048]{1,0:T(1,128)S(1)}, u32[]{:S(2)}, u32[]{:S(2)}) collective-permute-start(f32[1,2048]{1,0:T(1,128)S(1)} %get-tuple-element.15), channel_id=1, source_target_pairs={{0,8},{8,16},{16,24},{24,32},{32,40},{40,48},{48,56},{56,64},{64,7... | collective-permute-start | bytes 24584 | tf_op jit(solution)/shard_map/ppermute | solution.py:14
  16.1 13.2 %slice-start = ((s8[6291456]{0:T(1024)(128)(4,1)}), s8[2097152]{0:T(1024)(128)(4,1)S(1)}, s32[]{:S(2)}) async-start(s8[6291456]{0:T(1024)(128)(4,1)} %bitcast.22), calls=%async_computation.2 | async-start | bytes 4194304
  16.6 12.8 %slice-start.1 = ((s8[6291456]{0:T(1024)(128)(4,1)}), s8[4194304]{0:T(1024)(128)(4,1)S(1)}, s32[]{:S(2)}) async-start(s8[6291456]{0:T(1024)(128)(4,1)} %bitcast.22), calls=%async_computation.3 | async-start | bytes 8388608
  18.1 10.1 %collective-permute-start.2 = (f32[770,1]{1,0:T(8,128)S(1)}, f32[770,1]{1,0:T(8,128)S(1)}, u32[]{:S(2)}, u32[]{:S(2)}) collective-permute-start(f32[770,1]{1,0:T(8,128)S(1)} %get-tuple-element.11), channel_id=1, source_target_pairs={{1,0},{2,1},{3,2},{4,3},{5,4},{6,5},{7,6},{9,8},{10,9},{11,10},{12... | collective-permute-start | bytes 9248 | tf_op jit(solution)/shard_map/ppermute | solution.py:15
  21.5 7.9 %collective-permute-start.3 = (f32[770,1]{1,0:T(8,128)S(1)}, f32[770,1]{1,0:T(8,128)S(1)}, u32[]{:S(2)}, u32[]{:S(2)}) collective-permute-start(f32[770,1]{1,0:T(8,128)S(1)} %get-tuple-element.12), channel_id=1, source_target_pairs={{0,1},{1,2},{2,3},{3,4},{4,5},{5,6},{6,7},{8,9},{9,10},{10,11},{11... | collective-permute-start | bytes 9248 | tf_op jit(solution)/shard_map/ppermute | solution.py:14
  24.6 35.6 %slice-start.2 = ((s8[6291456]{0:T(1024)(128)(4,1)}), s8[4194304]{0:T(1024)(128)(4,1)S(1)}, s32[]{:S(2)}) async-start(s8[6291456]{0:T(1024)(128)(4,1)} %bitcast.24), calls=%async_computation.4 | async-start | bytes 8388608
  25.3 35.0 %slice-start.3 = ((s8[6291456]{0:T(1024)(128)(4,1)}), s8[2097152]{0:T(1024)(128)(4,1)S(1)}, s32[]{:S(2)}) async-start(s8[6291456]{0:T(1024)(128)(4,1)} %bitcast.24), calls=%async_computation.5 | async-start | bytes 4194304
  41.3 18.9 %copy-start.1 = (f32[768,2048]{1,0:T(8,128)}, f32[768,2048]{1,0:T(8,128)S(1)}, u32[]{:S(2)}) copy-start(f32[768,2048]{1,0:T(8,128)S(1)} %fusion.9) | copy-start | bytes 18874372
  41.3 14.2 %copy-start.5 = (s32[2048]{0:T(1024)S(1)}, s32[2048]{0:T(1024)}, u32[]{:S(2)}) copy-start(s32[2048]{0:T(1024)} %param.7) | copy-start | bytes 24580
  41.4 6.0 %collective-permute-start.4 = (f32[1,2048]{1,0:T(1,128)S(1)}, f32[1,2048]{1,0:T(1,128)S(1)}, u32[]{:S(2)}, u32[]{:S(2)}) collective-permute-start(f32[1,2048]{1,0:T(1,128)S(1)} %get-tuple-element.14), channel_id=1, source_target_pairs={{8,0},{16,8},{24,16},{32,24},{40,32},{48,40},{56,48},{64,56},{72,6... | collective-permute-start | bytes 24584 | tf_op jit(solution)/shard_map/ppermute | solution.py:15
  42.7 5.5 %collective-permute-start.5 = (f32[1,2048]{1,0:T(1,128)S(1)}, f32[1,2048]{1,0:T(1,128)S(1)}, u32[]{:S(2)}, u32[]{:S(2)}) collective-permute-start(f32[1,2048]{1,0:T(1,128)S(1)} %get-tuple-element.13), channel_id=1, source_target_pairs={{0,8},{8,16},{16,24},{24,32},{32,40},{40,48},{48,56},{56,64},{64,7... | collective-permute-start | bytes 24584 | tf_op jit(solution)/shard_map/ppermute | solution.py:14
  48.3 10.7 %collective-permute-start.6 = (f32[770,1]{1,0:T(8,128)S(1)}, f32[770,1]{1,0:T(8,128)S(1)}, u32[]{:S(2)}, u32[]{:S(2)}) collective-permute-start(f32[770,1]{1,0:T(8,128)S(1)} %get-tuple-element.9), channel_id=1, source_target_pairs={{1,0},{2,1},{3,2},{4,3},{5,4},{6,5},{7,6},{9,8},{10,9},{11,10},{12... | collective-permute-start | bytes 9248 | tf_op jit(solution)/shard_map/ppermute | solution.py:15
  50.2 10.0 %collective-permute-start.7 = (f32[770,1]{1,0:T(8,128)S(1)}, f32[770,1]{1,0:T(8,128)S(1)}, u32[]{:S(2)}, u32[]{:S(2)}) collective-permute-start(f32[770,1]{1,0:T(8,128)S(1)} %get-tuple-element.10), channel_id=1, source_target_pairs={{0,1},{1,2},{2,3},{3,4},{4,5},{5,6},{6,7},{8,9},{9,10},{10,11},{11... | collective-permute-start | bytes 9248 | tf_op jit(solution)/shard_map/ppermute | solution.py:14
  130.9 23.8 %all-to-all-start.1 = ((bf16[128,32,128]{2,1,0:T(8,128)(2,1)}), bf16[128,32,128]{2,1,0:T(8,128)(2,1)S(1)}, u32[]{:S(2)}, u32[]{:S(2)}) async-start(bf16[128,32,128]{2,1,0:T(8,128)(2,1)} %bitcast.10), calls=%async_computation.1 | async-start | bytes 2097152 | tf_op jit(solution)/shard_map/all_to_all | solution.py:52
  226.6 87.0 %copy-start.3 = (f32[2048,128]{1,0:T(8,128)}, f32[2048,128]{1,0:T(8,128)S(1)}, u32[]{:S(2)}) copy-start(f32[2048,128]{1,0:T(8,128)S(1)} %get-tuple-element.8) | copy-start | bytes 3145732
where the time goes:
time: 316 us; the launch traced here: 315 us
  blocking collectives  161 us (51%)
  other arithmetic  58.2 us (18%)
  local copies, waits for them, and re-layouts  38.9 us (12%)
  starting transfers between devices  30.4 us (10%)
  waiting for transfers between devices  21.8 us (7%)
  between operations  3.62 us (1%)
    psum x1, blocking collectives, per_device(): rr_new = lax.psum(jnp.sum(iface_residual * iface_residual), ('sx', 'sy'))  62.8 us
    psum x1, blocking collectives, per_device(): rr_old = lax.psum(jnp.sum(r_tiles * r_tiles), ('sx', 'sy'))  62.6 us
    all_to_all x1, blocking collectives, per_device(): lax.all_to_all(boxed, ('sx', 'sy'), split_axis=0, concat_axis=0, tiled=True)  35 us
    ppermute x4, starting transfers between devices, padded_2(): before = lax.ppermute(last, axis, up)  18 us
    scatter-add x1, other arithmetic, per_device(): second.reshape(-1, width).at[tile_list].add(alpha * r_tiles)  15.8 us
    reshape x2, local copies, waits for them, and re-layouts, per_device(): second.reshape(-1, width).at[tile_list].add(alpha * r_tiles)  14.1 us
    sub x1, other arithmetic, per_device(): field_res = rhs - apply_op(second, sigma)  12.7 us
    all_to_all x1, waiting for transfers between devices, per_device(): lax.all_to_all(products, ('sx', 'sy'), split_axis=0, concat_axis=0, tiled...  12.2 us
  transfers between devices with their start and end apart: 9, of which 6 were waited for; matrix products, arithmetic and copies ran while one was open for 3% of the time, Pallas kernels for 0%

commit v1 on v0

v1 whole, which is shorter than its diff:
```python
import jax
import jax.numpy as jnp
from jax import lax
from jax.experimental import pallas as pl
from jax.experimental.pallas import tpu as pltpu
from jax.sharding import Mesh, PartitionSpec as P

F32 = jnp.float32
BF16 = jnp.bfloat16
R, C, W = 768, 2048, 128
T = 2048
CAP = 32
NG = 64
RIM = 2 * R + 32
PR = 72
OFF = 16
FR = R + 2 * OFF
ROWS = ("y", "z")
COLS = ("x", "c")
ALL = ("y", "z", "x", "c")
CHIPS = ("y", "z", "x")
VM = pl.BlockSpec(memory_space=pltpu.VMEM)
SM = pl.BlockSpec(memory_space=pltpu.SMEM)
ANY = pl.BlockSpec(memory_space=pl.ANY)
PARAMS = pltpu.CompilerParams(vmem_limit_bytes=56 << 20)


def sds(shape, dtype=F32):
    return jax.ShapeDtypeStruct(shape, dtype)


def pack_kernel(s_ref, out_ref):
    s = s_ref[0].astype(F32)
    top, bot = s[:64], s[64:]
    i = lax.broadcasted_iota(jnp.int32, (64, W), 0)
    j = lax.broadcasted_iota(jnp.int32, (64, W), 1)
    d = j - i
    body = jnp.where((d >= 0) & (d < 64), top, bot)
    cross = jnp.where(d == 64, top, 0.0)
    half = jnp.sum(cross, axis=0, keepdims=True)
    row = half + pltpu.roll(half, 64, axis=1)
    full = jnp.concatenate([body, jnp.broadcast_to(row, (8, W))], axis=0).astype(BF16)
    for k in range(NG):
        out_ref[k] = full


def pack(blocks):
    return pl.pallas_call(pack_kernel, out_shape=sds((NG, PR, W), BF16), in_specs=[VM], out_specs=VM, compiler_params=PARAMS, name="pack")(blocks)


def dense_kernel(x_ref, s_ref, xp_ref, sp_ref, xn_ref, sn_ref, out_ref, f_ref):
    t = 4.0 + s_ref[...]
    dinv = 1.0 / t
    x = x_ref[...]
    f = 0.6111111 * dinv * x
    f_ref[8:72] = f
    f_ref[0:8] = 0.6111111 * (1.0 / (4.0 + sp_ref[...])) * xp_ref[...]
    f_ref[72:80] = 0.6111111 * (1.0 / (4.0 + sn_ref[...])) * xn_ref[...]
    beside = f_ref[9:73] + f_ref[7:71] + pltpu.roll(f, C - 1, axis=1) + pltpu.roll(f, 1, axis=1)
    out_ref[...] = f + 2.75 * dinv * (x - (t * f - beside))


def dense(rhs, sigma):
    main = pl.BlockSpec((64, C), lambda i: (i, 0))
    prev = pl.BlockSpec((8, C), lambda i: (jnp.maximum(8 * i - 1, 0), 0))
    succ = pl.BlockSpec((8, C), lambda i: (jnp.minimum(8 * i + 8, R // 8 - 1), 0))
    return pl.pallas_call(
        dense_kernel, grid=(R // 64,), out_shape=sds((R, C)), in_specs=[main, main, prev, prev, succ, succ], out_specs=main,
        scratch_shapes=[pltpu.VMEM((80, C), F32)], compiler_params=PARAMS, name="dense")(rhs, sigma, rhs, sigma, rhs, sigma)


def rim_kernel(has_ref, xl, sl, xr, sr, xt, st, xb, sb, hup, hdn, hcl, hcr, r_out, secl, secr, sect, secb, X, D, F, S, X2, D2, F2, S2):
    up, down, left, right = (has_ref[k] for k in range(4))

    def strip(x, s, c0, hc, lanes, alive, sec, base, lo):
        lane = lax.broadcasted_iota(jnp.int32, (1, 2 * W), 1)

        def put(v, rows, k):
            a = jnp.where(lane == lanes[0], hc[rows, k:k + 1], v)
            return jnp.where(lane == lanes[1], hc[rows, k + 1:k + 2], a)

        own, above, under = slice(OFF, OFF + R), slice(OFF - 2, OFF), slice(OFF + R, OFF + R + 2)
        cols = slice(c0, c0 + 2 * W)
        for ref, k, src in ((X, 0, x), (D, 2, s)):
            ref[0:OFF] = jnp.zeros((OFF, 2 * W), F32)
            ref[OFF + R:FR] = jnp.zeros((OFF, 2 * W), F32)
            ref[above] = put(hup[k:k + 2, cols], above, k)
            ref[own] = put(src[...], own, k)
            ref[under] = put(hdn[k:k + 2, cols], under, k)
        F[...] = 0.6111111 * (1.0 / (4.0 + D[...])) * X[...]
        mid = slice(8, FR - 8)
        t = 4.0 + D[mid]
        f = F[mid]
        beside = F[9:FR - 7] + F[7:FR - 9] + pltpu.roll(f, 2 * W - 1, axis=1) + pltpu.roll(f, 1, axis=1)
        sec_v = f + 2.75 * (1.0 / t) * (X[mid] - (t * f - beside))
        row = lax.broadcasted_iota(jnp.int32, (FR - 16, 1), 0) + (8 - OFF)
        keep = ((row >= 0) | (up > 0)) & ((row < R) | (down > 0))
        keep = keep & (((lane != lanes[0]) & (lane != lanes[1])) | (alive > 0))
        S[mid] = jnp.where(keep, sec_v, 0.0)
        g = S[own]
        beside = S[OFF + 1:OFF + R + 1] + S[OFF - 1:OFF + R - 1] + pltpu.roll(g, 2 * W - 1, axis=1) + pltpu.roll(g, 1, axis=1)
        res = X[own] - ((4.0 + D[own]) * g - beside)
        r_out[base:base + R] = res[:, lo:lo + W]
        sec[...] = g[:, lo:lo + W]

    strip(xl, sl, 0, hcl, (2 * W - 2, 2 * W - 1), left, secl, 0, 0)
    strip(xr, sr, C - 2 * W, hcr, (0, 1), right, secr, R, W)

    def edge(x, s, own, halo, h, at, alive, gone, sec, sec_rows, base):
        for ref, k, src in ((X2, 0, x), (D2, 2, s)):
            ref[...] = jnp.zeros((32, C), F32)
            ref[own] = src[...]
            ref[halo] = h[k:k + 2]
        F2[...] = 0.6111111 * (1.0 / (4.0 + D2[...])) * X2[...]
        mid = slice(8, 24)
        t = 4.0 + D2[mid]
        f = F2[mid]
        beside = F2[9:25] + F2[7:23] + pltpu.roll(f, C - 1, axis=1) + pltpu.roll(f, 1, axis=1)
        sec_v = f + 2.75 * (1.0 / t) * (X2[mid] - (t * f - beside))
        row = lax.broadcasted_iota(jnp.int32, (16, 1), 0) + 8
        S2[mid] = jnp.where(gone(row) & (alive == 0), 0.0, sec_v)
        sec[...] = S2[sec_rows]
        g = S2[mid]
        sides = pltpu.roll(g, C - 1, axis=1) + pltpu.roll(g, 1, axis=1)
        S2[0:1] = sides[at - 8:at - 7]
        a = slice(at, at + 1)
        res = X2[a] - ((4.0 + D2[a]) * S2[a] - (S2[at + 1:at + 2] + S2[at - 1:at] + S2[0:1]))
        for k in range(C // W):
            r_out[base + k:base + k + 1] = res[:, k * W:(k + 1) * W]

    edge(xt, st, slice(16, 32), slice(14, 16), hup, 16, up, lambda row: row < 16, sect, slice(16, 24), 2 * R)
    edge(xb, sb, slice(0, 16), slice(16, 18), hdn, 15, down, lambda row: row >= 16, secb, slice(8, 16), 2 * R + 16)


def rim(has, rhs, sigma, hup, hdn, hcl, hcr):
    left = pl.BlockSpec((R, 2 * W), lambda i: (0, 0))
    right = pl.BlockSpec((R, 2 * W), lambda i: (0, C // (2 * W) - 1))
    top = pl.BlockSpec((16, C), lambda i: (0, 0))
    bottom = pl.BlockSpec((16, C), lambda i: (R // 16 - 1, 0))

    def whole(shape):
        return pl.BlockSpec(shape, lambda i: (0,) * len(shape))

    outs = [(RIM, W), (R, W), (R, W), (8, C), (8, C)]
    return pl.pallas_call(
        rim_kernel, grid=(1,), out_shape=[sds(s) for s in outs],
        in_specs=[SM, left, left, right, right, top, top, bottom, bottom, whole((4, C)), whole((4, C)), whole((FR, 4)), whole((FR, 4))],
        out_specs=[whole(s) for s in outs],
        scratch_shapes=[pltpu.VMEM((FR, 2 * W), F32)] * 4 + [pltpu.VMEM((32, C), F32)] * 4,
        compiler_params=PARAMS, name="rim")(has, rhs, sigma, rhs, sigma, rhs, sigma, rhs, sigma, hup, hdn, hcl, hcr)


def place_kernel(run_ref, slot_ref, r_ref, tiles_ref, slots_ref):
    slots_ref[...] = jnp.zeros_like(slots_ref)

    def body(b, carry):
        for u in range(16):
            t = b * 16 + u
            row = r_ref[pl.ds(run_ref[t], 1), :]
            tiles_ref[pl.ds(t, 1), :] = row
            slots_ref[pl.ds(slot_ref[t], 1), :] = row
        return carry

    lax.fori_loop(0, T // 16, body, 0)


def place(run, slot, r_rim):
    return pl.pallas_call(place_kernel, out_shape=[sds((T, W)), sds((2 * NG * CAP, W))], in_specs=[SM, SM, VM], out_specs=[VM, VM],
                          compiler_params=PARAMS, name="place")(run, slot, r_rim)


def product_kernel(first, slots_ref, blk_ref, *refs):
    if first:
        q_ref, sums_ref, v_ref = refs
    else:
        prev_ref, q_ref, sums_ref = refs
    i = lax.broadcasted_iota(jnp.int32, (64, W), 0)
    j = lax.broadcasted_iota(jnp.int32, (64, W), 1)
    d = j - i
    band = jnp.where((d >= 0) & (d < 64), 1.0, 0.0)
    mask_top = jnp.where(d == 0, 0.5, band).astype(BF16)
    mask_bot = jnp.where(d == 64, 0.5, 1.0 - band).astype(BF16)

    def fold(v):
        return jnp.sum(v.reshape(CAP // 8, 8, W), axis=0)

    scale = 1.0 if first else prev_ref[3, 0:1, :]

    def body(g, carry):
        rr, pq, vv, ra, qa = carry
        rows = pl.ds(pl.multiple_of(g * CAP, CAP), CAP)
        r = slots_ref[rows, :]
        half = r.astype(BF16)
        b = blk_ref[g, 0:64, :]
        u = jnp.concatenate([b * mask_top, b * mask_bot], axis=0)
        cross = blk_ref[g, 64:72, :].astype(F32)
        swapped = pltpu.roll(half.astype(F32), 64, axis=1)
        q = jnp.dot(half, u, preferred_element_type=F32)
        q = q + lax.dot_general(half, u, (((1,), (1,)), ((), ())), preferred_element_type=F32)
        q = q + (swapped.reshape(CAP // 8, 8, W) * cross[None]).reshape(CAP, W)
        q = q.astype(BF16).astype(F32)
        q_ref[rows, :] = q
        rr = rr + fold(r * r)
        pq = pq + fold(r * q)
        if first:
            ra = ra + fold(jnp.abs(r))
            qa = qa + fold(jnp.abs(q))
        else:
            v = q * scale
            vv = vv + fold(v * v)
        return rr, pq, vv, ra, qa

    zero = jnp.zeros((8, W), F32)
    rr, pq, vv, ra, qa = lax.fori_loop(0, NG, body, (zero,) * 5, unroll=8)
    if first:
        ra, qa = jnp.sum(ra), jnp.sum(qa)
        ok = (qa > 0.0) & (ra > 0.0)
        a0 = jnp.full((1, W), jnp.where(ok, ra, 1.0)) / jnp.full((1, W), jnp.where(ok, qa, 1.0))

        def second_pass(k, acc):
            v = q_ref[pl.ds(pl.multiple_of(k * 64, 64), 64), :] * a0
            return acc + jnp.sum((v * v).reshape(8, 8, W), axis=0)

        vv = lax.fori_loop(0, NG * CAP // 64, second_pass, zero, unroll=8)
        sums_ref[0], sums_ref[1], sums_ref[2] = rr, pq, vv
        sums_ref[3] = jnp.broadcast_to(a0, (8, W))
    else:
        rows = [jnp.sum(v + prev_ref[k], axis=0, keepdims=True) for k, v in enumerate((rr, pq, vv))]
        full = jnp.concatenate(rows + [scale], axis=0)
        for k in range(2 * NG):
            sums_ref[k] = full


def product_first(slots, blocks):
    spec = pl.BlockSpec((NG * CAP, W), lambda i: (0, 0))

    def kernel(s, b, q, sums):
        product_kernel(True, s, b, q, sums, None)

    return pl.pallas_call(kernel, grid=(1,), out_shape=[sds((NG * CAP, W)), sds((4, 8, W))],
                          in_specs=[spec, pl.BlockSpec((NG, PR, W), lambda i: (0, 0, 0))],
                          out_specs=[spec, pl.BlockSpec((4, 8, W), lambda i: (0, 0, 0))], compiler_params=PARAMS, name="product_a")(slots, blocks)


def product_second(slots, blocks, prev):
    def kernel(s, b, p, q, sums):
        product_kernel(False, s, b, p, q, sums)

    return pl.pallas_call(kernel, grid=(1,), out_shape=[sds((NG * CAP, W)), sds((2 * NG, 4, W))],
                          in_specs=[pl.BlockSpec((NG * CAP, W), lambda i: (1, 0)), pl.BlockSpec((NG, PR, W), lambda i: (0, 0, 0)),
                                    pl.BlockSpec((4, 8, W), lambda i: (0, 0, 0))],
                          out_specs=[pl.BlockSpec((NG * CAP, W), lambda i: (0, 0)), pl.BlockSpec((2 * NG, 4, W), lambda i: (0, 0, 0))],
                          compiler_params=PARAMS, name="product_b")(slots, blocks, prev)


def order_kernel(slot_ref, qa_ref, qb_ref, out_ref, q_ref):
    q_ref[0:NG * CAP] = qa_ref[...]
    q_ref[NG * CAP:] = qb_ref[...]

    def body(b, carry):
        for u in range(16):
            t = b * 16 + u
            out_ref[pl.ds(t, 1), :] = q_ref[pl.ds(slot_ref[t], 1), :]
        return carry

    lax.fori_loop(0, T // 16, body, 0)


def order(slot, qa, qb):
    return pl.pallas_call(order_kernel, out_shape=sds((T, W)), in_specs=[SM, VM, VM], out_specs=VM,
                          scratch_shapes=[pltpu.VMEM((2 * NG * CAP, W), F32)], compiler_params=PARAMS, name="order")(slot, qa, qb)


CH = 8
TC = T // CH


def final_kernel(red_ref, r_ref, q_ref, rim_ref, cnt_ref, secl, secr, sect, secb, field_ref, out_ref, res_ref, dir_ref, coef, bl, br, bt, bb, sems):
    step = pl.program_id(0)
    inner = slice(W, C - W)
    copies = [
        pltpu.make_async_copy(bl, out_ref.at[:, 0:W], sems.at[0]),
        pltpu.make_async_copy(br, out_ref.at[:, C - W:C], sems.at[1]),
        pltpu.make_async_copy(bt.at[:, inner], out_ref.at[0:8, inner], sems.at[2]),
        pltpu.make_async_copy(bb.at[:, inner], out_ref.at[R - 8:R, inner], sems.at[3]),
    ]

    @pl.when(step == 0)
    def _():
        rr = jnp.sum(red_ref[:, 0, :])
        pq = jnp.sum(red_ref[:, 1, :])
        alpha = jnp.full((1, W), rr) / jnp.full((1, W), pq)
        t = alpha / red_ref[:, 3, :]
        qq = jnp.sum(t * t * red_ref[:, 2, :])
        rr_new = rr - 2.0 * alpha * pq + qq
        coef[0:1] = alpha
        coef[1:2] = rr_new / rr
        bl[...] = secl[...] + alpha * (cnt_ref[0:R] * rim_ref[0:R])
        br[...] = secr[...] + alpha * (cnt_ref[R:2 * R] * rim_ref[R:2 * R])
        bt[...] = sect[...]
        bb[...] = secb[...]
        for k in range(1, C // W - 1):
            lanes = slice(k * W, (k + 1) * W)
            a = slice(2 * R + k, 2 * R + k + 1)
            bt[0:1, lanes] = sect[0:1, lanes] + alpha * (cnt_ref[a] * rim_ref[a])
            b = slice(2 * R + 16 + k, 2 * R + 17 + k)
            bb[7:8, lanes] = secb[7:8, lanes] + alpha * (cnt_ref[b] * rim_ref[b])
        for c in copies:
            c.start()

    r = r_ref[...]
    res = r - coef[0:1] * q_ref[...]
    res_ref[...] = res
    dir_ref[...] = res + coef[1:2] * r

    @pl.when(step == CH - 1)
    def _():
        for c in copies:
            c.wait()


def final(red, r_tiles, q_tiles, r_rim, cnt, secl, secr, sect, secb, field):
    def whole(shape):
        return pl.BlockSpec(shape, lambda i: (0,) * len(shape))

    chunk = pl.BlockSpec((TC, W), lambda i: (i, 0))
    return pl.pallas_call(
        final_kernel, grid=(CH,), out_shape=[sds((R, C)), sds((T, W)), sds((T, W))],
        in_specs=[whole((2 * NG, 4, W)), chunk, chunk, whole((RIM, W)), whole((RIM, W)), whole((R, W)), whole((R, W)), whole((8, C)), whole((8, C)), ANY],
        out_specs=[ANY, chunk, chunk],
        scratch_shapes=[pltpu.VMEM((8, W), F32), pltpu.VMEM((R, W), F32), pltpu.VMEM((R, W), F32), pltpu.VMEM((8, C), F32), pltpu.VMEM((8, C), F32),
                        pltpu.SemaphoreType.DMA((4,))],
        input_output_aliases={9: 0}, compiler_params=PARAMS, name="final")(red, r_tiles, q_tiles, r_rim, cnt, secl, secr, sect, secb, field)


def per_device(rhs, sigma, tile_list, tile_owner, schur_blocks):
    core = lax.axis_index("c")
    packed = pack(schur_blocks)
    mine = lax.all_to_all(packed, CHIPS, 0, 0, tiled=True)
    theirs = lax.ppermute(mine, "c", [(0, 1), (1, 0)])
    nrow, ncol = 16, 8
    up = [(i, i + 1) for i in range(nrow - 1)]
    down = [(i + 1, i) for i in range(nrow - 1)]
    hup = lax.ppermute(jnp.concatenate([rhs[-2:], sigma[-2:]]), ROWS, up)
    hdn = lax.ppermute(jnp.concatenate([rhs[:2], sigma[:2]]), ROWS, down)

    def cols(sl):
        a = jnp.concatenate([hup[0:2, sl], rhs[:, sl], hdn[0:2, sl]], axis=0)
        b = jnp.concatenate([hup[2:4, sl], sigma[:, sl], hdn[2:4, sl]], axis=0)
        return jnp.concatenate([a.T, b.T], axis=0)

    rightward = [(i, i + 1) for i in range(ncol - 1)]
    leftward = [(i + 1, i) for i in range(ncol - 1)]
    hcl = lax.ppermute(cols(slice(C - 2, C)), COLS, rightward)
    hcr = lax.ppermute(cols(slice(0, 2)), COLS, leftward)
    hcl = jnp.pad(hcl.T, ((OFF - 2, OFF - 2), (0, 0)))
    hcr = jnp.pad(hcr.T, ((OFF - 2, OFF - 2), (0, 0)))
    row_at = lax.axis_index(ROWS)
    col_at = lax.axis_index(COLS)
    has = jnp.stack([row_at > 0, row_at < nrow - 1, col_at > 0, col_at < ncol - 1]).astype(jnp.int32)
    r_rim, secl, secr, sect, secb = rim(has, rhs, sigma, hup, hdn, hcl, hcr)
    runs = C // W
    trow, tcol = tile_list // runs, tile_list % runs
    run = jnp.where(tcol == 0, trow, jnp.where(tcol == runs - 1, R + trow, jnp.where(trow == 0, 2 * R + tcol, 2 * R + 16 + tcol)))
    owner = tile_owner[:, 0]
    onehot = (owner[:, None] == jnp.arange(2 * NG, dtype=jnp.int32)[None, :]).astype(jnp.int32)
    ranks = jnp.cumsum(onehot, axis=0) - onehot
    rank = jnp.sum(ranks * onehot, axis=1)
    slot = (((owner & 1) ^ core) * NG + (owner >> 1)) * CAP + rank
    hits = (jnp.arange(RIM, dtype=jnp.int32)[:, None] == run[None, :]).astype(BF16)
    cnt = jnp.dot(hits, jnp.ones((T, W), BF16), preferred_element_type=F32)
    r_tiles, slots = place(run, slot, r_rim)
    qa, part = product_first(slots, mine)
    qb, sums = product_second(slots, theirs, part)
    red = lax.all_to_all(sums, ALL, 0, 0, tiled=True)
    q_tiles = order(slot, qa, qb)
    field = dense(rhs, sigma)
    return tuple(final(red, r_tiles, q_tiles, r_rim, cnt, secl, secr, sect, secb, field))


def solution(mesh):
    grid = Mesh(mesh.devices.reshape(4, 4, 4, 2), ("y", "z", "x", "c"))
    in_specs = (P(ROWS, COLS), P(ROWS, COLS), P(ALL), P(ALL, None), P(ALL, None, None))
    out_specs = (P(ROWS, COLS), P(ALL, None), P(ALL, None))
    return jax.shard_map(per_device, mesh=grid, in_specs=in_specs, out_specs=out_specs, check_vma=False)
```

time: 316 us -> 114 us (0.36)
  blocking collectives: 161 us -> 0 us
  other arithmetic: 58.2 us -> 2.68 us
  Pallas kernels: 0 us -> 52.1 us
  local copies, waits for them, and re-layouts: 38.9 us -> 9.91 us
  waiting for transfers between devices: 21.8 us -> 15 us
    psum x2 -> x0, blocking collectives: 125 us -> none  [the longest x1 62.8 us: per_device(): rr_new = lax.psum(jnp.sum(iface_residual * iface_residual), ('sx', 'sy'))]
    pallas_call x0 -> x8, Pallas kernels: none -> 52.1 us  [the longest x1 13.5 us: dense(): pl.pallas_call(dense_kernel, grid=(R // 64,), out_shape=sds((R, C)), in_s...]
    all_to_all x1 -> x0, blocking collectives: 35 us -> none  [per_device(): lax.all_to_all(boxed, ('sx', 'sy'), split_axis=0, concat_axis=0, tiled=True)]
    reshape x3 -> x0, local copies, waits for them, and re-layouts: 21.2 us -> none  [the longest x2 14.1 us: per_device(): second.reshape(-1, width).at[tile_list].add(alpha * r_tiles)]
    scatter-add x1 -> x0, other arithmetic: 15.8 us -> none  [per_device(): second.reshape(-1, width).at[tile_list].add(alpha * r_tiles)]
    gather x2 -> x0, local copies, waits for them, and re-layouts: 14.4 us -> none  [the longest x1 8.24 us: per_device(): r_tiles = field_res.reshape(-1, width)[tile_list]]
    sub x1 -> x0, other arithmetic: 12.7 us -> none  [per_device(): field_res = rhs - apply_op(second, sigma)]
    add x2 -> x1, other arithmetic: 13 us -> 0.62 us  [per_device(): slot = ((owner & 1 ^ core) * NG + (owner >> 1)) * CAP + rank]
  transfers between devices with their start and end apart: 9 -> 7, of which waited for: 6 -> 2; matrix products, arithmetic and copies ran while one was open for 3% -> 12% of each run, Pallas kernels for 0% -> 35%
where the time goes in v1:
time: 114 us; the launch traced here: 113 us
  Pallas kernels  52.1 us (46%)
  starting transfers between devices  29.3 us (26%)
  waiting for transfers between devices  15 us (13%)
  local copies, waits for them, and re-layouts  9.91 us (9%)
  matrix products  3.2 us (3%)
  other arithmetic  2.68 us (2%)
    pallas_call x1, Pallas kernels, dense(): pl.pallas_call(dense_kernel, grid=(R // 64,), out_shape=sds((R, C)), in_s...  13.5 us
    all_to_all x1, waiting for transfers between devices, per_device(): mine = lax.all_to_all(packed, CHIPS, 0, 0, tiled=True)  12.6 us
    all_to_all x1, starting transfers between devices, per_device(): mine = lax.all_to_all(packed, CHIPS, 0, 0, tiled=True)  11.7 us
    pallas_call x1, Pallas kernels, final(): pl.pallas_call(final_kernel, grid=(CH,), out_shape=[sds((R, C)), sds((T,...  7.37 us
    pallas_call x1, Pallas kernels, rim(): pl.pallas_call(rim_kernel, grid=(1,), out_shape=[sds(s) for s in outs], i...  7.03 us
    pallas_call x1, Pallas kernels, place(): pl.pallas_call(place_kernel, out_shape=[sds((T, W)), sds((2 * NG * CAP, W...  6.51 us
    pallas_call x1, Pallas kernels, product_first(): pl.pallas_call(kernel, grid=(1,), out_shape=[sds((NG * CAP, W)), sds((4,...  5.53 us
    pallas_call x1, Pallas kernels, product_second(): pl.pallas_call(kernel, grid=(1,), out_shape=[sds((NG * CAP, W)), sds((2 *...  5.37 us
  transfers between devices with their start and end apart: 7, of which 2 were waited for; matrix products, arithmetic and copies ran while one was open for 12% of the time, Pallas kernels for 35%

profile of v1, /device:TPU:1, one launch (start us, length us, event | category | flops | bytes accessed | tf_op | source)
XLA Modules:
  0.0 113.1 jit_solution(6278470396371960826)
XLA Ops:
  0.6 1.0 fusion.13
  1.6 4.4 %collective-permute-start = (f32[4,2048]{1,0:T(4,128)S(1)}, f32[4,2048]{1,0:T(4,128)S(1)}, u32[]{:S(2)}, u32[]{:S(2)}) collective-permute-start(f32[4,2048]{1,0:T(4,128)S(1)} %pad_maximum_fusion), channel_id=1, source_target_pairs={{0,8},{8,16},{16,24},{24,32},{32,40},{40,48},{48,56},{56,64},{64,7... | collective-permute-start | bytes 98312 | tf_op jit(solution)/shard_map/ppermute | solution.py:344
  6.0 1.3 %collective-permute-start.1 = (f32[4,2048]{1,0:T(4,128)S(1)}, f32[4,2048]{1,0:T(4,128)S(1)}, u32[]{:S(2)}, u32[]{:S(2)}) collective-permute-start(f32[4,2048]{1,0:T(4,128)S(1)} %pad_maximum_fusion.1), channel_id=1, source_target_pairs={{8,0},{16,8},{24,16},{32,24},{40,32},{48,40},{56,48},{64,56},{72,6... | collective-permute-start | bytes 98312 | tf_op jit(solution)/shard_map/ppermute | solution.py:345
  7.3 1.9 %pack.1 = bf16[64,72,128]{2,1,0:T(8,128)(2,1)} custom-call(bf16[1,128,128]{2,1,0:T(8,128)(2,1)} %s_ref.2), custom_call_target="tpu_custom_call" | custom-call | tf_op jit(solution)/shard_map/pack/pallas_call | solution.py:48
  9.2 11.7 %all-to-all-start = ((bf16[64,72,128]{2,1,0:T(8,128)(2,1)}), bf16[64,72,128]{2,1,0:T(8,128)(2,1)S(1)}, u32[]{:S(2)}, u32[]{:S(2)}) async-start(bf16[64,72,128]{2,1,0:T(8,128)(2,1)} %pack.1), calls=%async_computation | async-start | bytes 2359296 | tf_op jit(solution)/shard_map/all_to_all | solution.py:339
  20.9 0.8 copy.12
  21.7 0.3 fusion.4
  22.2 0.3 copy.13
  22.6 0.6 fusion.3
  23.2 1.3 %fusion.11 = (f32[768,2]{1,0:T(8,128)S(1)}, f32[768,2]{1,0:T(8,128)S(1)}) fusion(f32[768,2048]{1,0:T(8,128)} %xn_ref.1), kind=kLoop, calls=%fused_computation.34 | loop fusion | bytes 24576 | tf_op jit(solution)/shard_map/slice | solution.py:348
  24.5 1.3 %fusion.12 = (f32[768,2]{1,0:T(8,128)S(1)}, f32[768,2]{1,0:T(8,128)S(1)}) fusion(f32[768,2048]{1,0:T(8,128)} %sn_ref.1), kind=kLoop, calls=%fused_computation.35 | loop fusion | bytes 24576 | tf_op jit(solution)/shard_map/slice | solution.py:349
  25.8 0.6 multiply_add_fusion
  26.4 0.1 copy.30
  26.6 0.2 copy.28
  26.7 0.2 copy.31
  26.9 0.2 copy.29
  27.0 12.6 %all-to-all-done.b = bf16[64,72,128]{2,1,0:T(8,128)(2,1)S(1)} async-done(((bf16[64,72,128]{2,1,0:T(8,128)(2,1)}), bf16[64,72,128]{2,1,0:T(8,128)(2,1)S(1)}, u32[]{:S(2)}, u32[]{:S(2)}) %all-to-all-start) | async-done | bytes 1179680 | tf_op jit(solution)/shard_map/all_to_all | solution.py:339
  39.6 2.6 %collective-permute-start.4 = (bf16[64,72,128]{2,1,0:T(8,128)(2,1)S(1)}, bf16[64,72,128]{2,1,0:T(8,128)(2,1)S(1)}, u32[]{:S(2)}, u32[]{:S(2)}) collective-permute-start(bf16[64,72,128]{2,1,0:T(8,128)(2,1)S(1)} %all-to-all-done.b), channel_id=1, source_target_pairs={{0,1},{1,0},{2,3},{3,2},{4,5},{5,4},{6,7},{7,6},{8,9},{9,8},{10,11... | collective-permute-start | bytes 3538952 | tf_op jit(solution)/shard_map/ppermute | solution.py:340
  42.3 0.1 copy.22
  42.4 0.1 copy.25
  42.5 0.1 copy.18
  42.6 0.1 copy.15
  42.7 0.1 copy.23
  42.8 0.1 copy.26
  42.9 0.1 copy.19
  43.0 0.1 copy.16
  43.1 0.1 maximum_bitcast_fusion
  43.2 0.1 maximum_bitcast_fusion.1
  43.3 0.2 copy.20
  43.6 0.1 maximum_bitcast_fusion.3
  43.7 0.2 copy.27
  43.9 1.9 %collective-permute-start.3 = (f32[4,772]{0,1:T(8,128)S(1)}, f32[4,772]{0,1:T(8,128)S(1)}, u32[]{:S(2)}, u32[]{:S(2)}) collective-permute-start(f32[4,772]{0,1:T(8,128)S(1)} %copy.27), channel_id=1, source_target_pairs={{1,0},{2,1},{3,2},{4,3},{5,4},{6,5},{7,6},{9,8},{10,9},{11,10},{12... | collective-permute-start | bytes 37064 | tf_op jit(solution)/shard_map/ppermute | solution.py:355
  45.8 3.6 %collective-permute-start.2 = (f32[4,772]{0,1:T(8,128)S(1)}, f32[4,772]{0,1:T(8,128)S(1)}, u32[]{:S(2)}, u32[]{:S(2)}) collective-permute-start(f32[4,772]{0,1:T(8,128)S(1)} %copy.20), channel_id=1, source_target_pairs={{0,1},{1,2},{2,3},{3,4},{4,5},{5,6},{6,7},{8,9},{9,10},{10,11},{11... | collective-permute-start | bytes 37064 | tf_op jit(solution)/shard_map/ppermute | solution.py:354
  49.4 0.6 add_convert_fusion.has_ref
  50.0 13.5 %dense.1.field_ref = f32[768,2048]{1,0:T(8,128)} custom-call(f32[768,2048]{1,0:T(8,128)} %xn_ref.1, f32[768,2048]{1,0:T(8,128)} %sn_ref.1, f32[768,2048]{1,0:T(8,128)} %xn_ref.1, f32[768,2048]{1,0:T(8,128)} %sn_ref.1, f32[768,2048]{1,0:T(8,128)} %xn_ref.1, f32[768,2048]{1,0:T(8,128)} %sn_ref.1), custom_call_target="tpu_custom_call" | custom-call | tf_op jit(solution)/shard_map/dense/pallas_call | solution.py:67
  63.6 0.8 pad.8.hcr
  64.4 0.8 pad.7.hcl
  65.2 7.0 %rim.1 = (f32[1568,128]{1,0:T(8,128)}, f32[768,128]{1,0:T(8,128)}, f32[768,128]{1,0:T(8,128)}, f32[8,2048]{1,0:T(8,128)}, f32[8,2048]{1,0:T(8,128)}) custom-call(s32[4]{0:T(128)} %add_convert_fusion.has_ref, f32[768,2048]{1,0:T(8,128)} %xn_ref.1, f32[768,2048]{1,0:T(8,128)} %sn_ref.1, f32[768,2048]{1,0:T(8,128)} %xn_ref.1, f32[768,2048]{1,0:T(8,128)} %sn_ref.1, ...), custom_call_target="tpu_custom_call" | custom-call | tf_op jit(solution)/shard_map/rim/pallas_call | solution.py:145
  72.2 6.5 %place.1 = (f32[2048,128]{1,0:T(8,128)}, f32[4096,128]{1,0:T(8,128)}) custom-call(s32[2048]{0:T(1024)} %get-tuple-element.44.run_ref, s32[2048]{0:T(1024)} %get-tuple-element.43.slot_ref, f32[1568,128]{1,0:T(8,128)} %get-tuple-element.14.r_ref.rim_ref), custom_call_target="tpu_custom_call" | custom-call | tf_op jit(solution)/shard_map/place/pallas_call | solution.py:168
  78.7 5.5 %product_a.1 = (f32[2048,128]{1,0:T(8,128)}, f32[4,8,128]{2,1,0:T(8,128)}) custom-call(f32[4096,128]{1,0:T(8,128)} %get-tuple-element.15.s, bf16[64,72,128]{2,1,0:T(8,128)(2,1)} %copy-done), custom_call_target="tpu_custom_call" | custom-call | tf_op jit(solution)/shard_map/product_a/pallas_call | solution.py:240
  84.3 1.0 copy-done.1
  85.3 5.4 %product_b.1 = (f32[2048,128]{1,0:T(8,128)}, f32[128,4,128]{2,1,0:T(4,128)}) custom-call(f32[4096,128]{1,0:T(8,128)} %get-tuple-element.15.s, bf16[64,72,128]{2,1,0:T(8,128)(2,1)} %copy-done.1, f32[4,8,128]{2,1,0:T(8,128)} %get-tuple-element.16.p), custom_call_target="tpu_custom_call" | custom-call | tf_op jit(solution)/shard_map/product_b/pallas_call | solution.py:249
  90.6 3.7 %all-to-all-start.1 = ((f32[128,4,128]{2,1,0:T(4,128)}), f32[128,4,128]{2,1,0:T(4,128)S(1)}, u32[]{:S(2)}, u32[]{:S(2)}) async-start(f32[128,4,128]{2,1,0:T(4,128)} %get-tuple-element.17), calls=%async_computation.1 | async-start | bytes 524288 | tf_op jit(solution)/shard_map/all_to_all | solution.py:375
  94.4 3.2 %fusion.cnt_ref = f32[1568,128]{1,0:T(8,128)} fusion(s32[2048]{0:T(1024)S(1)} %copy-done.6), kind=kOutput, calls=%fused_computation.1 | convolution fusion | flops 825294848 | bytes 811008 | tf_op jit(solution)/shard_map/dot_general | solution.py:371
  97.6 4.9 %order.1.q_ref = f32[2048,128]{1,0:T(8,128)} custom-call(s32[2048]{0:T(1024)} %get-tuple-element.43.slot_ref, f32[2048,128]{1,0:T(8,128)} %get-tuple-element.19.qa_ref, f32[2048,128]{1,0:T(8,128)} %get-tuple-element.20.qb_ref), custom_call_target="tpu_custom_call" | custom-call | tf_op jit(solution)/shard_map/order/pallas_call | solution.py:270
  102.5 2.4 %all-to-all-done.1.red_ref = f32[128,4,128]{2,1,0:T(4,128)S(1)} async-done(((f32[128,4,128]{2,1,0:T(4,128)}), f32[128,4,128]{2,1,0:T(4,128)S(1)}, u32[]{:S(2)}, u32[]{:S(2)}) %all-to-all-start.1) | async-done | bytes 262176 | tf_op jit(solution)/shard_map/all_to_all | solution.py:375
  104.9 0.7 copy-done.2
  105.6 7.4 %final.1 = (f32[768,2048]{1,0:T(8,128)}, f32[2048,128]{1,0:T(8,128)}, f32[2048,128]{1,0:T(8,128)}) custom-call(f32[128,4,128]{2,1,0:T(4,128)} %copy-done.2, f32[2048,128]{1,0:T(8,128)} %get-tuple-element.18.r_ref, f32[2048,128]{1,0:T(8,128)} %order.1.q_ref, f32[1568,128]{1,0:T(8,128)} %get-tuple-element.14.r_ref.rim_ref, ...), custom_call_target="tpu_custom_call", output_to_operand_aliasing={{0}: (9, {})} | custom-call | tf_op jit(solution)/shard_map/final/pallas_call | solution.py:327
  (30 shorter events, 0.4 us)
Async XLA Ops:
  0.6 21.9 %copy-start.3 = (s32[2048,1]{0,1:T(1,128)S(1)}, s32[2048,1]{0,1:T(1,128)}, u32[]{:S(2)}) copy-start(s32[2048,1]{0,1:T(1,128)} %param.8) | copy-start | bytes 24580
  1.6 40.6 %collective-permute-start = (f32[4,2048]{1,0:T(4,128)S(1)}, f32[4,2048]{1,0:T(4,128)S(1)}, u32[]{:S(2)}, u32[]{:S(2)}) collective-permute-start(f32[4,2048]{1,0:T(4,128)S(1)} %pad_maximum_fusion), channel_id=1, source_target_pairs={{0,8},{8,16},{16,24},{24,32},{32,40},{40,48},{48,56},{56,64},{64,7... | collective-permute-start | bytes 98312 | tf_op jit(solution)/shard_map/ppermute | solution.py:344
  6.0 36.6 %collective-permute-start.1 = (f32[4,2048]{1,0:T(4,128)S(1)}, f32[4,2048]{1,0:T(4,128)S(1)}, u32[]{:S(2)}, u32[]{:S(2)}) collective-permute-start(f32[4,2048]{1,0:T(4,128)S(1)} %pad_maximum_fusion.1), channel_id=1, source_target_pairs={{8,0},{16,8},{24,16},{32,24},{40,32},{48,40},{56,48},{64,56},{72,6... | collective-permute-start | bytes 98312 | tf_op jit(solution)/shard_map/ppermute | solution.py:345
  9.2 16.6 %copy-start.7 = (s32[2048]{0:T(1024)S(1)}, s32[2048]{0:T(1024)}, u32[]{:S(2)}) copy-start(s32[2048]{0:T(1024)} %param.7) | copy-start | bytes 24580
  9.2 30.4 %all-to-all-start = ((bf16[64,72,128]{2,1,0:T(8,128)(2,1)}), bf16[64,72,128]{2,1,0:T(8,128)(2,1)S(1)}, u32[]{:S(2)}, u32[]{:S(2)}) async-start(bf16[64,72,128]{2,1,0:T(8,128)(2,1)} %pack.1), calls=%async_computation | async-start | bytes 2359296 | tf_op jit(solution)/shard_map/all_to_all | solution.py:339
  39.6 24.0 %copy-start = (bf16[64,72,128]{2,1,0:T(8,128)(2,1)}, bf16[64,72,128]{2,1,0:T(8,128)(2,1)S(1)}, u32[]{:S(2)}) copy-start(bf16[64,72,128]{2,1,0:T(8,128)(2,1)S(1)} %all-to-all-done.b) | copy-start | bytes 3538948
  39.6 44.7 %collective-permute-start.4 = (bf16[64,72,128]{2,1,0:T(8,128)(2,1)S(1)}, bf16[64,72,128]{2,1,0:T(8,128)(2,1)S(1)}, u32[]{:S(2)}, u32[]{:S(2)}) collective-permute-start(bf16[64,72,128]{2,1,0:T(8,128)(2,1)S(1)} %all-to-all-done.b), channel_id=1, source_target_pairs={{0,1},{1,0},{2,3},{3,2},{4,5},{5,4},{6,7},{7,6},{8,9},{9,8},{10,11... | collective-permute-start | bytes 3538952 | tf_op jit(solution)/shard_map/ppermute | solution.py:340
  42.2 21.3 %copy-start.4 = (f32[4,2048]{1,0:T(4,128)}, f32[4,2048]{1,0:T(4,128)S(1)}, u32[]{:S(2)}) copy-start(f32[4,2048]{1,0:T(4,128)S(1)} %collective-permute-done.hup) | copy-start | bytes 98308
  42.7 20.9 %copy-start.5 = (f32[4,2048]{1,0:T(4,128)}, f32[4,2048]{1,0:T(4,128)S(1)}, u32[]{:S(2)}) copy-start(f32[4,2048]{1,0:T(4,128)S(1)} %collective-permute-done.1.hdn) | copy-start | bytes 98308
  43.9 19.7 %collective-permute-start.3 = (f32[4,772]{0,1:T(8,128)S(1)}, f32[4,772]{0,1:T(8,128)S(1)}, u32[]{:S(2)}, u32[]{:S(2)}) collective-permute-start(f32[4,772]{0,1:T(8,128)S(1)} %copy.27), channel_id=1, source_target_pairs={{1,0},{2,1},{3,2},{4,3},{5,4},{6,5},{7,6},{9,8},{10,9},{11,10},{12... | collective-permute-start | bytes 37064 | tf_op jit(solution)/shard_map/ppermute | solution.py:355
  45.8 18.6 %collective-permute-start.2 = (f32[4,772]{0,1:T(8,128)S(1)}, f32[4,772]{0,1:T(8,128)S(1)}, u32[]{:S(2)}, u32[]{:S(2)}) collective-permute-start(f32[4,772]{0,1:T(8,128)S(1)} %copy.20), channel_id=1, source_target_pairs={{0,1},{1,2},{2,3},{3,4},{4,5},{5,6},{6,7},{8,9},{9,10},{10,11},{11... | collective-permute-start | bytes 37064 | tf_op jit(solution)/shard_map/ppermute | solution.py:354
  72.2 22.2 %copy-start.6 = (s32[2048]{0:T(1024)S(1)}, s32[2048]{0:T(1024)}, u32[]{:S(2)}) copy-start(s32[2048]{0:T(1024)} %get-tuple-element.44.run_ref) | copy-start | bytes 24580
  84.3 1.0 copy-start.1
  90.6 14.2 %all-to-all-start.1 = ((f32[128,4,128]{2,1,0:T(4,128)}), f32[128,4,128]{2,1,0:T(4,128)S(1)}, u32[]{:S(2)}, u32[]{:S(2)}) async-start(f32[128,4,128]{2,1,0:T(4,128)} %get-tuple-element.17), calls=%async_computation.1 | async-start | bytes 524288 | tf_op jit(solution)/shard_map/all_to_all | solution.py:375
  104.9 0.7 copy-start.2

commit v2 on v1

--- a/solution.py
+++ b/solution.py
@@ -15,6 +15,7 @@
 PR = 72
 OFF = 16
 FR = R + 2 * OFF
+FC = 896
 ROWS = ("y", "z")
 COLS = ("x", "c")
 ALL = ("y", "z", "x", "c")
@@ -22,7 +23,11 @@
 VM = pl.BlockSpec(memory_space=pltpu.VMEM)
 SM = pl.BlockSpec(memory_space=pltpu.SMEM)
 ANY = pl.BlockSpec(memory_space=pl.ANY)
-PARAMS = pltpu.CompilerParams(vmem_limit_bytes=56 << 20)
+ND = 8
+C1 = 0.6111111
+K1 = C1 + 2.75 * (1.0 - C1)
+K2 = 2.75 * C1
+PARAMS = pltpu.CompilerParams(vmem_limit_bytes=20 << 20)
 
 
 def sds(shape, dtype=F32):
@@ -48,88 +53,150 @@
     return pl.pallas_call(pack_kernel, out_shape=sds((NG, PR, W), BF16), in_specs=[VM], out_specs=VM, compiler_params=PARAMS, name="pack")(blocks)
 
 
-def dense_kernel(x_ref, s_ref, xp_ref, sp_ref, xn_ref, sn_ref, out_ref, f_ref):
-    t = 4.0 + s_ref[...]
-    dinv = 1.0 / t
-    x = x_ref[...]
-    f = 0.6111111 * dinv * x
-    f_ref[8:72] = f
-    f_ref[0:8] = 0.6111111 * (1.0 / (4.0 + sp_ref[...])) * xp_ref[...]
-    f_ref[72:80] = 0.6111111 * (1.0 / (4.0 + sn_ref[...])) * xn_ref[...]
-    beside = f_ref[9:73] + f_ref[7:71] + pltpu.roll(f, C - 1, axis=1) + pltpu.roll(f, 1, axis=1)
-    out_ref[...] = f + 2.75 * dinv * (x - (t * f - beside))
+def sides(tiles):
+    lane = lax.broadcasted_iota(jnp.int32, (1, W), 1)
+    n = len(tiles)
+    prev = [pltpu.roll(t, 1, axis=1) for t in tiles]
+    succ = [pltpu.roll(t, W - 1, axis=1) for t in tiles]
+    return [jnp.where(lane == 0, prev[c - 1], prev[c]) + jnp.where(lane == W - 1, succ[(c + 1) % n], succ[c]) for c in range(n)]
+
+
+def dense_kernel(x_ref, s_ref, xp_ref, sp_ref, xn_ref, sn_ref, out_ref, g_ref, d_ref):
+    tiles = [slice(c * W, (c + 1) * W) for c in range(C // W)]
+    n = 8 * ND
+    for c, lanes in enumerate(tiles):
+        dinv = 1.0 / (4.0 + s_ref[:, lanes])
+        d_ref[c] = dinv
+        g_ref[c, 8:8 + n] = dinv * x_ref[:, lanes]
+        g_ref[c, 7:8] = xp_ref[7:8, lanes] / (4.0 + sp_ref[7:8, lanes])
+        g_ref[c, 8 + n:9 + n] = xn_ref[0:1, lanes] / (4.0 + sn_ref[0:1, lanes])
+    for k in range(ND):
+        rows = slice(8 * k, 8 * k + 8)
+        side = sides([g_ref[c, 8 * k + 8:8 * k + 16] for c in range(C // W)])
+        for c, lanes in enumerate(tiles):
+            beside = (g_ref[c, 8 * k + 7:8 * k + 15] + g_ref[c, 8 * k + 9:8 * k + 17]) + side[c]
+            out_ref[rows, lanes] = d_ref[c, rows] * (K1 * x_ref[rows, lanes] + K2 * beside)
 
 
 def dense(rhs, sigma):
-    main = pl.BlockSpec((64, C), lambda i: (i, 0))
-    prev = pl.BlockSpec((8, C), lambda i: (jnp.maximum(8 * i - 1, 0), 0))
-    succ = pl.BlockSpec((8, C), lambda i: (jnp.minimum(8 * i + 8, R // 8 - 1), 0))
+    n = 8 * ND
+    main = pl.BlockSpec((n, C), lambda i: (i, 0))
+    prev = pl.BlockSpec((8, C), lambda i: (jnp.maximum(ND * i - 1, 0), 0))
+    succ = pl.BlockSpec((8, C), lambda i: (jnp.minimum(ND * i + ND, R // 8 - 1), 0))
     return pl.pallas_call(
-        dense_kernel, grid=(R // 64,), out_shape=sds((R, C)), in_specs=[main, main, prev, prev, succ, succ], out_specs=main,
-        scratch_shapes=[pltpu.VMEM((80, C), F32)], compiler_params=PARAMS, name="dense")(rhs, sigma, rhs, sigma, rhs, sigma)
-
-
-def rim_kernel(has_ref, xl, sl, xr, sr, xt, st, xb, sb, hup, hdn, hcl, hcr, r_out, secl, secr, sect, secb, X, D, F, S, X2, D2, F2, S2):
+        dense_kernel, grid=(R // n,), out_shape=sds((R, C)), in_specs=[main, main, prev, prev, succ, succ], out_specs=main,
+        scratch_shapes=[pltpu.VMEM((C // W, n + 16, W), F32), pltpu.VMEM((C // W, n, W), F32)],
+        compiler_params=PARAMS, name="dense")(rhs, sigma, rhs, sigma, rhs, sigma)
+
+
+def cols_kernel(xl, sl, xr, sr, hup, hdn, right_out, left_out, buf):
+    buf[0:OFF] = jnp.zeros((OFF, W), F32)
+    buf[OFF + R:FC] = jnp.zeros((FC - OFF - R, W), F32)
+    for out, x, s, c0, lane in ((right_out, xr, sr, C - W, W - 8), (left_out, xl, sl, 0, 0)):
+        cols = slice(c0, c0 + W)
+        for k, src in ((0, x), (2, s)):
+            buf[OFF - 2:OFF] = hup[k:k + 2, cols]
+            buf[OFF:OFF + R] = src[...]
+            buf[OFF + R:OFF + R + 2] = hdn[k:k + 2, cols]
+            for c in range(FC // W):
+                out[4 * k:4 * k + 8, c * W:(c + 1) * W] = buf[c * W:(c + 1) * W].T[lane:lane + 8]
+
+
+def edge_cols(rhs, sigma, hup, hdn):
+    left = pl.BlockSpec((R, W), lambda i: (0, 0))
+    right = pl.BlockSpec((R, W), lambda i: (0, C // W - 1))
+    rows = pl.BlockSpec((4, C), lambda i: (0, 0))
+    out = pl.BlockSpec((16, FC), lambda i: (0, 0))
+    return pl.pallas_call(cols_kernel, grid=(1,), out_shape=[sds((16, FC))] * 2, in_specs=[left, left, right, right, rows, rows], out_specs=[out, out],
+                          scratch_shapes=[pltpu.VMEM((FC, W), F32)], compiler_params=PARAMS, name="cols")(rhs, sigma, rhs, sigma, hup, hdn)
+
+
+def rim_kernel(has_ref, xl, sl, xr, sr, xt, st, xb, sb, hup, hdn, hcl, hcr, r_out, secl, secr, sect, secb, X, D, G, S, H, D2, G2, S2):
     up, down, left, right = (has_ref[k] for k in range(4))
-
-    def strip(x, s, c0, hc, lanes, alive, sec, base, lo):
-        lane = lax.broadcasted_iota(jnp.int32, (1, 2 * W), 1)
-
-        def put(v, rows, k):
-            a = jnp.where(lane == lanes[0], hc[rows, k:k + 1], v)
-            return jnp.where(lane == lanes[1], hc[rows, k + 1:k + 2], a)
-
-        own, above, under = slice(OFF, OFF + R), slice(OFF - 2, OFF), slice(OFF + R, OFF + R + 2)
-        cols = slice(c0, c0 + 2 * W)
-        for ref, k, src in ((X, 0, x), (D, 2, s)):
-            ref[0:OFF] = jnp.zeros((OFF, 2 * W), F32)
-            ref[OFF + R:FR] = jnp.zeros((OFF, 2 * W), F32)
-            ref[above] = put(hup[k:k + 2, cols], above, k)
-            ref[own] = put(src[...], own, k)
-            ref[under] = put(hdn[k:k + 2, cols], under, k)
-        F[...] = 0.6111111 * (1.0 / (4.0 + D[...])) * X[...]
-        mid = slice(8, FR - 8)
-        t = 4.0 + D[mid]
-        f = F[mid]
-        beside = F[9:FR - 7] + F[7:FR - 9] + pltpu.roll(f, 2 * W - 1, axis=1) + pltpu.roll(f, 1, axis=1)
-        sec_v = f + 2.75 * (1.0 / t) * (X[mid] - (t * f - beside))
-        row = lax.broadcasted_iota(jnp.int32, (FR - 16, 1), 0) + (8 - OFF)
-        keep = ((row >= 0) | (up > 0)) & ((row < R) | (down > 0))
-        keep = keep & (((lane != lanes[0]) & (lane != lanes[1])) | (alive > 0))
-        S[mid] = jnp.where(keep, sec_v, 0.0)
-        g = S[own]
-        beside = S[OFF + 1:OFF + R + 1] + S[OFF - 1:OFF + R - 1] + pltpu.roll(g, 2 * W - 1, axis=1) + pltpu.roll(g, 1, axis=1)
-        res = X[own] - ((4.0 + D[own]) * g - beside)
-        r_out[base:base + R] = res[:, lo:lo + W]
-        sec[...] = g[:, lo:lo + W]
-
-    strip(xl, sl, 0, hcl, (2 * W - 2, 2 * W - 1), left, secl, 0, 0)
-    strip(xr, sr, C - 2 * W, hcr, (0, 1), right, secr, R, W)
-
-    def edge(x, s, own, halo, h, at, alive, gone, sec, sec_rows, base):
-        for ref, k, src in ((X2, 0, x), (D2, 2, s)):
-            ref[...] = jnp.zeros((32, C), F32)
-            ref[own] = src[...]
-            ref[halo] = h[k:k + 2]
-        F2[...] = 0.6111111 * (1.0 / (4.0 + D2[...])) * X2[...]
-        mid = slice(8, 24)
-        t = 4.0 + D2[mid]
-        f = F2[mid]
-        beside = F2[9:25] + F2[7:23] + pltpu.roll(f, C - 1, axis=1) + pltpu.roll(f, 1, axis=1)
-        sec_v = f + 2.75 * (1.0 / t) * (X2[mid] - (t * f - beside))
-        row = lax.broadcasted_iota(jnp.int32, (16, 1), 0) + 8
-        S2[mid] = jnp.where(gone(row) & (alive == 0), 0.0, sec_v)
-        sec[...] = S2[sec_rows]
-        g = S2[mid]
-        sides = pltpu.roll(g, C - 1, axis=1) + pltpu.roll(g, 1, axis=1)
-        S2[0:1] = sides[at - 8:at - 7]
-        a = slice(at, at + 1)
-        res = X2[a] - ((4.0 + D2[a]) * S2[a] - (S2[at + 1:at + 2] + S2[at - 1:at] + S2[0:1]))
-        for k in range(C // W):
-            r_out[base + k:base + k + 1] = res[:, k * W:(k + 1) * W]
-
-    edge(xt, st, slice(16, 32), slice(14, 16), hup, 16, up, lambda row: row < 16, sect, slice(16, 24), 2 * R)
-    edge(xb, sb, slice(0, 16), slice(16, 18), hdn, 15, down, lambda row: row >= 16, secb, slice(8, 16), 2 * R + 16)
+    lane = lax.broadcasted_iota(jnp.int32, (1, W), 1)
+
+    def stencil(x, d, above, under, side):
+        return d * (K1 * x + K2 * ((above + under) + side))
+
+    def strip(x, s, c0, hc, m, a, alive, sec, base):
+        q = 1 - m
+        sel = (lane == a) | (lane == a + 1)
+        pad = jnp.zeros((W - 8, W), F32)
+        for n in (0, 1):
+            for c in range(FC // W):
+                got = hc[8 * n:8 * n + 8, c * W:(c + 1) * W]
+                H[n, c * W:(c + 1) * W] = jnp.concatenate([got, pad] if a == 0 else [pad, got], axis=0).T
+        for c in (0, 1):
+            cols = slice(c0 + c * W, c0 + (c + 1) * W)
+            for rows, xv, sv in ((slice(OFF - 2, OFF), hup[0:2, cols], hup[2:4, cols]),
+                                 (slice(OFF + R, OFF + R + 2), hdn[0:2, cols], hdn[2:4, cols]),
+                                 (slice(OFF, OFF + R), x[:, c * W:(c + 1) * W], s[:, c * W:(c + 1) * W])):
+                if c == m:
+                    xv = jnp.where(sel, H[0, rows], xv)
+                    sv = jnp.where(sel, H[1, rows], sv)
+                dinv = 1.0 / (4.0 + sv)
+                D[c, rows] = dinv
+                X[c, rows] = xv
+                G[c, rows] = dinv * xv
+        live = ~sel | (alive > 0)
+
+        def second(r0, n, ok):
+            rows = slice(r0, r0 + n)
+            side = sides([G[0, rows], G[1, rows]])
+            for c in (0, 1):
+                v = stencil(X[c, rows], D[c, rows], G[c, r0 - 1:r0 + n - 1], G[c, r0 + 1:r0 + n + 1], side[c])
+                keep = live if c == m else None
+                if ok is not None:
+                    keep = ok if keep is None else keep & ok
+                S[c, rows] = v if keep is None else jnp.where(keep, v, 0.0)
+
+        second(OFF - 1, 1, up > 0)
+        second(OFF + R, 1, down > 0)
+        for k in range(R // 8):
+            second(OFF + 8 * k, 8, None)
+        for k in range(R // 8):
+            r0 = OFF + 8 * k
+            rows = slice(r0, r0 + 8)
+            side = sides([S[0, rows], S[1, rows]])[q]
+            v = S[q, rows]
+            own = slice(8 * k, 8 * k + 8)
+            t = 4.0 + s[own, q * W:(q + 1) * W]
+            r_out[base + 8 * k:base + 8 * k + 8] = X[q, rows] - (t * v - ((S[q, r0 - 1:r0 + 7] + S[q, r0 + 1:r0 + 9]) + side))
+            sec[own] = v
+
+    strip(xl, sl, 0, hcl, 1, W - 2, left, secl, 0)
+    strip(xr, sr, C - 2 * W, hcr, 0, 0, right, secr, R)
+
+    def edge(x, s, halo, h, g, o, alive, sec, line, base):
+        nt = C // W
+        tiles = [slice(c * W, (c + 1) * W) for c in range(nt)]
+        ok = alive > 0
+        for c, cols in enumerate(tiles):
+            dinv = 1.0 / (4.0 + s[:, cols])
+            D2[c, 8:24] = dinv
+            G2[c, 8:24] = dinv * x[:, cols]
+            dinv = 1.0 / (4.0 + halo[2:4, cols])
+            D2[c, h:h + 2] = dinv
+            G2[c, h:h + 2] = dinv * halo[0:2, cols]
+        side = sides([G2[c, g:g + 8] for c in range(nt)])
+        outer = sides([G2[c, o:o + 1] for c in range(nt)])
+        near = halo[1:2, :] if o < g else halo[0:1, :]
+        for c, cols in enumerate(tiles):
+            S2[c, g:g + 8] = stencil(x[g - 8:g, cols], D2[c, g:g + 8], G2[c, g - 1:g + 7], G2[c, g + 1:g + 9], side[c])
+            v = stencil(near[:, cols], D2[c, o:o + 1], G2[c, o - 1:o], G2[c, o + 1:o + 2], outer[c])
+            S2[c, o:o + 1] = jnp.where(ok, v, 0.0)
+        side = sides([S2[c, g:g + 8] for c in range(nt)])
+        for c, cols in enumerate(tiles):
+            v = S2[c, g:g + 8]
+            sec[:, cols] = v
+            at = g + line
+            one = slice(at, at + 1)
+            t = 4.0 + s[at - 8:at - 7, cols]
+            res = x[at - 8:at - 7, cols] - (t * S2[c, one] - ((S2[c, at - 1:at] + S2[c, at + 1:at + 2]) + side[c][line:line + 1]))
+            r_out[base + c:base + c + 1] = res
+
+    edge(xt, st, hup, 6, 8, 7, up, sect, 0, 2 * R)
+    edge(xb, sb, hdn, 24, 16, 24, down, secb, 7, 2 * R + 16)
 
 
 def rim(has, rhs, sigma, hup, hdn, hcl, hcr):
@@ -144,9 +211,9 @@
     outs = [(RIM, W), (R, W), (R, W), (8, C), (8, C)]
     return pl.pallas_call(
         rim_kernel, grid=(1,), out_shape=[sds(s) for s in outs],
-        in_specs=[SM, left, left, right, right, top, top, bottom, bottom, whole((4, C)), whole((4, C)), whole((FR, 4)), whole((FR, 4))],
+        in_specs=[SM, left, left, right, right, top, top, bottom, bottom, whole((4, C)), whole((4, C)), whole((16, FC)), whole((16, FC))],
         out_specs=[whole(s) for s in outs],
-        scratch_shapes=[pltpu.VMEM((FR, 2 * W), F32)] * 4 + [pltpu.VMEM((32, C), F32)] * 4,
+        scratch_shapes=[pltpu.VMEM((2, FR, W), F32)] * 4 + [pltpu.VMEM((2, FC, W), F32)] + [pltpu.VMEM((C // W, 32, W), F32)] * 3,
         compiler_params=PARAMS, name="rim")(has, rhs, sigma, rhs, sigma, rhs, sigma, rhs, sigma, hup, hdn, hcl, hcr)
 
 
@@ -237,26 +304,23 @@
     def kernel(s, b, q, sums):
         product_kernel(True, s, b, q, sums, None)
 
-    return pl.pallas_call(kernel, grid=(1,), out_shape=[sds((NG * CAP, W)), sds((4, 8, W))],
+    return pl.pallas_call(kernel, grid=(1,), out_shape=[sds((2 * NG * CAP, W)), sds((4, 8, W))],
                           in_specs=[spec, pl.BlockSpec((NG, PR, W), lambda i: (0, 0, 0))],
                           out_specs=[spec, pl.BlockSpec((4, 8, W), lambda i: (0, 0, 0))], compiler_params=PARAMS, name="product_a")(slots, blocks)
 
 
-def product_second(slots, blocks, prev):
-    def kernel(s, b, p, q, sums):
+def product_second(slots, blocks, prev, half):
+    def kernel(s, b, p, h, q, sums):
         product_kernel(False, s, b, p, q, sums)
 
-    return pl.pallas_call(kernel, grid=(1,), out_shape=[sds((NG * CAP, W)), sds((2 * NG, 4, W))],
+    return pl.pallas_call(kernel, grid=(1,), out_shape=[sds((2 * NG * CAP, W)), sds((2 * NG, 4, W))], input_output_aliases={3: 0},
                           in_specs=[pl.BlockSpec((NG * CAP, W), lambda i: (1, 0)), pl.BlockSpec((NG, PR, W), lambda i: (0, 0, 0)),
-                                    pl.BlockSpec((4, 8, W), lambda i: (0, 0, 0))],
-                          out_specs=[pl.BlockSpec((NG * CAP, W), lambda i: (0, 0)), pl.BlockSpec((2 * NG, 4, W), lambda i: (0, 0, 0))],
-                          compiler_params=PARAMS, name="product_b")(slots, blocks, prev)
-
-
-def order_kernel(slot_ref, qa_ref, qb_ref, out_ref, q_ref):
-    q_ref[0:NG * CAP] = qa_ref[...]
-    q_ref[NG * CAP:] = qb_ref[...]
-
+                                    pl.BlockSpec((4, 8, W), lambda i: (0, 0, 0)), ANY],
+                          out_specs=[pl.BlockSpec((NG * CAP, W), lambda i: (1, 0)), pl.BlockSpec((2 * NG, 4, W), lambda i: (0, 0, 0))],
+                          compiler_params=PARAMS, name="product_b")(slots, blocks, prev, half)
+
+
+def order_kernel(slot_ref, q_ref, out_ref):
     def body(b, carry):
         for u in range(16):
             t = b * 16 + u
@@ -266,9 +330,8 @@
     lax.fori_loop(0, T // 16, body, 0)
 
 
-def order(slot, qa, qb):
-    return pl.pallas_call(order_kernel, out_shape=sds((T, W)), in_specs=[SM, VM, VM], out_specs=VM,
-                          scratch_shapes=[pltpu.VMEM((2 * NG * CAP, W), F32)], compiler_params=PARAMS, name="order")(slot, qa, qb)
+def order(slot, q):
+    return pl.pallas_call(order_kernel, out_shape=sds((T, W)), in_specs=[SM, VM], out_specs=VM, compiler_params=PARAMS, name="order")(slot, q)
 
 
 CH = 8
@@ -337,24 +400,17 @@
     core = lax.axis_index("c")
     packed = pack(schur_blocks)
     mine = lax.all_to_all(packed, CHIPS, 0, 0, tiled=True)
-    theirs = lax.ppermute(mine, "c", [(0, 1), (1, 0)])
     nrow, ncol = 16, 8
     up = [(i, i + 1) for i in range(nrow - 1)]
     down = [(i + 1, i) for i in range(nrow - 1)]
     hup = lax.ppermute(jnp.concatenate([rhs[-2:], sigma[-2:]]), ROWS, up)
     hdn = lax.ppermute(jnp.concatenate([rhs[:2], sigma[:2]]), ROWS, down)
 
-    def cols(sl):
-        a = jnp.concatenate([hup[0:2, sl], rhs[:, sl], hdn[0:2, sl]], axis=0)
-        b = jnp.concatenate([hup[2:4, sl], sigma[:, sl], hdn[2:4, sl]], axis=0)
-        return jnp.concatenate([a.T, b.T], axis=0)
-
     rightward = [(i, i + 1) for i in range(ncol - 1)]
     leftward = [(i + 1, i) for i in range(ncol - 1)]
-    hcl = lax.ppermute(cols(slice(C - 2, C)), COLS, rightward)
-    hcr = lax.ppermute(cols(slice(0, 2)), COLS, leftward)
-    hcl = jnp.pad(hcl.T, ((OFF - 2, OFF - 2), (0, 0)))
-    hcr = jnp.pad(hcr.T, ((OFF - 2, OFF - 2), (0, 0)))
+    to_right, to_left = edge_cols(rhs, sigma, hup, hdn)
+    hcl = lax.ppermute(to_right, COLS, rightward)
+    hcr = lax.ppermute(to_left, COLS, leftward)
     row_at = lax.axis_index(ROWS)
     col_at = lax.axis_index(COLS)
     has = jnp.stack([row_at > 0, row_at < nrow - 1, col_at > 0, col_at < ncol - 1]).astype(jnp.int32)
@@ -370,10 +426,12 @@
     hits = (jnp.arange(RIM, dtype=jnp.int32)[:, None] == run[None, :]).astype(BF16)
     cnt = jnp.dot(hits, jnp.ones((T, W), BF16), preferred_element_type=F32)
     r_tiles, slots = place(run, slot, r_rim)
-    qa, part = product_first(slots, mine)
-    qb, sums = product_second(slots, theirs, part)
+    mine, slots = lax.optimization_barrier((mine, slots))
+    theirs = lax.ppermute(mine, "c", [(0, 1), (1, 0)])
+    q, part = product_first(slots, mine)
+    q, sums = product_second(slots, theirs, part, q)
     red = lax.all_to_all(sums, ALL, 0, 0, tiled=True)
-    q_tiles = order(slot, qa, qb)
+    q_tiles = order(slot, q)
     field = dense(rhs, sigma)
     return tuple(final(red, r_tiles, q_tiles, r_rim, cnt, secl, secr, sect, secb, field))
 

time: 114 us -> 101 us (0.89)
  Pallas kernels: 52.1 us -> 29.7 us
  local copies, waits for them, and re-layouts: 9.91 us -> 24.2 us
  waiting for transfers between devices: 15 us -> 8.79 us
  starting transfers between devices: 29.3 us -> 32.5 us
  other arithmetic: 2.68 us -> 1.21 us
    unnamed x20 -> x36, local copies, waits for them, and re-layouts: 2.38 us -> 22.1 us
    all_to_all x1, waiting for transfers between devices: 12.6 us -> 0.01 us  [per_device(): mine = lax.all_to_all(packed, CHIPS, 0, 0, tiled=True)]
    pallas_call x4 -> x5, Pallas kernels: 29.3 us -> 17.1 us  [the longest x1 7.24 us: dense(): pl.pallas_call(dense_kernel, grid=(R // n,), out_shape=sds((R, C)), in_sp...]
    all_to_all x1, starting transfers between devices: 3.72 us -> 8.73 us  [per_device(): red = lax.all_to_all(sums, ALL, 0, 0, tiled=True)]
    ppermute x2, waiting for transfers between devices: 0.01 us -> 3.78 us  [the longest x1 3.78 us: per_device(): hcr = lax.ppermute(to_left, COLS, leftward)]
    pallas_call x1, Pallas kernels: 7.37 us -> 3.75 us  [final(): pl.pallas_call(final_kernel, grid=(CH,), out_shape=[sds((R, C)), sds((T,...]
    slice x12 -> x0, local copies, waits for them, and re-layouts: 3.46 us -> none  [the longest x7 1.8 us: cols(): a = jnp.concatenate([hup[0:2, sl], rhs[:, sl], hdn[0:2, sl]], axis=0)]
    pallas_call x1, Pallas kernels: 7.03 us -> 3.64 us  [rim(): pl.pallas_call(rim_kernel, grid=(1,), out_shape=[sds(s) for s in outs], i...]
  transfers between devices with their start and end apart: 7 -> 7, of which waited for: 2 -> 2; matrix products, arithmetic and copies ran while one was open for 12% -> 6% of each run, Pallas kernels for 35% -> 22%
where the time goes in v2:
time: 101 us; the launch traced here: 100 us
  starting transfers between devices  32.5 us (32%)
  Pallas kernels  29.7 us (29%)
  local copies, waits for them, and re-layouts  24.2 us (24%)
  waiting for transfers between devices  8.79 us (9%)
  matrix products  3.19 us (3%)
  other arithmetic  1.21 us (1%)
    unnamed x36, local copies, waits for them, and re-layouts  22.1 us
    all_to_all x1, starting transfers between devices, per_device(): mine = lax.all_to_all(packed, CHIPS, 0, 0, tiled=True)  11.6 us
    all_to_all x1, starting transfers between devices, per_device(): red = lax.all_to_all(sums, ALL, 0, 0, tiled=True)  8.73 us
    pallas_call x1, Pallas kernels, dense(): pl.pallas_call(dense_kernel, grid=(R // n,), out_shape=sds((R, C)), in_sp...  7.24 us
    all_to_all x1, waiting for transfers between devices, per_device(): red = lax.all_to_all(sums, ALL, 0, 0, tiled=True)  5 us
    ppermute x1, starting transfers between devices, per_device(): hcl = lax.ppermute(to_right, COLS, rightward)  4.6 us
    ppermute x1, starting transfers between devices, per_device(): hup = lax.ppermute(jnp.concatenate([rhs[-2:], sigma[-2:]]), ROWS, up)  4.36 us
    pallas_call x1, Pallas kernels, place(): pl.pallas_call(place_kernel, out_shape=[sds((T, W)), sds((2 * NG * CAP, W...  4.1 us
  transfers between devices with their start and end apart: 7, of which 2 were waited for; matrix products, arithmetic and copies ran while one was open for 6% of the time, Pallas kernels for 22%

profile of v2, /device:TPU:1, one launch (start us, length us, event | category | flops | bytes accessed | tf_op | source)
XLA Modules:
  0.0 100.4 jit_solution(9133734156528926611)
XLA Ops:
  0.6 0.0 copy-start.16
  0.7 1.0 fusion.11
  1.7 4.4 %collective-permute-start = (f32[4,2048]{1,0:T(4,128)S(1)}, f32[4,2048]{1,0:T(4,128)S(1)}, u32[]{:S(2)}, u32[]{:S(2)}) collective-permute-start(f32[4,2048]{1,0:T(4,128)S(1)} %pad_maximum_fusion), channel_id=1, source_target_pairs={{0,8},{8,16},{16,24},{24,32},{32,40},{40,48},{48,56},{56,64},{64,7... | collective-permute-start | bytes 98312 | tf_op jit(solution)/shard_map/ppermute | solution.py:406
  6.0 1.3 %collective-permute-start.1 = (f32[4,2048]{1,0:T(4,128)S(1)}, f32[4,2048]{1,0:T(4,128)S(1)}, u32[]{:S(2)}, u32[]{:S(2)}) collective-permute-start(f32[4,2048]{1,0:T(4,128)S(1)} %pad_maximum_fusion.1), channel_id=1, source_target_pairs={{8,0},{16,8},{24,16},{32,24},{40,32},{48,40},{56,48},{64,56},{72,6... | collective-permute-start | bytes 98312 | tf_op jit(solution)/shard_map/ppermute | solution.py:407
  7.3 0.0 copy-start.15
  7.4 0.7 copy-done.15
  8.1 1.1 %pack.1 = bf16[64,72,128]{2,1,0:T(8,128)(2,1)} custom-call(bf16[1,128,128]{2,1,0:T(8,128)(2,1)S(1)} %copy-done.15), custom_call_target="tpu_custom_call" | custom-call | tf_op jit(solution)/shard_map/pack/pallas_call | solution.py:53
  9.2 11.6 %all-to-all-start = ((bf16[64,72,128]{2,1,0:T(8,128)(2,1)}), bf16[64,72,128]{2,1,0:T(8,128)(2,1)S(1)}, u32[]{:S(2)}, u32[]{:S(2)}) async-start(bf16[64,72,128]{2,1,0:T(8,128)(2,1)} %pack.1), calls=%async_computation | async-start | bytes 2359296 | tf_op jit(solution)/shard_map/all_to_all | solution.py:402
  20.8 0.8 copy.11
  21.6 0.3 fusion.4
  22.0 0.1 broadcast_add_fusion
  22.1 0.3 copy.12
  22.4 0.6 fusion.3
  23.1 0.0 collective-permute-done.hup
  23.1 0.0 collective-permute-done.1.hdn
  23.2 0.0 copy-start
  23.2 2.8 %copy-done = f32[768,2048]{1,0:T(8,128)S(1)} copy-done((f32[768,2048]{1,0:T(8,128)S(1)}, f32[768,2048]{1,0:T(8,128)}, u32[]{:S(2)}) %copy-start) | copy-done | bytes 6291480
  26.0 2.8 %copy-done.2 = f32[768,2048]{1,0:T(8,128)S(1)} copy-done((f32[768,2048]{1,0:T(8,128)S(1)}, f32[768,2048]{1,0:T(8,128)}, u32[]{:S(2)}) %copy-start.2) | copy-done | bytes 6291480
  28.7 0.5 cols.1
  29.3 4.6 %collective-permute-start.2 = (f32[16,896]{1,0:T(8,128)S(1)}, f32[16,896]{1,0:T(8,128)S(1)}, u32[]{:S(2)}, u32[]{:S(2)}) collective-permute-start(f32[16,896]{1,0:T(8,128)S(1)} %get-tuple-element.18), channel_id=1, source_target_pairs={{0,1},{1,2},{2,3},{3,4},{4,5},{5,6},{6,7},{8,9},{9,10},{10,11},{11... | collective-permute-start | bytes 172040 | tf_op jit(solution)/shard_map/ppermute | solution.py:412
  33.9 1.9 %collective-permute-start.3 = (f32[16,896]{1,0:T(8,128)S(1)}, f32[16,896]{1,0:T(8,128)S(1)}, u32[]{:S(2)}, u32[]{:S(2)}) collective-permute-start(f32[16,896]{1,0:T(8,128)S(1)} %get-tuple-element.19), channel_id=1, source_target_pairs={{1,0},{2,1},{3,2},{4,3},{5,4},{6,5},{7,6},{9,8},{10,9},{11,10},{12... | collective-permute-start | bytes 172040 | tf_op jit(solution)/shard_map/ppermute | solution.py:413
  35.8 0.1 add_convert_fusion.has_ref
  35.9 0.0 collective-permute-done.2.hcl
  35.9 3.8 %collective-permute-done.3.hcr = f32[16,896]{1,0:T(8,128)S(1)} collective-permute-done((f32[16,896]{1,0:T(8,128)S(1)}, f32[16,896]{1,0:T(8,128)S(1)}, u32[]{:S(2)}, u32[]{:S(2)}) %collective-permute-start.3) | collective-permute-done | bytes 57376 | tf_op jit(solution)/shard_map/ppermute | solution.py:413
  39.7 3.6 %rim.1 = (f32[1568,128]{1,0:T(8,128)S(1)}, f32[768,128]{1,0:T(8,128)S(1)}, f32[768,128]{1,0:T(8,128)S(1)}, f32[8,2048]{1,0:T(8,128)S(1)}, f32[8,2048]{1,0:T(8,128)S(1)}) custom-call(s32[4]{0:T(128)S(1)} %add_convert_fusion.has_ref, f32[768,2048]{1,0:T(8,128)S(1)} %copy-done, f32[768,2048]{1,0:T(8,128)S(1)} %copy-done.2, f32[768,2048]{1,0:T(8,128)S(1)} %copy-done, ...), custom_call_target="tpu_custom_call" | custom-call | tf_op jit(solution)/shard_map/rim/pallas_call | solution.py:212
  43.3 0.7 copy-done.11
  44.1 0.8 copy-done.13
  44.8 4.1 %place.1 = (f32[2048,128]{1,0:T(8,128)S(1)}, f32[4096,128]{1,0:T(8,128)S(1)}) custom-call(s32[2048]{0:T(1024)S(1)} %get-tuple-element.40.run_ref, s32[2048]{0:T(1024)S(1)} %get-tuple-element.39.slot_ref, f32[1568,128]{1,0:T(8,128)S(1)} %get-tuple-element.20.r_ref.rim_ref), custom_call_target="tpu_custom_call" | custom-call | tf_op jit(solution)/shard_map/place/pallas_call | solution.py:235
  48.9 0.0 copy-start.6
  48.9 0.9 copy-done.6
  49.8 1.0 copy-done.8
  50.8 0.0 collective-permute-start.4
  50.8 2.8 %copy-done.1 = f32[768,2048]{1,0:T(8,128)S(1)} copy-done((f32[768,2048]{1,0:T(8,128)S(1)}, f32[768,2048]{1,0:T(8,128)}, u32[]{:S(2)}) %copy-start.1) | copy-done | bytes 6291480
  53.6 2.8 %copy-done.3 = f32[768,2048]{1,0:T(8,128)S(1)} copy-done((f32[768,2048]{1,0:T(8,128)S(1)}, f32[768,2048]{1,0:T(8,128)}, u32[]{:S(2)}) %copy-start.3) | copy-done | bytes 6291480
  56.4 7.2 %dense.1.field_ref = f32[768,2048]{1,0:T(8,128)} custom-call(f32[768,2048]{1,0:T(8,128)S(1)} %copy-done.1, f32[768,2048]{1,0:T(8,128)S(1)} %copy-done.3, f32[768,2048]{1,0:T(8,128)S(1)} %copy-done.1, f32[768,2048]{1,0:T(8,128)S(1)} %copy-done.3, f32[768,2048]{1,0:T(8,128)S(1)} %copy-done.1, f32[768,2048]{1,0:T(8,128)S(1)} %copy-done.3), custom_call_target="tpu_custom_call" | custom-call | tf_op jit(solution)/shard_map/dense/pallas_call | solution.py:86
  63.6 3.0 %product_a.1 = (f32[4096,128]{1,0:T(8,128)S(1)}, f32[4,8,128]{2,1,0:T(8,128)S(1)}) custom-call(f32[4096,128]{1,0:T(8,128)S(1)} %get-tuple-element.22.s, bf16[64,72,128]{2,1,0:T(8,128)(2,1)S(1)} %all-to-all-done.b), custom_call_target="tpu_custom_call" | custom-call | tf_op jit(solution)/shard_map/product_a/pallas_call | solution.py:307
  66.6 3.5 %product_b.1 = (f32[4096,128]{1,0:T(8,128)S(1)}, f32[128,4,128]{2,1,0:T(4,128)}) custom-call(f32[4096,128]{1,0:T(8,128)S(1)} %get-tuple-element.22.s, bf16[64,72,128]{2,1,0:T(8,128)(2,1)S(1)} %collective-permute-done.4.b, f32[4,8,128]{2,1,0:T(8,128)S(1)} %get-tuple-element.24.p, f32[4096,128]{1,0:T(8,128)S(1)} %get-tuple-element.25.h), custom_call_target="tpu_custom_call", output_to_operand_aliasing={{0}: (3, {})} | custom-call | tf_op jit(solution)/shard_map/product_b/pallas_call | solution.py:316
  70.1 1.3 %copy-done.4 = f32[4096,128]{1,0:T(8,128)} copy-done((f32[4096,128]{1,0:T(8,128)}, f32[4096,128]{1,0:T(8,128)S(1)}, u32[]{:S(2)}) %copy-start.4) | copy-done | bytes 2097176
  71.4 8.7 %all-to-all-start.1 = ((f32[128,4,128]{2,1,0:T(4,128)}), f32[128,4,128]{2,1,0:T(4,128)S(1)}, u32[]{:S(2)}, u32[]{:S(2)}) async-start(f32[128,4,128]{2,1,0:T(4,128)} %get-tuple-element.26), calls=%async_computation.1 | async-start | bytes 524288 | tf_op jit(solution)/shard_map/all_to_all | solution.py:433
  80.2 3.2 %fusion.cnt_ref = f32[1568,128]{1,0:T(8,128)} fusion(s32[2048]{0:T(1024)S(1)} %get-tuple-element.40.run_ref), kind=kOutput, calls=%fused_computation.1 | convolution fusion | flops 825294848 | bytes 811008 | tf_op jit(solution)/shard_map/dot_general | solution.py:427
  83.4 2.8 %order.1.q_ref = f32[2048,128]{1,0:T(8,128)S(1)} custom-call(s32[2048]{0:T(1024)S(1)} %get-tuple-element.39.slot_ref, f32[4096,128]{1,0:T(8,128)S(1)} %copy-done.5), custom_call_target="tpu_custom_call" | custom-call | tf_op jit(solution)/shard_map/order/pallas_call | solution.py:334
  86.2 5.0 %all-to-all-done.1.red_ref = f32[128,4,128]{2,1,0:T(4,128)S(1)} async-done(((f32[128,4,128]{2,1,0:T(4,128)}), f32[128,4,128]{2,1,0:T(4,128)S(1)}, u32[]{:S(2)}, u32[]{:S(2)}) %all-to-all-start.1) | async-done | bytes 262176 | tf_op jit(solution)/shard_map/all_to_all | solution.py:433
  91.2 1.1 %copy-done.7 = f32[1568,128]{1,0:T(8,128)S(1)} copy-done((f32[1568,128]{1,0:T(8,128)S(1)}, f32[1568,128]{1,0:T(8,128)}, u32[]{:S(2)}) %copy-start.7) | copy-done | bytes 802840
  92.3 1.2 %copy-done.9 = f32[2048,128]{1,0:T(8,128)S(1)} copy-done((f32[2048,128]{1,0:T(8,128)S(1)}, f32[2048,128]{1,0:T(8,128)}, u32[]{:S(2)}) %copy-start.9) | copy-done | bytes 1048600
  93.6 1.1 %copy-done.10 = f32[1568,128]{1,0:T(8,128)S(1)} copy-done((f32[1568,128]{1,0:T(8,128)S(1)}, f32[1568,128]{1,0:T(8,128)}, u32[]{:S(2)}) %copy-start.10) | copy-done | bytes 802840
  94.7 1.0 copy-done.12
  95.7 1.0 copy-done.14
  96.7 3.7 %final.1 = (f32[768,2048]{1,0:T(8,128)}, f32[2048,128]{1,0:T(8,128)}, f32[2048,128]{1,0:T(8,128)}) custom-call(f32[128,4,128]{2,1,0:T(4,128)S(1)} %all-to-all-done.1.red_ref, f32[2048,128]{1,0:T(8,128)S(1)} %copy-done.9, f32[2048,128]{1,0:T(8,128)S(1)} %order.1.q_ref, f32[1568,128]{1,0:T(8,128)S(1)} %copy-done.7, ...), custom_call_target="tpu_custom_call", output_to_operand_aliasing={{0}: (9, {})} | custom-call | tf_op jit(solution)/shard_map/final/pallas_call | solution.py:390
  (25 shorter events, 0.1 us)
Async XLA Ops:
  0.6 21.8 %copy-start.16 = (s32[2048,1]{0,1:T(1,128)S(1)}, s32[2048,1]{0,1:T(1,128)}, u32[]{:S(2)}) copy-start(s32[2048,1]{0,1:T(1,128)} %param.8) | copy-start | bytes 24580
  0.6 22.4 %copy-start.17 = (s32[2048]{0:T(1024)S(1)}, s32[2048]{0:T(1024)}, u32[]{:S(2)}) copy-start(s32[2048]{0:T(1024)} %param.7) | copy-start | bytes 24580
  1.7 21.5 %collective-permute-start = (f32[4,2048]{1,0:T(4,128)S(1)}, f32[4,2048]{1,0:T(4,128)S(1)}, u32[]{:S(2)}, u32[]{:S(2)}) collective-permute-start(f32[4,2048]{1,0:T(4,128)S(1)} %pad_maximum_fusion), channel_id=1, source_target_pairs={{0,8},{8,16},{16,24},{24,32},{32,40},{40,48},{48,56},{56,64},{64,7... | collective-permute-start | bytes 98312 | tf_op jit(solution)/shard_map/ppermute | solution.py:406
  6.0 17.1 %collective-permute-start.1 = (f32[4,2048]{1,0:T(4,128)S(1)}, f32[4,2048]{1,0:T(4,128)S(1)}, u32[]{:S(2)}, u32[]{:S(2)}) collective-permute-start(f32[4,2048]{1,0:T(4,128)S(1)} %pad_maximum_fusion.1), channel_id=1, source_target_pairs={{8,0},{16,8},{24,16},{32,24},{40,32},{48,40},{56,48},{64,56},{72,6... | collective-permute-start | bytes 98312 | tf_op jit(solution)/shard_map/ppermute | solution.py:407
  7.3 0.8 copy-start.15
  9.2 41.6 %all-to-all-start = ((bf16[64,72,128]{2,1,0:T(8,128)(2,1)}), bf16[64,72,128]{2,1,0:T(8,128)(2,1)S(1)}, u32[]{:S(2)}, u32[]{:S(2)}) async-start(bf16[64,72,128]{2,1,0:T(8,128)(2,1)} %pack.1), calls=%async_computation | async-start | bytes 2359296 | tf_op jit(solution)/shard_map/all_to_all | solution.py:402
  23.2 2.8 %copy-start = (f32[768,2048]{1,0:T(8,128)S(1)}, f32[768,2048]{1,0:T(8,128)}, u32[]{:S(2)}) copy-start(f32[768,2048]{1,0:T(8,128)} %xn_ref.1) | copy-start | bytes 18874372
  25.9 2.8 %copy-start.2 = (f32[768,2048]{1,0:T(8,128)S(1)}, f32[768,2048]{1,0:T(8,128)}, u32[]{:S(2)}) copy-start(f32[768,2048]{1,0:T(8,128)} %sn_ref.1) | copy-start | bytes 18874372
  29.3 6.6 %collective-permute-start.2 = (f32[16,896]{1,0:T(8,128)S(1)}, f32[16,896]{1,0:T(8,128)S(1)}, u32[]{:S(2)}, u32[]{:S(2)}) collective-permute-start(f32[16,896]{1,0:T(8,128)S(1)} %get-tuple-element.18), channel_id=1, source_target_pairs={{0,1},{1,2},{2,3},{3,4},{4,5},{5,6},{6,7},{8,9},{9,10},{10,11},{11... | collective-permute-start | bytes 172040 | tf_op jit(solution)/shard_map/ppermute | solution.py:412
  33.9 5.8 %collective-permute-start.3 = (f32[16,896]{1,0:T(8,128)S(1)}, f32[16,896]{1,0:T(8,128)S(1)}, u32[]{:S(2)}, u32[]{:S(2)}) collective-permute-start(f32[16,896]{1,0:T(8,128)S(1)} %get-tuple-element.19), channel_id=1, source_target_pairs={{1,0},{2,1},{3,2},{4,3},{5,4},{6,5},{7,6},{9,8},{10,9},{11,10},{12... | collective-permute-start | bytes 172040 | tf_op jit(solution)/shard_map/ppermute | solution.py:413
  43.3 0.8 copy-start.11
  44.1 0.8 copy-start.13
  48.9 0.9 copy-start.6
  49.8 1.0 copy-start.8
  50.8 15.8 %collective-permute-start.4 = (bf16[64,72,128]{2,1,0:T(8,128)(2,1)S(1)}, bf16[64,72,128]{2,1,0:T(8,128)(2,1)S(1)}, u32[]{:S(2)}, u32[]{:S(2)}) collective-permute-start(bf16[64,72,128]{2,1,0:T(8,128)(2,1)S(1)} %all-to-all-done.b), channel_id=1, source_target_pairs={{0,1},{1,0},{2,3},{3,2},{4,5},{5,4},{6,7},{7,6},{8,9},{9,8},{10,11... | collective-permute-start | bytes 3538952 | tf_op jit(solution)/shard_map/ppermute | solution.py:430
  50.8 2.8 %copy-start.1 = (f32[768,2048]{1,0:T(8,128)S(1)}, f32[768,2048]{1,0:T(8,128)}, u32[]{:S(2)}) copy-start(f32[768,2048]{1,0:T(8,128)} %xn_ref.1) | copy-start | bytes 18874372
  53.6 2.8 %copy-start.3 = (f32[768,2048]{1,0:T(8,128)S(1)}, f32[768,2048]{1,0:T(8,128)}, u32[]{:S(2)}) copy-start(f32[768,2048]{1,0:T(8,128)} %sn_ref.1) | copy-start | bytes 18874372
  70.1 1.3 %copy-start.4 = (f32[4096,128]{1,0:T(8,128)}, f32[4096,128]{1,0:T(8,128)S(1)}, u32[]{:S(2)}) copy-start(f32[4096,128]{1,0:T(8,128)S(1)} %get-tuple-element.28.q_ref) | copy-start | bytes 6291460
  71.4 11.9 %copy-start.5 = (f32[4096,128]{1,0:T(8,128)S(1)}, f32[4096,128]{1,0:T(8,128)}, u32[]{:S(2)}) copy-start(f32[4096,128]{1,0:T(8,128)} %copy-done.4) | copy-start | bytes 6291460
  71.4 19.8 %all-to-all-start.1 = ((f32[128,4,128]{2,1,0:T(4,128)}), f32[128,4,128]{2,1,0:T(4,128)S(1)}, u32[]{:S(2)}, u32[]{:S(2)}) async-start(f32[128,4,128]{2,1,0:T(4,128)} %get-tuple-element.26), calls=%async_computation.1 | async-start | bytes 524288 | tf_op jit(solution)/shard_map/all_to_all | solution.py:433
  91.2 1.1 %copy-start.7 = (f32[1568,128]{1,0:T(8,128)S(1)}, f32[1568,128]{1,0:T(8,128)}, u32[]{:S(2)}) copy-start(f32[1568,128]{1,0:T(8,128)} %copy-done.6) | copy-start | bytes 2408452
  92.3 1.2 %copy-start.9 = (f32[2048,128]{1,0:T(8,128)S(1)}, f32[2048,128]{1,0:T(8,128)}, u32[]{:S(2)}) copy-start(f32[2048,128]{1,0:T(8,128)} %copy-done.8) | copy-start | bytes 3145732
  93.6 1.1 %copy-start.10 = (f32[1568,128]{1,0:T(8,128)S(1)}, f32[1568,128]{1,0:T(8,128)}, u32[]{:S(2)}) copy-start(f32[1568,128]{1,0:T(8,128)} %fusion.cnt_ref) | copy-start | bytes 2408452
  94.7 1.0 copy-start.12
  95.7 1.0 copy-start.14

commit v3 on v2

--- a/solution.py
+++ b/solution.py
@@ -34,6 +34,18 @@
     return jax.ShapeDtypeStruct(shape, dtype)
 
 
+def keep(shape, dtype=F32):
+    return pltpu.VMEM(shape, dtype)
+
+
+def in_hbm(x):
+    return pltpu.with_memory_space_constraint(x, pltpu.HBM)
+
+
+def in_vmem(x):
+    return pltpu.with_memory_space_constraint(x, pltpu.VMEM)
+
+
 def pack_kernel(s_ref, out_ref):
     s = s_ref[0].astype(F32)
     top, bot = s[:64], s[64:]
@@ -111,14 +123,15 @@
                           scratch_shapes=[pltpu.VMEM((FC, W), F32)], compiler_params=PARAMS, name="cols")(rhs, sigma, rhs, sigma, hup, hdn)
 
 
-def rim_kernel(has_ref, xl, sl, xr, sr, xt, st, xb, sb, hup, hdn, hcl, hcr, r_out, secl, secr, sect, secb, X, D, G, S, H, D2, G2, S2):
+def rim_kernel(has_ref, run_ref, slot_ref, xl, sl, xr, sr, xt, st, xb, sb, hup, hdn, hcl, hcr, cnt, strips_out, rows_out, tiles_out, slots_ref,
+               r_out, strips, rows_buf, tiles, sems, X, D, G, S, H, D2, G2, S2):
     up, down, left, right = (has_ref[k] for k in range(4))
     lane = lax.broadcasted_iota(jnp.int32, (1, W), 1)
 
     def stencil(x, d, above, under, side):
         return d * (K1 * x + K2 * ((above + under) + side))
 
-    def strip(x, s, c0, hc, m, a, alive, sec, base):
+    def strip(x, s, c0, hc, m, a, alive, base):
         q = 1 - m
         sel = (lane == a) | (lane == a + 1)
         pad = jnp.zeros((W - 8, W), F32)
@@ -161,13 +174,18 @@
             v = S[q, rows]
             own = slice(8 * k, 8 * k + 8)
             t = 4.0 + s[own, q * W:(q + 1) * W]
-            r_out[base + 8 * k:base + 8 * k + 8] = X[q, rows] - (t * v - ((S[q, r0 - 1:r0 + 7] + S[q, r0 + 1:r0 + 9]) + side))
-            sec[own] = v
-
-    strip(xl, sl, 0, hcl, 1, W - 2, left, secl, 0)
-    strip(xr, sr, C - 2 * W, hcr, 0, 0, right, secr, R)
-
-    def edge(x, s, halo, h, g, o, alive, sec, line, base):
+            res = X[q, rows] - (t * v - ((S[q, r0 - 1:r0 + 7] + S[q, r0 + 1:r0 + 9]) + side))
+            at = slice(base + 8 * k, base + 8 * k + 8)
+            r_out[at] = res
+            strips[0, at] = v
+            strips[1, at] = cnt[at] * res
+
+    strip(xl, sl, 0, hcl, 1, W - 2, left, 0)
+    strip(xr, sr, C - 2 * W, hcr, 0, 0, right, R)
+    copies = [pltpu.make_async_copy(strips, strips_out, sems.at[0]), pltpu.make_async_copy(rows_buf, rows_out, sems.at[1])]
+    copies[0].start()
+
+    def edge(x, s, halo, h, g, o, alive, part, line, base):
         nt = C // W
         tiles = [slice(c * W, (c + 1) * W) for c in range(nt)]
         ok = alive > 0
@@ -188,52 +206,49 @@
         side = sides([S2[c, g:g + 8] for c in range(nt)])
         for c, cols in enumerate(tiles):
             v = S2[c, g:g + 8]
-            sec[:, cols] = v
+            rows_buf[part, :, cols] = v
             at = g + line
             one = slice(at, at + 1)
             t = 4.0 + s[at - 8:at - 7, cols]
             res = x[at - 8:at - 7, cols] - (t * S2[c, one] - ((S2[c, at - 1:at] + S2[c, at + 1:at + 2]) + side[c][line:line + 1]))
             r_out[base + c:base + c + 1] = res
-
-    edge(xt, st, hup, 6, 8, 7, up, sect, 0, 2 * R)
-    edge(xb, sb, hdn, 24, 16, 24, down, secb, 7, 2 * R + 16)
-
-
-def rim(has, rhs, sigma, hup, hdn, hcl, hcr):
+            rows_buf[2, part:part + 1, cols] = cnt[base + c:base + c + 1] * res
+
+    edge(xt, st, hup, 6, 8, 7, up, 0, 0, 2 * R)
+    edge(xb, sb, hdn, 24, 16, 24, down, 1, 7, 2 * R + 16)
+    copies[1].start()
+
+    slots_ref[...] = jnp.zeros_like(slots_ref)
+
+    def body(b, carry):
+        for u in range(16):
+            t = b * 16 + u
+            row = r_out[pl.ds(run_ref[t], 1), :]
+            tiles[pl.ds(t, 1), :] = row
+            slots_ref[pl.ds(slot_ref[t], 1), :] = row
+        return carry
+
+    lax.fori_loop(0, T // 16, body, 0)
+    last = pltpu.make_async_copy(tiles, tiles_out, sems.at[2])
+    last.start()
+    for c in copies:
+        c.wait()
+    last.wait()
+
+
+def rim(has, run, slot, rhs, sigma, hup, hdn, hcl, hcr, cnt):
     left = pl.BlockSpec((R, 2 * W), lambda i: (0, 0))
     right = pl.BlockSpec((R, 2 * W), lambda i: (0, C // (2 * W) - 1))
     top = pl.BlockSpec((16, C), lambda i: (0, 0))
     bottom = pl.BlockSpec((16, C), lambda i: (R // 16 - 1, 0))
-
-    def whole(shape):
-        return pl.BlockSpec(shape, lambda i: (0,) * len(shape))
-
-    outs = [(RIM, W), (R, W), (R, W), (8, C), (8, C)]
+    strips, rows, tiles = (2, 2 * R, W), (3, 8, C), (T, W)
     return pl.pallas_call(
-        rim_kernel, grid=(1,), out_shape=[sds(s) for s in outs],
-        in_specs=[SM, left, left, right, right, top, top, bottom, bottom, whole((4, C)), whole((4, C)), whole((16, FC)), whole((16, FC))],
-        out_specs=[whole(s) for s in outs],
-        scratch_shapes=[pltpu.VMEM((2, FR, W), F32)] * 4 + [pltpu.VMEM((2, FC, W), F32)] + [pltpu.VMEM((C // W, 32, W), F32)] * 3,
-        compiler_params=PARAMS, name="rim")(has, rhs, sigma, rhs, sigma, rhs, sigma, rhs, sigma, hup, hdn, hcl, hcr)
-
-
-def place_kernel(run_ref, slot_ref, r_ref, tiles_ref, slots_ref):
-    slots_ref[...] = jnp.zeros_like(slots_ref)
-
-    def body(b, carry):
-        for u in range(16):
-            t = b * 16 + u
-            row = r_ref[pl.ds(run_ref[t], 1), :]
-            tiles_ref[pl.ds(t, 1), :] = row
-            slots_ref[pl.ds(slot_ref[t], 1), :] = row
-        return carry
-
-    lax.fori_loop(0, T // 16, body, 0)
-
-
-def place(run, slot, r_rim):
-    return pl.pallas_call(place_kernel, out_shape=[sds((T, W)), sds((2 * NG * CAP, W))], in_specs=[SM, SM, VM], out_specs=[VM, VM],
-                          compiler_params=PARAMS, name="place")(run, slot, r_rim)
+        rim_kernel, grid=(1,), out_shape=[pltpu.HBM(strips, F32), pltpu.HBM(rows, F32), pltpu.HBM(tiles, F32), keep((2 * NG * CAP, W))],
+        in_specs=[SM, SM, SM, left, left, right, right, top, top, bottom, bottom, VM, VM, VM, VM, VM],
+        out_specs=[ANY, ANY, ANY, VM],
+        scratch_shapes=[pltpu.VMEM((RIM, W), F32), pltpu.VMEM(strips, F32), pltpu.VMEM(rows, F32), pltpu.VMEM(tiles, F32), pltpu.SemaphoreType.DMA((3,))]
+        + [pltpu.VMEM((2, FR, W), F32)] * 4 + [pltpu.VMEM((2, FC, W), F32)] + [pltpu.VMEM((C // W, 32, W), F32)] * 3,
+        compiler_params=PARAMS, name="rim")(has, run, slot, rhs, sigma, rhs, sigma, rhs, sigma, rhs, sigma, hup, hdn, in_vmem(hcl), in_vmem(hcr), in_vmem(cnt))
 
 
 def product_kernel(first, slots_ref, blk_ref, *refs):
@@ -299,25 +314,19 @@
 
 
 def product_first(slots, blocks):
-    spec = pl.BlockSpec((NG * CAP, W), lambda i: (0, 0))
-
     def kernel(s, b, q, sums):
-        product_kernel(True, s, b, q, sums, None)
-
-    return pl.pallas_call(kernel, grid=(1,), out_shape=[sds((2 * NG * CAP, W)), sds((4, 8, W))],
-                          in_specs=[spec, pl.BlockSpec((NG, PR, W), lambda i: (0, 0, 0))],
-                          out_specs=[spec, pl.BlockSpec((4, 8, W), lambda i: (0, 0, 0))], compiler_params=PARAMS, name="product_a")(slots, blocks)
+        product_kernel(True, s.at[0:NG * CAP], b, q.at[0:NG * CAP], sums, None)
+
+    return pl.pallas_call(kernel, out_shape=[keep((2 * NG * CAP, W)), keep((4, 8, W))], in_specs=[VM, VM], out_specs=[VM, VM],
+                          compiler_params=PARAMS, name="product_a")(slots, in_vmem(blocks))
 
 
 def product_second(slots, blocks, prev, half):
     def kernel(s, b, p, h, q, sums):
-        product_kernel(False, s, b, p, q, sums)
-
-    return pl.pallas_call(kernel, grid=(1,), out_shape=[sds((2 * NG * CAP, W)), sds((2 * NG, 4, W))], input_output_aliases={3: 0},
-                          in_specs=[pl.BlockSpec((NG * CAP, W), lambda i: (1, 0)), pl.BlockSpec((NG, PR, W), lambda i: (0, 0, 0)),
-                                    pl.BlockSpec((4, 8, W), lambda i: (0, 0, 0)), ANY],
-                          out_specs=[pl.BlockSpec((NG * CAP, W), lambda i: (1, 0)), pl.BlockSpec((2 * NG, 4, W), lambda i: (0, 0, 0))],
-                          compiler_params=PARAMS, name="product_b")(slots, blocks, prev, half)
+        product_kernel(False, s.at[NG * CAP:2 * NG * CAP], b, p, q.at[NG * CAP:2 * NG * CAP], sums)
+
+    return pl.pallas_call(kernel, out_shape=[keep((2 * NG * CAP, W)), keep((2 * NG, 4, W))], input_output_aliases={3: 0},
+                          in_specs=[VM, VM, VM, VM], out_specs=[VM, VM], compiler_params=PARAMS, name="product_b")(slots, in_vmem(blocks), prev, half)
 
 
 def order_kernel(slot_ref, q_ref, out_ref):
@@ -331,25 +340,29 @@
 
 
 def order(slot, q):
-    return pl.pallas_call(order_kernel, out_shape=sds((T, W)), in_specs=[SM, VM], out_specs=VM, compiler_params=PARAMS, name="order")(slot, q)
+    return pl.pallas_call(order_kernel, out_shape=keep((T, W)), in_specs=[SM, VM], out_specs=VM, compiler_params=PARAMS, name="order")(slot, q)
 
 
 CH = 8
 TC = T // CH
-
-
-def final_kernel(red_ref, r_ref, q_ref, rim_ref, cnt_ref, secl, secr, sect, secb, field_ref, out_ref, res_ref, dir_ref, coef, bl, br, bt, bb, sems):
+AT = 2
+
+
+def final_kernel(red_ref, r_ref, q_ref, strips_ref, rows_ref, field_ref, out_ref, res_ref, dir_ref, coef, strips, rows, sems):
     step = pl.program_id(0)
     inner = slice(W, C - W)
+    loads = [pltpu.make_async_copy(strips_ref, strips, sems.at[4]), pltpu.make_async_copy(rows_ref, rows, sems.at[5])]
     copies = [
-        pltpu.make_async_copy(bl, out_ref.at[:, 0:W], sems.at[0]),
-        pltpu.make_async_copy(br, out_ref.at[:, C - W:C], sems.at[1]),
-        pltpu.make_async_copy(bt.at[:, inner], out_ref.at[0:8, inner], sems.at[2]),
-        pltpu.make_async_copy(bb.at[:, inner], out_ref.at[R - 8:R, inner], sems.at[3]),
+        pltpu.make_async_copy(strips.at[0, 0:R], out_ref.at[:, 0:W], sems.at[0]),
+        pltpu.make_async_copy(strips.at[0, R:2 * R], out_ref.at[:, C - W:C], sems.at[1]),
+        pltpu.make_async_copy(rows.at[0, :, inner], out_ref.at[0:8, inner], sems.at[2]),
+        pltpu.make_async_copy(rows.at[1, :, inner], out_ref.at[R - 8:R, inner], sems.at[3]),
     ]
 
     @pl.when(step == 0)
     def _():
+        for c in loads:
+            c.start()
         rr = jnp.sum(red_ref[:, 0, :])
         pq = jnp.sum(red_ref[:, 1, :])
         alpha = jnp.full((1, W), rr) / jnp.full((1, W), pq)
@@ -358,23 +371,25 @@
         rr_new = rr - 2.0 * alpha * pq + qq
         coef[0:1] = alpha
         coef[1:2] = rr_new / rr
-        bl[...] = secl[...] + alpha * (cnt_ref[0:R] * rim_ref[0:R])
-        br[...] = secr[...] + alpha * (cnt_ref[R:2 * R] * rim_ref[R:2 * R])
-        bt[...] = sect[...]
-        bb[...] = secb[...]
-        for k in range(1, C // W - 1):
+
+    at = pl.ds(pl.multiple_of(step * TC, TC), TC)
+    r = r_ref[...]
+    res = r - coef[0:1] * q_ref[at, :]
+    res_ref[...] = res
+    dir_ref[...] = res + coef[1:2] * r
+
+    @pl.when(step == AT)
+    def _():
+        for c in loads:
+            c.wait()
+        alpha = coef[0:1]
+        strips[0] = strips[0] + alpha * strips[1]
+        for k in range(C // W):
             lanes = slice(k * W, (k + 1) * W)
-            a = slice(2 * R + k, 2 * R + k + 1)
-            bt[0:1, lanes] = sect[0:1, lanes] + alpha * (cnt_ref[a] * rim_ref[a])
-            b = slice(2 * R + 16 + k, 2 * R + 17 + k)
-            bb[7:8, lanes] = secb[7:8, lanes] + alpha * (cnt_ref[b] * rim_ref[b])
+            rows[0, 0:1, lanes] = rows[0, 0:1, lanes] + alpha * rows[2, 0:1, lanes]
+            rows[1, 7:8, lanes] = rows[1, 7:8, lanes] + alpha * rows[2, 1:2, lanes]
         for c in copies:
             c.start()
-
-    r = r_ref[...]
-    res = r - coef[0:1] * q_ref[...]
-    res_ref[...] = res
-    dir_ref[...] = res + coef[1:2] * r
 
     @pl.when(step == CH - 1)
     def _():
@@ -382,22 +397,19 @@
             c.wait()
 
 
-def final(red, r_tiles, q_tiles, r_rim, cnt, secl, secr, sect, secb, field):
-    def whole(shape):
-        return pl.BlockSpec(shape, lambda i: (0,) * len(shape))
-
+def final(red, r_tiles, q_tiles, strips, rows, field):
     chunk = pl.BlockSpec((TC, W), lambda i: (i, 0))
     return pl.pallas_call(
         final_kernel, grid=(CH,), out_shape=[sds((R, C)), sds((T, W)), sds((T, W))],
-        in_specs=[whole((2 * NG, 4, W)), chunk, chunk, whole((RIM, W)), whole((RIM, W)), whole((R, W)), whole((R, W)), whole((8, C)), whole((8, C)), ANY],
+        in_specs=[VM, chunk, VM, ANY, ANY, ANY],
         out_specs=[ANY, chunk, chunk],
-        scratch_shapes=[pltpu.VMEM((8, W), F32), pltpu.VMEM((R, W), F32), pltpu.VMEM((R, W), F32), pltpu.VMEM((8, C), F32), pltpu.VMEM((8, C), F32),
-                        pltpu.SemaphoreType.DMA((4,))],
-        input_output_aliases={9: 0}, compiler_params=PARAMS, name="final")(red, r_tiles, q_tiles, r_rim, cnt, secl, secr, sect, secb, field)
+        scratch_shapes=[pltpu.VMEM((8, W), F32), pltpu.VMEM((2, 2 * R, W), F32), pltpu.VMEM((3, 8, C), F32), pltpu.SemaphoreType.DMA((6,))],
+        input_output_aliases={5: 0}, compiler_params=PARAMS, name="final")(in_vmem(red), in_hbm(r_tiles), q_tiles, in_hbm(strips), in_hbm(rows), field)
 
 
 def per_device(rhs, sigma, tile_list, tile_owner, schur_blocks):
     core = lax.axis_index("c")
+    big = (in_hbm(rhs), in_hbm(sigma))
     packed = pack(schur_blocks)
     mine = lax.all_to_all(packed, CHIPS, 0, 0, tiled=True)
     nrow, ncol = 16, 8
@@ -408,13 +420,12 @@
 
     rightward = [(i, i + 1) for i in range(ncol - 1)]
     leftward = [(i + 1, i) for i in range(ncol - 1)]
-    to_right, to_left = edge_cols(rhs, sigma, hup, hdn)
+    to_right, to_left = edge_cols(*big, hup, hdn)
     hcl = lax.ppermute(to_right, COLS, rightward)
     hcr = lax.ppermute(to_left, COLS, leftward)
     row_at = lax.axis_index(ROWS)
     col_at = lax.axis_index(COLS)
     has = jnp.stack([row_at > 0, row_at < nrow - 1, col_at > 0, col_at < ncol - 1]).astype(jnp.int32)
-    r_rim, secl, secr, sect, secb = rim(has, rhs, sigma, hup, hdn, hcl, hcr)
     runs = C // W
     trow, tcol = tile_list // runs, tile_list % runs
     run = jnp.where(tcol == 0, trow, jnp.where(tcol == runs - 1, R + trow, jnp.where(trow == 0, 2 * R + tcol, 2 * R + 16 + tcol)))
@@ -425,15 +436,16 @@
     slot = (((owner & 1) ^ core) * NG + (owner >> 1)) * CAP + rank
     hits = (jnp.arange(RIM, dtype=jnp.int32)[:, None] == run[None, :]).astype(BF16)
     cnt = jnp.dot(hits, jnp.ones((T, W), BF16), preferred_element_type=F32)
-    r_tiles, slots = place(run, slot, r_rim)
+    strips, rows, r_tiles, slots = rim(has, run, slot, *big, hup, hdn, hcl, hcr, cnt)
     mine, slots = lax.optimization_barrier((mine, slots))
     theirs = lax.ppermute(mine, "c", [(0, 1), (1, 0)])
     q, part = product_first(slots, mine)
     q, sums = product_second(slots, theirs, part, q)
+    q, sums, late_rhs, late_sigma = lax.optimization_barrier((q, sums, rhs, sigma))
     red = lax.all_to_all(sums, ALL, 0, 0, tiled=True)
     q_tiles = order(slot, q)
-    field = dense(rhs, sigma)
-    return tuple(final(red, r_tiles, q_tiles, r_rim, cnt, secl, secr, sect, secb, field))
+    field = dense(in_hbm(late_rhs), in_hbm(late_sigma))
+    return tuple(final(red, r_tiles, q_tiles, strips, rows, field))
 
 
 def solution(mesh):

time: 101 us -> 89.2 us (0.88)
  local copies, waits for them, and re-layouts: 24.2 us -> 5.08 us
  Pallas kernels: 29.7 us -> 41.6 us
  waiting for transfers between devices: 8.79 us -> 3.8 us
    unnamed x36 -> x12, local copies, waits for them, and re-layouts: 22.1 us -> 3.67 us
    pallas_call x1, Pallas kernels: 7.24 us -> 13.1 us  [dense(): pl.pallas_call(dense_kernel, grid=(R // n,), out_shape=sds((R, C)), in_sp...]
    all_to_all x1, waiting for transfers between devices: 5 us -> 0.01 us  [per_device(): red = lax.all_to_all(sums, ALL, 0, 0, tiled=True)]
    pallas_call x1, Pallas kernels: 3.75 us -> 6.54 us  [final(): pl.pallas_call(final_kernel, grid=(CH,), out_shape=[sds((R, C)), sds((T,...]
    pallas_call x5 -> x4, Pallas kernels: 17 us -> 18.8 us  [the longest x1 9.5 us: rim(): pl.pallas_call(rim_kernel, grid=(1,), out_shape=[pltpu.HBM(strips, F32),...]
    pallas_call x1, Pallas kernels: 0.53 us -> 1.95 us  [edge_cols(): pl.pallas_call(cols_kernel, grid=(1,), out_shape=[sds((16, FC))] * 2, in_...]
  transfers between devices with their start and end apart: 7 -> 7, of which waited for: 2 -> 1; matrix products, arithmetic and copies ran while one was open for 6% -> 5% of each run, Pallas kernels for 22% -> 36%
where the time goes in v3:
time: 89.2 us; the launch traced here: 88.2 us
  Pallas kernels  41.6 us (47%)
  starting transfers between devices  32.5 us (36%)
  local copies, waits for them, and re-layouts  5.08 us (6%)
  waiting for transfers between devices  3.8 us (4%)
  matrix products  3.17 us (4%)
  other arithmetic  1.21 us (1%)
    pallas_call x1, Pallas kernels, dense(): pl.pallas_call(dense_kernel, grid=(R // n,), out_shape=sds((R, C)), in_sp...  13.1 us
    all_to_all x1, starting transfers between devices, per_device(): mine = lax.all_to_all(packed, CHIPS, 0, 0, tiled=True)  11.6 us
    pallas_call x1, Pallas kernels, rim(): pl.pallas_call(rim_kernel, grid=(1,), out_shape=[pltpu.HBM(strips, F32),...  9.5 us
    all_to_all x1, starting transfers between devices, per_device(): red = lax.all_to_all(sums, ALL, 0, 0, tiled=True)  8.72 us
    pallas_call x1, Pallas kernels, final(): pl.pallas_call(final_kernel, grid=(CH,), out_shape=[sds((R, C)), sds((T,...  6.54 us
    ppermute x1, starting transfers between devices, per_device(): hcl = lax.ppermute(to_right, COLS, rightward)  4.59 us
    ppermute x1, starting transfers between devices, per_device(): hup = lax.ppermute(jnp.concatenate([rhs[-2:], sigma[-2:]]), ROWS, up)  4.36 us
    ppermute x1, waiting for transfers between devices, per_device(): hcr = lax.ppermute(to_left, COLS, leftward)  3.78 us
  transfers between devices with their start and end apart: 7, of which 1 were waited for; matrix products, arithmetic and copies ran while one was open for 5% of the time, Pallas kernels for 36%

profile of v3, /device:TPU:1, one launch (start us, length us, event | category | flops | bytes accessed | tf_op | source)
XLA Modules:
  0.0 88.2 jit_solution(10648000643411236670)
XLA Ops:
  0.6 0.0 copy-start.4
  0.6 1.0 %fusion.11 = (f32[2,2048]{1,0:T(2,128)S(1)}, f32[2,2048]{1,0:T(2,128)S(1)}, f32[2,2048]{1,0:T(2,128)S(1)}, f32[2,2048]{1,0:T(2,128)S(1)}) fusion(f32[768,2048]{1,0:T(8,128)} %xn_ref, f32[768,2048]{1,0:T(8,128)} %sn_ref), kind=kLoop, calls=%fused_computation.28 | loop fusion | bytes 131072 | tf_op jit(solution)/shard_map/slice | solution.py:419
  1.6 4.4 %collective-permute-start = (f32[4,2048]{1,0:T(4,128)S(1)}, f32[4,2048]{1,0:T(4,128)S(1)}, u32[]{:S(2)}, u32[]{:S(2)}) collective-permute-start(f32[4,2048]{1,0:T(4,128)S(1)} %pad_maximum_fusion), channel_id=1, source_target_pairs={{0,8},{8,16},{16,24},{24,32},{32,40},{40,48},{48,56},{56,64},{64,7... | collective-permute-start | bytes 98312 | tf_op jit(solution)/shard_map/ppermute | solution.py:418
  6.0 1.3 %collective-permute-start.1 = (f32[4,2048]{1,0:T(4,128)S(1)}, f32[4,2048]{1,0:T(4,128)S(1)}, u32[]{:S(2)}, u32[]{:S(2)}) collective-permute-start(f32[4,2048]{1,0:T(4,128)S(1)} %pad_maximum_fusion.1), channel_id=1, source_target_pairs={{8,0},{16,8},{24,16},{32,24},{40,32},{48,40},{56,48},{64,56},{72,6... | collective-permute-start | bytes 98312 | tf_op jit(solution)/shard_map/ppermute | solution.py:419
  7.3 0.0 copy-start.3
  7.3 0.7 copy-done.3
  8.1 1.1 %pack.1 = bf16[64,72,128]{2,1,0:T(8,128)(2,1)} custom-call(bf16[1,128,128]{2,1,0:T(8,128)(2,1)S(1)} %copy-done.3), custom_call_target="tpu_custom_call" | custom-call | tf_op jit(solution)/shard_map/pack/pallas_call | solution.py:65
  9.2 11.6 %all-to-all-start = ((bf16[64,72,128]{2,1,0:T(8,128)(2,1)}), bf16[64,72,128]{2,1,0:T(8,128)(2,1)S(1)}, u32[]{:S(2)}, u32[]{:S(2)}) async-start(bf16[64,72,128]{2,1,0:T(8,128)(2,1)} %pack.1), calls=%async_computation | async-start | bytes 2359296 | tf_op jit(solution)/shard_map/all_to_all | solution.py:414
  20.8 0.0 copy-done.4
  20.8 0.1 copy.11
  20.9 0.0 copy-start.5
  20.9 0.3 fusion.4
  21.3 0.1 broadcast_add_fusion
  21.4 0.3 copy.12
  21.7 0.6 fusion.3
  22.4 0.0 copy-done.5
  22.4 3.2 %fusion.cnt = f32[1568,128]{1,0:T(8,128)} fusion(s32[2048]{0:T(1024)S(1)} %get-tuple-element.42.run_ref), kind=kOutput, calls=%fused_computation.1 | convolution fusion | flops 825294848 | bytes 811008 | tf_op jit(solution)/shard_map/dot_general | solution.py:438
  25.6 0.0 copy-start.2
  25.6 0.0 collective-permute-done.hup
  25.6 0.0 collective-permute-done.1.hdn
  25.6 2.0 %cols.1 = (f32[16,896]{1,0:T(8,128)S(1)}, f32[16,896]{1,0:T(8,128)S(1)}) custom-call(f32[768,2048]{1,0:T(8,128)} %xn_ref, f32[768,2048]{1,0:T(8,128)} %sn_ref, f32[768,2048]{1,0:T(8,128)} %xn_ref, f32[768,2048]{1,0:T(8,128)} %sn_ref, f32[4,2048]{1,0:T(4,128)S(1)} %collective-permute-done.hup, f32[4,2048]{1,0:T(4,128)S(1)} %collective-permute-done.1.hdn), custom_call_target="tpu_custom_call" | custom-call | tf_op jit(solution)/shard_map/cols/pallas_call | solution.py:122
  27.6 4.6 %collective-permute-start.2 = (f32[16,896]{1,0:T(8,128)S(1)}, f32[16,896]{1,0:T(8,128)S(1)}, u32[]{:S(2)}, u32[]{:S(2)}) collective-permute-start(f32[16,896]{1,0:T(8,128)S(1)} %get-tuple-element.19), channel_id=1, source_target_pairs={{0,1},{1,2},{2,3},{3,4},{4,5},{5,6},{6,7},{8,9},{9,10},{10,11},{11... | collective-permute-start | bytes 172040 | tf_op jit(solution)/shard_map/ppermute | solution.py:424
  32.1 1.9 %collective-permute-start.3 = (f32[16,896]{1,0:T(8,128)S(1)}, f32[16,896]{1,0:T(8,128)S(1)}, u32[]{:S(2)}, u32[]{:S(2)}) collective-permute-start(f32[16,896]{1,0:T(8,128)S(1)} %get-tuple-element.20), channel_id=1, source_target_pairs={{1,0},{2,1},{3,2},{4,3},{5,4},{6,5},{7,6},{9,8},{10,9},{11,10},{12... | collective-permute-start | bytes 172040 | tf_op jit(solution)/shard_map/ppermute | solution.py:425
  34.1 0.1 add_convert_fusion.has_ref
  34.2 0.0 collective-permute-done.2.hcl
  34.2 3.8 %collective-permute-done.3.hcr = f32[16,896]{1,0:T(8,128)S(1)} collective-permute-done((f32[16,896]{1,0:T(8,128)S(1)}, f32[16,896]{1,0:T(8,128)S(1)}, u32[]{:S(2)}, u32[]{:S(2)}) %collective-permute-start.3) | collective-permute-done | bytes 57376 | tf_op jit(solution)/shard_map/ppermute | solution.py:425
  37.9 0.0 copy-done.2
  37.9 9.5 %rim.1 = (f32[2,1536,128]{2,1,0:T(8,128)}, f32[3,8,2048]{2,1,0:T(8,128)}, f32[2048,128]{1,0:T(8,128)}, f32[4096,128]{1,0:T(8,128)S(1)}) custom-call(s32[4]{0:T(128)S(1)} %add_convert_fusion.has_ref, s32[2048]{0:T(1024)S(1)} %get-tuple-element.42.run_ref, s32[2048]{0:T(1024)S(1)} %get-tuple-element.41.slot_ref, f32[768,2048]{1,0:T(8,128)} %xn_ref, ...), custom_call_target="tpu_custom_call" | custom-call | tf_op jit(solution)/shard_map/rim/pallas_call | solution.py:245
  47.5 0.0 all-to-all-done.b
  47.5 0.1 collective-permute-start.4
  47.6 3.0 %product_a.1 = (f32[4096,128]{1,0:T(8,128)S(1)}, f32[4,8,128]{2,1,0:T(8,128)S(1)}) custom-call(f32[4096,128]{1,0:T(8,128)S(1)} %get-tuple-element.22.s, bf16[64,72,128]{2,1,0:T(8,128)(2,1)S(1)} %all-to-all-done.b), custom_call_target="tpu_custom_call" | custom-call | tf_op jit(solution)/shard_map/product_a/pallas_call | solution.py:320
  50.6 0.0 collective-permute-done.4.b
  50.6 3.5 %product_b.1 = (f32[4096,128]{1,0:T(8,128)S(1)}, f32[128,4,128]{2,1,0:T(4,128)}) custom-call(f32[4096,128]{1,0:T(8,128)S(1)} %get-tuple-element.22.s, bf16[64,72,128]{2,1,0:T(8,128)(2,1)S(1)} %collective-permute-done.4.b, f32[4,8,128]{2,1,0:T(8,128)S(1)} %get-tuple-element.24.p, f32[4096,128]{1,0:T(8,128)S(1)} %get-tuple-element.25.h), custom_call_target="tpu_custom_call", output_to_operand_aliasing={{0}: (3, {})} | custom-call | tf_op jit(solution)/shard_map/product_b/pallas_call | solution.py:328
  54.1 0.0 copy-start
  54.1 1.3 %copy-done = f32[4096,128]{1,0:T(8,128)} copy-done((f32[4096,128]{1,0:T(8,128)}, f32[4096,128]{1,0:T(8,128)S(1)}, u32[]{:S(2)}) %copy-start) | copy-done | bytes 2097176
  55.4 8.7 %all-to-all-start.1 = ((f32[128,4,128]{2,1,0:T(4,128)}), f32[128,4,128]{2,1,0:T(4,128)S(1)}, u32[]{:S(2)}, u32[]{:S(2)}) async-start(f32[128,4,128]{2,1,0:T(4,128)} %get-tuple-element.28), calls=%async_computation.1 | async-start | bytes 524288 | tf_op jit(solution)/shard_map/all_to_all | solution.py:445
  64.1 0.0 copy-start.1
  64.1 1.6 %copy-done.1 = f32[4096,128]{1,0:T(8,128)S(1)} copy-done((f32[4096,128]{1,0:T(8,128)S(1)}, f32[4096,128]{1,0:T(8,128)}, u32[]{:S(2)}) %copy-start.1) | copy-done | bytes 2097176
  65.7 2.8 %order.1.q_ref = f32[2048,128]{1,0:T(8,128)S(1)} custom-call(s32[2048]{0:T(1024)S(1)} %get-tuple-element.41.slot_ref, f32[4096,128]{1,0:T(8,128)S(1)} %copy-done.1), custom_call_target="tpu_custom_call" | custom-call | tf_op jit(solution)/shard_map/order/pallas_call | solution.py:343
  68.5 13.1 %dense.1.field_ref = f32[768,2048]{1,0:T(8,128)} custom-call(f32[768,2048]{1,0:T(8,128)} %xn_ref, f32[768,2048]{1,0:T(8,128)} %sn_ref, f32[768,2048]{1,0:T(8,128)} %xn_ref, f32[768,2048]{1,0:T(8,128)} %sn_ref, f32[768,2048]{1,0:T(8,128)} %xn_ref, f32[768,2048]{1,0:T(8,128)} %sn_ref), custom_call_target="tpu_custom_call" | custom-call | tf_op jit(solution)/shard_map/dense/pallas_call | solution.py:98
  81.7 0.0 all-to-all-done.1.red_ref
  81.7 6.5 %final.1 = (f32[768,2048]{1,0:T(8,128)}, f32[2048,128]{1,0:T(8,128)}, f32[2048,128]{1,0:T(8,128)}) custom-call(f32[128,4,128]{2,1,0:T(4,128)S(1)} %all-to-all-done.1.red_ref, f32[2048,128]{1,0:T(8,128)} %get-tuple-element.29.r_ref, f32[2048,128]{1,0:T(8,128)S(1)} %order.1.q_ref, ...), custom_call_target="tpu_custom_call", output_to_operand_aliasing={{0}: (5, {})} | custom-call | tf_op jit(solution)/shard_map/final/pallas_call | solution.py:402
  (6 shorter events, 0.1 us)
Async XLA Ops:
  0.6 20.2 %copy-start.4 = (s32[2048,1]{0,1:T(1,128)S(1)}, s32[2048,1]{0,1:T(1,128)}, u32[]{:S(2)}) copy-start(s32[2048,1]{0,1:T(1,128)} %param.8) | copy-start | bytes 24580
  1.6 24.0 %collective-permute-start = (f32[4,2048]{1,0:T(4,128)S(1)}, f32[4,2048]{1,0:T(4,128)S(1)}, u32[]{:S(2)}, u32[]{:S(2)}) collective-permute-start(f32[4,2048]{1,0:T(4,128)S(1)} %pad_maximum_fusion), channel_id=1, source_target_pairs={{0,8},{8,16},{16,24},{24,32},{32,40},{40,48},{48,56},{56,64},{64,7... | collective-permute-start | bytes 98312 | tf_op jit(solution)/shard_map/ppermute | solution.py:418
  6.0 19.6 %collective-permute-start.1 = (f32[4,2048]{1,0:T(4,128)S(1)}, f32[4,2048]{1,0:T(4,128)S(1)}, u32[]{:S(2)}, u32[]{:S(2)}) collective-permute-start(f32[4,2048]{1,0:T(4,128)S(1)} %pad_maximum_fusion.1), channel_id=1, source_target_pairs={{8,0},{16,8},{24,16},{32,24},{40,32},{48,40},{56,48},{64,56},{72,6... | collective-permute-start | bytes 98312 | tf_op jit(solution)/shard_map/ppermute | solution.py:419
  7.3 0.8 copy-start.3
  9.2 38.2 %all-to-all-start = ((bf16[64,72,128]{2,1,0:T(8,128)(2,1)}), bf16[64,72,128]{2,1,0:T(8,128)(2,1)S(1)}, u32[]{:S(2)}, u32[]{:S(2)}) async-start(bf16[64,72,128]{2,1,0:T(8,128)(2,1)} %pack.1), calls=%async_computation | async-start | bytes 2359296 | tf_op jit(solution)/shard_map/all_to_all | solution.py:414
  20.9 1.5 %copy-start.5 = (s32[2048]{0:T(1024)S(1)}, s32[2048]{0:T(1024)}, u32[]{:S(2)}) copy-start(s32[2048]{0:T(1024)} %param.7) | copy-start | bytes 24580
  25.6 12.4 %copy-start.2 = (f32[1568,128]{1,0:T(8,128)S(1)}, f32[1568,128]{1,0:T(8,128)}, u32[]{:S(2)}) copy-start(f32[1568,128]{1,0:T(8,128)} %fusion.cnt) | copy-start | bytes 2408452
  27.6 6.6 %collective-permute-start.2 = (f32[16,896]{1,0:T(8,128)S(1)}, f32[16,896]{1,0:T(8,128)S(1)}, u32[]{:S(2)}, u32[]{:S(2)}) collective-permute-start(f32[16,896]{1,0:T(8,128)S(1)} %get-tuple-element.19), channel_id=1, source_target_pairs={{0,1},{1,2},{2,3},{3,4},{4,5},{5,6},{6,7},{8,9},{9,10},{10,11},{11... | collective-permute-start | bytes 172040 | tf_op jit(solution)/shard_map/ppermute | solution.py:424
  32.1 5.8 %collective-permute-start.3 = (f32[16,896]{1,0:T(8,128)S(1)}, f32[16,896]{1,0:T(8,128)S(1)}, u32[]{:S(2)}, u32[]{:S(2)}) collective-permute-start(f32[16,896]{1,0:T(8,128)S(1)} %get-tuple-element.20), channel_id=1, source_target_pairs={{1,0},{2,1},{3,2},{4,3},{5,4},{6,5},{7,6},{9,8},{10,9},{11,10},{12... | collective-permute-start | bytes 172040 | tf_op jit(solution)/shard_map/ppermute | solution.py:425
  47.5 3.1 %collective-permute-start.4 = (bf16[64,72,128]{2,1,0:T(8,128)(2,1)S(1)}, bf16[64,72,128]{2,1,0:T(8,128)(2,1)S(1)}, u32[]{:S(2)}, u32[]{:S(2)}) collective-permute-start(bf16[64,72,128]{2,1,0:T(8,128)(2,1)S(1)} %all-to-all-done.b), channel_id=1, source_target_pairs={{0,1},{1,0},{2,3},{3,2},{4,5},{5,4},{6,7},{7,6},{8,9},{9,8},{10,11... | collective-permute-start | bytes 3538952 | tf_op jit(solution)/shard_map/ppermute | solution.py:441
  54.1 1.3 %copy-start = (f32[4096,128]{1,0:T(8,128)}, f32[4096,128]{1,0:T(8,128)S(1)}, u32[]{:S(2)}) copy-start(f32[4096,128]{1,0:T(8,128)S(1)} %get-tuple-element.30.q_ref) | copy-start | bytes 6291460
  55.4 26.3 %all-to-all-start.1 = ((f32[128,4,128]{2,1,0:T(4,128)}), f32[128,4,128]{2,1,0:T(4,128)S(1)}, u32[]{:S(2)}, u32[]{:S(2)}) async-start(f32[128,4,128]{2,1,0:T(4,128)} %get-tuple-element.28), calls=%async_computation.1 | async-start | bytes 524288 | tf_op jit(solution)/shard_map/all_to_all | solution.py:445
  64.1 1.6 %copy-start.1 = (f32[4096,128]{1,0:T(8,128)S(1)}, f32[4096,128]{1,0:T(8,128)}, u32[]{:S(2)}) copy-start(f32[4096,128]{1,0:T(8,128)} %copy-done) | copy-start | bytes 6291460

commit v4 on v3

--- a/solution.py
+++ b/solution.py
@@ -23,7 +23,7 @@
 VM = pl.BlockSpec(memory_space=pltpu.VMEM)
 SM = pl.BlockSpec(memory_space=pltpu.SMEM)
 ANY = pl.BlockSpec(memory_space=pl.ANY)
-ND = 8
+ND = 16
 C1 = 0.6111111
 K1 = C1 + 2.75 * (1.0 - C1)
 K2 = 2.75 * C1
@@ -315,18 +315,20 @@
 
 def product_first(slots, blocks):
     def kernel(s, b, q, sums):
-        product_kernel(True, s.at[0:NG * CAP], b, q.at[0:NG * CAP], sums, None)
-
-    return pl.pallas_call(kernel, out_shape=[keep((2 * NG * CAP, W)), keep((4, 8, W))], in_specs=[VM, VM], out_specs=[VM, VM],
+        here = q.at[0:NG * CAP]
+        product_kernel(True, here, b, here, sums, None)
+
+    return pl.pallas_call(kernel, out_shape=[keep((2 * NG * CAP, W)), keep((4, 8, W))], in_specs=[VM, VM], out_specs=[VM, VM], input_output_aliases={0: 0},
                           compiler_params=PARAMS, name="product_a")(slots, in_vmem(blocks))
 
 
-def product_second(slots, blocks, prev, half):
-    def kernel(s, b, p, h, q, sums):
-        product_kernel(False, s.at[NG * CAP:2 * NG * CAP], b, p, q.at[NG * CAP:2 * NG * CAP], sums)
-
-    return pl.pallas_call(kernel, out_shape=[keep((2 * NG * CAP, W)), keep((2 * NG, 4, W))], input_output_aliases={3: 0},
-                          in_specs=[VM, VM, VM, VM], out_specs=[VM, VM], compiler_params=PARAMS, name="product_b")(slots, in_vmem(blocks), prev, half)
+def product_second(slots, blocks, prev):
+    def kernel(s, b, p, q, sums):
+        here = q.at[NG * CAP:2 * NG * CAP]
+        product_kernel(False, here, b, p, here, sums)
+
+    return pl.pallas_call(kernel, out_shape=[keep((2 * NG * CAP, W)), keep((2 * NG, 4, W))], input_output_aliases={0: 0},
+                          in_specs=[VM, VM, VM], out_specs=[VM, VM], compiler_params=PARAMS, name="product_b")(slots, in_vmem(blocks), prev)
 
 
 def order_kernel(slot_ref, q_ref, out_ref):
@@ -343,84 +345,81 @@
     return pl.pallas_call(order_kernel, out_shape=keep((T, W)), in_specs=[SM, VM], out_specs=VM, compiler_params=PARAMS, name="order")(slot, q)
 
 
-CH = 8
+CH = 4
 TC = T // CH
-AT = 2
-
-
-def final_kernel(red_ref, r_ref, q_ref, strips_ref, rows_ref, field_ref, out_ref, res_ref, dir_ref, coef, strips, rows, sems):
-    step = pl.program_id(0)
+
+
+def final_kernel(red_ref, r_hbm, q_ref, strips_ref, rows_ref, field_ref, out_ref, res_hbm, dir_hbm, r_buf, res_buf, dir_buf, strips, rows, ins, outs):
     inner = slice(W, C - W)
-    loads = [pltpu.make_async_copy(strips_ref, strips, sems.at[4]), pltpu.make_async_copy(rows_ref, rows, sems.at[5])]
-    copies = [
-        pltpu.make_async_copy(strips.at[0, 0:R], out_ref.at[:, 0:W], sems.at[0]),
-        pltpu.make_async_copy(strips.at[0, R:2 * R], out_ref.at[:, C - W:C], sems.at[1]),
-        pltpu.make_async_copy(rows.at[0, :, inner], out_ref.at[0:8, inner], sems.at[2]),
-        pltpu.make_async_copy(rows.at[1, :, inner], out_ref.at[R - 8:R, inner], sems.at[3]),
-    ]
-
-    @pl.when(step == 0)
-    def _():
-        for c in loads:
-            c.start()
-        rr = jnp.sum(red_ref[:, 0, :])
-        pq = jnp.sum(red_ref[:, 1, :])
-        alpha = jnp.full((1, W), rr) / jnp.full((1, W), pq)
-        t = alpha / red_ref[:, 3, :]
-        qq = jnp.sum(t * t * red_ref[:, 2, :])
-        rr_new = rr - 2.0 * alpha * pq + qq
-        coef[0:1] = alpha
-        coef[1:2] = rr_new / rr
-
-    at = pl.ds(pl.multiple_of(step * TC, TC), TC)
-    r = r_ref[...]
-    res = r - coef[0:1] * q_ref[at, :]
-    res_ref[...] = res
-    dir_ref[...] = res + coef[1:2] * r
-
-    @pl.when(step == AT)
-    def _():
-        for c in loads:
+    parts = [slice(k * TC, (k + 1) * TC) for k in range(CH)]
+    tiles_in = [pltpu.make_async_copy(r_hbm.at[p], r_buf.at[p], ins.at[k]) for k, p in enumerate(parts)]
+    rim_in = [pltpu.make_async_copy(strips_ref, strips, ins.at[CH]), pltpu.make_async_copy(rows_ref, rows, ins.at[CH + 1])]
+    for c in tiles_in + rim_in:
+        c.start()
+    rr = jnp.sum(red_ref[:, 0, :])
+    pq = jnp.sum(red_ref[:, 1, :])
+    alpha = jnp.full((1, W), rr) / jnp.full((1, W), pq)
+    t = alpha / red_ref[:, 3, :]
+    qq = jnp.sum(t * t * red_ref[:, 2, :])
+    beta = (rr - 2.0 * alpha * pq + qq) / rr
+    sent = []
+
+    def send(src, dst):
+        c = pltpu.make_async_copy(src, dst, outs.at[len(sent)])
+        c.start()
+        sent.append(c)
+
+    def rim_out():
+        for c in rim_in:
             c.wait()
-        alpha = coef[0:1]
         strips[0] = strips[0] + alpha * strips[1]
+        send(strips.at[0, 0:R], out_ref.at[:, 0:W])
+        send(strips.at[0, R:2 * R], out_ref.at[:, C - W:C])
         for k in range(C // W):
             lanes = slice(k * W, (k + 1) * W)
             rows[0, 0:1, lanes] = rows[0, 0:1, lanes] + alpha * rows[2, 0:1, lanes]
             rows[1, 7:8, lanes] = rows[1, 7:8, lanes] + alpha * rows[2, 1:2, lanes]
-        for c in copies:
-            c.start()
-
-    @pl.when(step == CH - 1)
-    def _():
-        for c in copies:
-            c.wait()
+        send(rows.at[0, :, inner], out_ref.at[0:8, inner])
+        send(rows.at[1, :, inner], out_ref.at[R - 8:R, inner])
+
+    for k, p in enumerate(parts):
+        tiles_in[k].wait()
+        r = r_buf[p]
+        res = r - alpha * q_ref[p]
+        res_buf[p] = res
+        dir_buf[p] = res + beta * r
+        send(res_buf.at[p], res_hbm.at[p])
+        send(dir_buf.at[p], dir_hbm.at[p])
+        if k == 1:
+            rim_out()
+    for c in sent:
+        c.wait()
 
 
 def final(red, r_tiles, q_tiles, strips, rows, field):
-    chunk = pl.BlockSpec((TC, W), lambda i: (i, 0))
     return pl.pallas_call(
-        final_kernel, grid=(CH,), out_shape=[sds((R, C)), sds((T, W)), sds((T, W))],
-        in_specs=[VM, chunk, VM, ANY, ANY, ANY],
-        out_specs=[ANY, chunk, chunk],
-        scratch_shapes=[pltpu.VMEM((8, W), F32), pltpu.VMEM((2, 2 * R, W), F32), pltpu.VMEM((3, 8, C), F32), pltpu.SemaphoreType.DMA((6,))],
+        final_kernel, out_shape=[sds((R, C)), sds((T, W)), sds((T, W))],
+        in_specs=[VM, ANY, VM, ANY, ANY, ANY], out_specs=[ANY, ANY, ANY],
+        scratch_shapes=[pltpu.VMEM((T, W), F32)] * 3 + [pltpu.VMEM((2, 2 * R, W), F32), pltpu.VMEM((3, 8, C), F32),
+                        pltpu.SemaphoreType.DMA((CH + 2,)), pltpu.SemaphoreType.DMA((2 * CH + 4,))],
         input_output_aliases={5: 0}, compiler_params=PARAMS, name="final")(in_vmem(red), in_hbm(r_tiles), q_tiles, in_hbm(strips), in_hbm(rows), field)
 
 
 def per_device(rhs, sigma, tile_list, tile_owner, schur_blocks):
     core = lax.axis_index("c")
     big = (in_hbm(rhs), in_hbm(sigma))
-    packed = pack(schur_blocks)
+    packed, *ready = lax.optimization_barrier((pack(schur_blocks), rhs, sigma))
     mine = lax.all_to_all(packed, CHIPS, 0, 0, tiled=True)
     nrow, ncol = 16, 8
     up = [(i, i + 1) for i in range(nrow - 1)]
     down = [(i + 1, i) for i in range(nrow - 1)]
-    hup = lax.ppermute(jnp.concatenate([rhs[-2:], sigma[-2:]]), ROWS, up)
-    hdn = lax.ppermute(jnp.concatenate([rhs[:2], sigma[:2]]), ROWS, down)
+    tail, head = jnp.concatenate([ready[0][-2:], ready[1][-2:]]), jnp.concatenate([ready[0][:2], ready[1][:2]])
+    hup = lax.ppermute(tail, ROWS, up)
+    hdn = lax.ppermute(head, ROWS, down)
 
     rightward = [(i, i + 1) for i in range(ncol - 1)]
     leftward = [(i + 1, i) for i in range(ncol - 1)]
-    to_right, to_left = edge_cols(*big, hup, hdn)
+    to_right, to_left, tile_list = lax.optimization_barrier((*edge_cols(*big, hup, hdn), tile_list))
     hcl = lax.ppermute(to_right, COLS, rightward)
     hcr = lax.ppermute(to_left, COLS, leftward)
     row_at = lax.axis_index(ROWS)
@@ -440,7 +439,7 @@
     mine, slots = lax.optimization_barrier((mine, slots))
     theirs = lax.ppermute(mine, "c", [(0, 1), (1, 0)])
     q, part = product_first(slots, mine)
-    q, sums = product_second(slots, theirs, part, q)
+    q, sums = product_second(q, theirs, part)
     q, sums, late_rhs, late_sigma = lax.optimization_barrier((q, sums, rhs, sigma))
     red = lax.all_to_all(sums, ALL, 0, 0, tiled=True)
     q_tiles = order(slot, q)

time: 89.2 us -> 83.2 us (0.933)
  Pallas kernels: 41.6 us -> 35.8 us
  starting transfers between devices: 32.5 us -> 36.4 us
  local copies, waits for them, and re-layouts: 5.08 us -> 2.17 us
    ppermute x1, starting transfers between devices: 4.59 us -> 10.6 us  [per_device(): hcl = lax.ppermute(to_right, COLS, rightward)]
    pallas_call x1, Pallas kernels: 6.54 us -> 3.55 us  [final(): pl.pallas_call(final_kernel, out_shape=[sds((R, C)), sds((T, W)), sds((T,...]
    unnamed x12 -> x6, local copies, waits for them, and re-layouts: 3.67 us -> 0.76 us
    pallas_call x1, Pallas kernels: 13.1 us -> 10.5 us  [dense(): pl.pallas_call(dense_kernel, grid=(R // n,), out_shape=sds((R, C)), in_sp...]
    ppermute x2, waiting for transfers between devices: 0.01 us -> 2.68 us  [the longest x1 2.43 us: per_device(): hdn = lax.ppermute(head, ROWS, down)]
    ppermute x1, waiting for transfers between devices: 3.78 us -> 1.24 us  [per_device(): hcr = lax.ppermute(to_left, COLS, leftward)]
    ppermute x2, starting transfers between devices: 5.65 us -> 4.21 us  [the longest x1 2.92 us: per_device(): hup = lax.ppermute(tail, ROWS, up)]
    all_to_all x1, starting transfers between devices: 8.72 us -> 7.64 us  [per_device(): red = lax.all_to_all(sums, ALL, 0, 0, tiled=True)]
  transfers between devices with their start and end apart: 7 -> 7, of which waited for: 1 -> 3; matrix products, arithmetic and copies ran while one was open for 5% -> 6% of each run, Pallas kernels for 36% -> 33%
where the time goes in v4:
time: 83.2 us; the launch traced here: 82.6 us
  starting transfers between devices  36.4 us (44%)
  Pallas kernels  35.8 us (43%)
  waiting for transfers between devices  3.92 us (5%)
  matrix products  2.28 us (3%)
  local copies, waits for them, and re-layouts  2.17 us (3%)
  other arithmetic  1.22 us (1%)
  between operations  0.85 us (1%)
    all_to_all x1, starting transfers between devices, per_device(): mine = lax.all_to_all(packed, CHIPS, 0, 0, tiled=True)  12 us
    ppermute x1, starting transfers between devices, per_device(): hcl = lax.ppermute(to_right, COLS, rightward)  10.6 us
    pallas_call x1, Pallas kernels, dense(): pl.pallas_call(dense_kernel, grid=(R // n,), out_shape=sds((R, C)), in_sp...  10.5 us
    pallas_call x1, Pallas kernels, rim(): pl.pallas_call(rim_kernel, grid=(1,), out_shape=[pltpu.HBM(strips, F32),...  9.48 us
    all_to_all x1, starting transfers between devices, per_device(): red = lax.all_to_all(sums, ALL, 0, 0, tiled=True)  7.64 us
    pallas_call x1, Pallas kernels, final(): pl.pallas_call(final_kernel, out_shape=[sds((R, C)), sds((T, W)), sds((T,...  3.55 us
    pallas_call x1, Pallas kernels, product_second(): pl.pallas_call(kernel, out_shape=[keep((2 * NG * CAP, W)), keep((2 * NG,...  3.5 us
    pallas_call x1, Pallas kernels, product_first(): pl.pallas_call(kernel, out_shape=[keep((2 * NG * CAP, W)), keep((4, 8, W)...  2.99 us
  transfers between devices with their start and end apart: 7, of which 3 were waited for; matrix products, arithmetic and copies ran while one was open for 6% of the time, Pallas kernels for 33%

profile of v4, /device:TPU:1, one launch (start us, length us, event | category | flops | bytes accessed | tf_op | source)
XLA Modules:
  0.0 82.6 jit_solution(3310160848711187480)
XLA Ops:
  0.6 0.0 copy-start
  0.6 0.7 copy-done
  1.4 0.0 copy-start.1
  1.4 1.1 %pack.1 = bf16[64,72,128]{2,1,0:T(8,128)(2,1)} custom-call(bf16[1,128,128]{2,1,0:T(8,128)(2,1)S(1)} %copy-done), custom_call_target="tpu_custom_call" | custom-call | tf_op jit(solution)/shard_map/pack/pallas_call | solution.py:65
  2.5 12.0 %all-to-all-start = ((bf16[64,72,128]{2,1,0:T(8,128)(2,1)}), bf16[64,72,128]{2,1,0:T(8,128)(2,1)S(1)}, u32[]{:S(2)}, u32[]{:S(2)}) async-start(bf16[64,72,128]{2,1,0:T(8,128)(2,1)} %pack.1), calls=%async_computation | async-start | bytes 2359296 | tf_op jit(solution)/shard_map/all_to_all | solution.py:412
  14.5 1.0 %fusion.11 = (f32[2,2048]{1,0:T(2,128)S(1)}, f32[2,2048]{1,0:T(2,128)S(1)}, f32[2,2048]{1,0:T(2,128)S(1)}, f32[2,2048]{1,0:T(2,128)S(1)}) fusion(f32[768,2048]{1,0:T(8,128)} %xn_ref, f32[768,2048]{1,0:T(8,128)} %sn_ref), kind=kLoop, calls=%fused_computation.28 | loop fusion | bytes 131072 | tf_op jit(solution)/shard_map/slice | solution.py:416
  15.5 2.9 %collective-permute-start = (f32[4,2048]{1,0:T(4,128)S(1)}, f32[4,2048]{1,0:T(4,128)S(1)}, u32[]{:S(2)}, u32[]{:S(2)}) collective-permute-start(f32[4,2048]{1,0:T(4,128)S(1)} %pad_maximum_fusion), channel_id=1, source_target_pairs={{0,8},{8,16},{16,24},{24,32},{32,40},{40,48},{48,56},{56,64},{64,7... | collective-permute-start | bytes 98312 | tf_op jit(solution)/shard_map/ppermute | solution.py:417
  18.4 1.3 %collective-permute-start.1 = (f32[4,2048]{1,0:T(4,128)S(1)}, f32[4,2048]{1,0:T(4,128)S(1)}, u32[]{:S(2)}, u32[]{:S(2)}) collective-permute-start(f32[4,2048]{1,0:T(4,128)S(1)} %pad_maximum_fusion.1), channel_id=1, source_target_pairs={{8,0},{16,8},{24,16},{32,24},{40,32},{48,40},{56,48},{64,56},{72,6... | collective-permute-start | bytes 98312 | tf_op jit(solution)/shard_map/ppermute | solution.py:418
  19.7 0.0 copy-done.1
  19.7 0.1 copy.12
  19.8 0.3 fusion.4
  20.2 0.1 broadcast_add_fusion
  20.3 0.3 copy.13
  20.7 0.6 fusion.3
  21.3 0.1 add_convert_fusion.has_ref
  21.4 0.0 copy-start.2
  21.4 0.2 collective-permute-done.hup
  21.6 2.4 %collective-permute-done.1.hdn = f32[4,2048]{1,0:T(4,128)S(1)} collective-permute-done((f32[4,2048]{1,0:T(4,128)S(1)}, f32[4,2048]{1,0:T(4,128)S(1)}, u32[]{:S(2)}, u32[]{:S(2)}) %collective-permute-start.1) | collective-permute-done | bytes 32800 | tf_op jit(solution)/shard_map/ppermute | solution.py:418
  24.1 1.9 %cols.1 = (f32[16,896]{1,0:T(8,128)S(1)}, f32[16,896]{1,0:T(8,128)S(1)}) custom-call(f32[768,2048]{1,0:T(8,128)} %xn_ref, f32[768,2048]{1,0:T(8,128)} %sn_ref, f32[768,2048]{1,0:T(8,128)} %xn_ref, f32[768,2048]{1,0:T(8,128)} %sn_ref, f32[4,2048]{1,0:T(4,128)S(1)} %collective-permute-done.hup, f32[4,2048]{1,0:T(4,128)S(1)} %collective-permute-done.1.hdn), custom_call_target="tpu_custom_call" | custom-call | tf_op jit(solution)/shard_map/cols/pallas_call | solution.py:122
  25.9 10.6 %collective-permute-start.2 = (f32[16,896]{1,0:T(8,128)S(1)}, f32[16,896]{1,0:T(8,128)S(1)}, u32[]{:S(2)}, u32[]{:S(2)}) collective-permute-start(f32[16,896]{1,0:T(8,128)S(1)} %get-tuple-element.31), channel_id=1, source_target_pairs={{0,1},{1,2},{2,3},{3,4},{4,5},{5,6},{6,7},{8,9},{9,10},{10,11},{11... | collective-permute-start | bytes 172040 | tf_op jit(solution)/shard_map/ppermute | solution.py:423
  36.5 1.9 %collective-permute-start.3 = (f32[16,896]{1,0:T(8,128)S(1)}, f32[16,896]{1,0:T(8,128)S(1)}, u32[]{:S(2)}, u32[]{:S(2)}) collective-permute-start(f32[16,896]{1,0:T(8,128)S(1)} %get-tuple-element.32), channel_id=1, source_target_pairs={{1,0},{2,1},{3,2},{4,3},{5,4},{6,5},{7,6},{9,8},{10,9},{11,10},{12... | collective-permute-start | bytes 172040 | tf_op jit(solution)/shard_map/ppermute | solution.py:424
  38.5 0.0 copy-done.2
  38.5 2.3 %fusion.cnt = f32[1568,128]{1,0:T(8,128)S(1)} fusion(s32[2048]{0:T(1024)S(1)} %select_select_fusion.run_ref), kind=kOutput, calls=%fused_computation.1 | convolution fusion | flops 825294848 | bytes 811008 | tf_op jit(solution)/shard_map/dot_general | solution.py:437
  40.8 0.0 collective-permute-done.2.hcl
  40.8 1.2 %collective-permute-done.3.hcr = f32[16,896]{1,0:T(8,128)S(1)} collective-permute-done((f32[16,896]{1,0:T(8,128)S(1)}, f32[16,896]{1,0:T(8,128)S(1)}, u32[]{:S(2)}, u32[]{:S(2)}) %collective-permute-start.3) | collective-permute-done | bytes 57376 | tf_op jit(solution)/shard_map/ppermute | solution.py:424
  42.0 9.5 %rim.1 = (f32[2,1536,128]{2,1,0:T(8,128)}, f32[3,8,2048]{2,1,0:T(8,128)}, f32[2048,128]{1,0:T(8,128)}, f32[4096,128]{1,0:T(8,128)S(1)}) custom-call(s32[4]{0:T(128)S(1)} %add_convert_fusion.has_ref, s32[2048]{0:T(1024)S(1)} %select_select_fusion.run_ref, s32[2048]{0:T(1024)S(1)} %multiply_add_fusion.slot_ref, f32[768,2048]{1,0:T(8,128)} %xn_ref, ...), custom_call_target="tpu_custom_call" | custom-call | tf_op jit(solution)/shard_map/rim/pallas_call | solution.py:245
  51.5 0.0 all-to-all-done.b
  51.5 0.1 collective-permute-start.4
  51.6 3.0 %product_a.1 = (f32[4096,128]{1,0:T(8,128)S(1)}, f32[4,8,128]{2,1,0:T(8,128)S(1)}) custom-call(f32[4096,128]{1,0:T(8,128)S(1)} %get-tuple-element.34.s, bf16[64,72,128]{2,1,0:T(8,128)(2,1)S(1)} %all-to-all-done.b), custom_call_target="tpu_custom_call", output_to_operand_aliasing={{0}: (0, {})} | custom-call | tf_op jit(solution)/shard_map/product_a/pallas_call | solution.py:321
  54.6 0.0 collective-permute-done.4.b
  54.6 3.5 %product_b.1 = (f32[4096,128]{1,0:T(8,128)S(1)}, f32[128,4,128]{2,1,0:T(4,128)}) custom-call(f32[4096,128]{1,0:T(8,128)S(1)} %get-tuple-element.36.s, bf16[64,72,128]{2,1,0:T(8,128)(2,1)S(1)} %collective-permute-done.4.b, f32[4,8,128]{2,1,0:T(8,128)S(1)} %get-tuple-element.37.p), custom_call_target="tpu_custom_call", output_to_operand_aliasing={{0}: (0, {})} | custom-call | tf_op jit(solution)/shard_map/product_b/pallas_call | solution.py:330
  58.1 7.6 %all-to-all-start.1 = ((f32[128,4,128]{2,1,0:T(4,128)}), f32[128,4,128]{2,1,0:T(4,128)S(1)}, u32[]{:S(2)}, u32[]{:S(2)}) async-start(f32[128,4,128]{2,1,0:T(4,128)} %get-tuple-element.40), calls=%async_computation.1 | async-start | bytes 524288 | tf_op jit(solution)/shard_map/all_to_all | solution.py:444
  65.8 2.8 %order.1.q_ref = f32[2048,128]{1,0:T(8,128)S(1)} custom-call(s32[2048]{0:T(1024)S(1)} %multiply_add_fusion.slot_ref, f32[4096,128]{1,0:T(8,128)S(1)} %get-tuple-element.42.q_ref), custom_call_target="tpu_custom_call" | custom-call | tf_op jit(solution)/shard_map/order/pallas_call | solution.py:345
  68.6 10.5 %dense.1.field_ref = f32[768,2048]{1,0:T(8,128)} custom-call(f32[768,2048]{1,0:T(8,128)} %xn_ref, f32[768,2048]{1,0:T(8,128)} %sn_ref, f32[768,2048]{1,0:T(8,128)} %xn_ref, f32[768,2048]{1,0:T(8,128)} %sn_ref, f32[768,2048]{1,0:T(8,128)} %xn_ref, f32[768,2048]{1,0:T(8,128)} %sn_ref), custom_call_target="tpu_custom_call" | custom-call | tf_op jit(solution)/shard_map/dense/pallas_call | solution.py:98
  79.1 0.0 all-to-all-done.1.red_ref
  79.1 3.6 %final.1 = (f32[768,2048]{1,0:T(8,128)}, f32[2048,128]{1,0:T(8,128)}, f32[2048,128]{1,0:T(8,128)}) custom-call(f32[128,4,128]{2,1,0:T(4,128)S(1)} %all-to-all-done.1.red_ref, f32[2048,128]{1,0:T(8,128)} %get-tuple-element.41.r_hbm, f32[2048,128]{1,0:T(8,128)S(1)} %order.1.q_ref, ...), custom_call_target="tpu_custom_call", output_to_operand_aliasing={{0}: (5, {})} | custom-call | tf_op jit(solution)/shard_map/final/pallas_call | solution.py:400
  (7 shorter events, 0.1 us)
Async XLA Ops:
  0.6 0.8 copy-start
  1.4 18.3 %copy-start.1 = (s32[2048,1]{0,1:T(1,128)S(1)}, s32[2048,1]{0,1:T(1,128)}, u32[]{:S(2)}) copy-start(s32[2048,1]{0,1:T(1,128)} %param.8) | copy-start | bytes 24580
  2.5 49.0 %all-to-all-start = ((bf16[64,72,128]{2,1,0:T(8,128)(2,1)}), bf16[64,72,128]{2,1,0:T(8,128)(2,1)S(1)}, u32[]{:S(2)}, u32[]{:S(2)}) async-start(bf16[64,72,128]{2,1,0:T(8,128)(2,1)} %pack.1), calls=%async_computation | async-start | bytes 2359296 | tf_op jit(solution)/shard_map/all_to_all | solution.py:412
  15.5 6.2 %collective-permute-start = (f32[4,2048]{1,0:T(4,128)S(1)}, f32[4,2048]{1,0:T(4,128)S(1)}, u32[]{:S(2)}, u32[]{:S(2)}) collective-permute-start(f32[4,2048]{1,0:T(4,128)S(1)} %pad_maximum_fusion), channel_id=1, source_target_pairs={{0,8},{8,16},{16,24},{24,32},{32,40},{40,48},{48,56},{56,64},{64,7... | collective-permute-start | bytes 98312 | tf_op jit(solution)/shard_map/ppermute | solution.py:417
  18.4 5.7 %collective-permute-start.1 = (f32[4,2048]{1,0:T(4,128)S(1)}, f32[4,2048]{1,0:T(4,128)S(1)}, u32[]{:S(2)}, u32[]{:S(2)}) collective-permute-start(f32[4,2048]{1,0:T(4,128)S(1)} %pad_maximum_fusion.1), channel_id=1, source_target_pairs={{8,0},{16,8},{24,16},{32,24},{40,32},{48,40},{56,48},{64,56},{72,6... | collective-permute-start | bytes 98312 | tf_op jit(solution)/shard_map/ppermute | solution.py:418
  21.4 17.1 %copy-start.2 = (s32[2048]{0:T(1024)S(1)}, s32[2048]{0:T(1024)}, u32[]{:S(2)}) copy-start(s32[2048]{0:T(1024)} %param.7) | copy-start | bytes 24580
  25.9 14.8 %collective-permute-start.2 = (f32[16,896]{1,0:T(8,128)S(1)}, f32[16,896]{1,0:T(8,128)S(1)}, u32[]{:S(2)}, u32[]{:S(2)}) collective-permute-start(f32[16,896]{1,0:T(8,128)S(1)} %get-tuple-element.31), channel_id=1, source_target_pairs={{0,1},{1,2},{2,3},{3,4},{4,5},{5,6},{6,7},{8,9},{9,10},{10,11},{11... | collective-permute-start | bytes 172040 | tf_op jit(solution)/shard_map/ppermute | solution.py:423
  36.5 5.5 %collective-permute-start.3 = (f32[16,896]{1,0:T(8,128)S(1)}, f32[16,896]{1,0:T(8,128)S(1)}, u32[]{:S(2)}, u32[]{:S(2)}) collective-permute-start(f32[16,896]{1,0:T(8,128)S(1)} %get-tuple-element.32), channel_id=1, source_target_pairs={{1,0},{2,1},{3,2},{4,3},{5,4},{6,5},{7,6},{9,8},{10,9},{11,10},{12... | collective-permute-start | bytes 172040 | tf_op jit(solution)/shard_map/ppermute | solution.py:424
  51.5 3.1 %collective-permute-start.4 = (bf16[64,72,128]{2,1,0:T(8,128)(2,1)S(1)}, bf16[64,72,128]{2,1,0:T(8,128)(2,1)S(1)}, u32[]{:S(2)}, u32[]{:S(2)}) collective-permute-start(bf16[64,72,128]{2,1,0:T(8,128)(2,1)S(1)} %all-to-all-done.b), channel_id=1, source_target_pairs={{0,1},{1,0},{2,3},{3,2},{4,5},{5,4},{6,7},{7,6},{8,9},{9,8},{10,11... | collective-permute-start | bytes 3538952 | tf_op jit(solution)/shard_map/ppermute | solution.py:440
  58.1 20.9 %all-to-all-start.1 = ((f32[128,4,128]{2,1,0:T(4,128)}), f32[128,4,128]{2,1,0:T(4,128)S(1)}, u32[]{:S(2)}, u32[]{:S(2)}) async-start(f32[128,4,128]{2,1,0:T(4,128)} %get-tuple-element.40), calls=%async_computation.1 | async-start | bytes 524288 | tf_op jit(solution)/shard_map/all_to_all | solution.py:444

commit v5 on v4

--- a/solution.py
+++ b/solution.py
@@ -23,7 +23,7 @@
 VM = pl.BlockSpec(memory_space=pltpu.VMEM)
 SM = pl.BlockSpec(memory_space=pltpu.SMEM)
 ANY = pl.BlockSpec(memory_space=pl.ANY)
-ND = 16
+ND = 12
 C1 = 0.6111111
 K1 = C1 + 2.75 * (1.0 - C1)
 K2 = 2.75 * C1
@@ -73,7 +73,17 @@
     return [jnp.where(lane == 0, prev[c - 1], prev[c]) + jnp.where(lane == W - 1, succ[(c + 1) % n], succ[c]) for c in range(n)]
 
 
-def dense_kernel(x_ref, s_ref, xp_ref, sp_ref, xn_ref, sn_ref, out_ref, g_ref, d_ref):
+def dense_kernel(slot_ref, q_ref, x_ref, s_ref, xp_ref, sp_ref, xn_ref, sn_ref, out_ref, tiles_ref, g_ref, d_ref):
+    share = T // (R // (8 * ND))
+    first = pl.program_id(0) * share
+
+    def body(b, carry):
+        for u in range(16):
+            t = first + b * 16 + u
+            tiles_ref[pl.ds(t, 1), :] = q_ref[pl.ds(slot_ref[t], 1), :]
+        return carry
+
+    lax.fori_loop(0, share // 16, body, 0)
     tiles = [slice(c * W, (c + 1) * W) for c in range(C // W)]
     n = 8 * ND
     for c, lanes in enumerate(tiles):
@@ -90,15 +100,15 @@
             out_ref[rows, lanes] = d_ref[c, rows] * (K1 * x_ref[rows, lanes] + K2 * beside)
 
 
-def dense(rhs, sigma):
+def dense(slot, q, rhs, sigma):
     n = 8 * ND
     main = pl.BlockSpec((n, C), lambda i: (i, 0))
     prev = pl.BlockSpec((8, C), lambda i: (jnp.maximum(ND * i - 1, 0), 0))
     succ = pl.BlockSpec((8, C), lambda i: (jnp.minimum(ND * i + ND, R // 8 - 1), 0))
     return pl.pallas_call(
-        dense_kernel, grid=(R // n,), out_shape=sds((R, C)), in_specs=[main, main, prev, prev, succ, succ], out_specs=main,
+        dense_kernel, grid=(R // n,), out_shape=[sds((R, C)), keep((T, W))], in_specs=[SM, VM, main, main, prev, prev, succ, succ], out_specs=[main, VM],
         scratch_shapes=[pltpu.VMEM((C // W, n + 16, W), F32), pltpu.VMEM((C // W, n, W), F32)],
-        compiler_params=PARAMS, name="dense")(rhs, sigma, rhs, sigma, rhs, sigma)
+        compiler_params=PARAMS, name="dense")(slot, q, rhs, sigma, rhs, sigma, rhs, sigma)
 
 
 def cols_kernel(xl, sl, xr, sr, hup, hdn, right_out, left_out, buf):
@@ -123,8 +133,19 @@
                           scratch_shapes=[pltpu.VMEM((FC, W), F32)], compiler_params=PARAMS, name="cols")(rhs, sigma, rhs, sigma, hup, hdn)
 
 
-def rim_kernel(has_ref, run_ref, slot_ref, xl, sl, xr, sr, xt, st, xb, sb, hup, hdn, hcl, hcr, cnt, strips_out, rows_out, tiles_out, slots_ref,
-               r_out, strips, rows_buf, tiles, sems, X, D, G, S, H, D2, G2, S2):
+def rim_kernel(has_ref, run_ref, slot_ref, rhs, sigma, hup, hdn, hcl, hcr, cnt, strips_out, rows_out, tiles_out, slots_ref,
+               r_out, strips, rows_buf, tiles, sems, ins, xl, sl, xr, sr, xt, st, xb, sb, X, D, G, S, H, D2, G2, S2):
+    wide, low, high = slice(C - 2 * W, C), slice(0, 16), slice(R - 16, R)
+    loads = [
+        pltpu.make_async_copy(src.at[where], dst, ins.at[k])
+        for k, (src, where, dst) in enumerate((
+            (rhs, (slice(None), slice(0, 2 * W)), xl), (sigma, (slice(None), slice(0, 2 * W)), sl),
+            (rhs, (slice(None), wide), xr), (sigma, (slice(None), wide), sr),
+            (rhs, (low, slice(None)), xt), (sigma, (low, slice(None)), st), (rhs, (high, slice(None)), xb), (sigma, (high, slice(None)), sb)))
+    ]
+    for c in loads:
+        c.start()
+    slots_ref[...] = jnp.zeros_like(slots_ref)
     up, down, left, right = (has_ref[k] for k in range(4))
     lane = lax.broadcasted_iota(jnp.int32, (1, W), 1)
 
@@ -180,8 +201,14 @@
             strips[0, at] = v
             strips[1, at] = cnt[at] * res
 
+    loads[0].wait()
+    loads[1].wait()
     strip(xl, sl, 0, hcl, 1, W - 2, left, 0)
+    loads[2].wait()
+    loads[3].wait()
     strip(xr, sr, C - 2 * W, hcr, 0, 0, right, R)
+    for c in loads[4:]:
+        c.wait()
     copies = [pltpu.make_async_copy(strips, strips_out, sems.at[0]), pltpu.make_async_copy(rows_buf, rows_out, sems.at[1])]
     copies[0].start()
 
@@ -218,8 +245,6 @@
     edge(xb, sb, hdn, 24, 16, 24, down, 1, 7, 2 * R + 16)
     copies[1].start()
 
-    slots_ref[...] = jnp.zeros_like(slots_ref)
-
     def body(b, carry):
         for u in range(16):
             t = b * 16 + u
@@ -228,32 +253,30 @@
             slots_ref[pl.ds(slot_ref[t], 1), :] = row
         return carry
 
-    lax.fori_loop(0, T // 16, body, 0)
-    last = pltpu.make_async_copy(tiles, tiles_out, sems.at[2])
-    last.start()
+    for k in range(4):
+        lax.fori_loop(k * T // 64, (k + 1) * T // 64, body, 0)
+        part = pl.ds(k * T // 4, T // 4)
+        copies.append(pltpu.make_async_copy(tiles.at[part], tiles_out.at[part], sems.at[2 + k]))
+        copies[-1].start()
     for c in copies:
         c.wait()
-    last.wait()
 
 
 def rim(has, run, slot, rhs, sigma, hup, hdn, hcl, hcr, cnt):
-    left = pl.BlockSpec((R, 2 * W), lambda i: (0, 0))
-    right = pl.BlockSpec((R, 2 * W), lambda i: (0, C // (2 * W) - 1))
-    top = pl.BlockSpec((16, C), lambda i: (0, 0))
-    bottom = pl.BlockSpec((16, C), lambda i: (R // 16 - 1, 0))
     strips, rows, tiles = (2, 2 * R, W), (3, 8, C), (T, W)
     return pl.pallas_call(
-        rim_kernel, grid=(1,), out_shape=[pltpu.HBM(strips, F32), pltpu.HBM(rows, F32), pltpu.HBM(tiles, F32), keep((2 * NG * CAP, W))],
-        in_specs=[SM, SM, SM, left, left, right, right, top, top, bottom, bottom, VM, VM, VM, VM, VM],
+        rim_kernel, out_shape=[pltpu.HBM(strips, F32), pltpu.HBM(rows, F32), pltpu.HBM(tiles, F32), keep((2 * NG * CAP, W))],
+        in_specs=[SM, SM, SM, ANY, ANY, VM, VM, VM, VM, VM],
         out_specs=[ANY, ANY, ANY, VM],
-        scratch_shapes=[pltpu.VMEM((RIM, W), F32), pltpu.VMEM(strips, F32), pltpu.VMEM(rows, F32), pltpu.VMEM(tiles, F32), pltpu.SemaphoreType.DMA((3,))]
-        + [pltpu.VMEM((2, FR, W), F32)] * 4 + [pltpu.VMEM((2, FC, W), F32)] + [pltpu.VMEM((C // W, 32, W), F32)] * 3,
-        compiler_params=PARAMS, name="rim")(has, run, slot, rhs, sigma, rhs, sigma, rhs, sigma, rhs, sigma, hup, hdn, in_vmem(hcl), in_vmem(hcr), in_vmem(cnt))
+        scratch_shapes=[pltpu.VMEM((RIM, W), F32), pltpu.VMEM(strips, F32), pltpu.VMEM(rows, F32), pltpu.VMEM(tiles, F32), pltpu.SemaphoreType.DMA((6,)),
+                        pltpu.SemaphoreType.DMA((8,))]
+        + [pltpu.VMEM((R, 2 * W), F32)] * 4 + [pltpu.VMEM((16, C), F32)] * 4 + [pltpu.VMEM((2, FR, W), F32)] * 4 + [pltpu.VMEM((2, FC, W), F32)] + [pltpu.VMEM((C // W, 32, W), F32)] * 3,
+        compiler_params=PARAMS, name="rim")(has, run, slot, rhs, sigma, hup, hdn, in_vmem(hcl), in_vmem(hcr), in_vmem(cnt))
 
 
 def product_kernel(first, slots_ref, blk_ref, *refs):
     if first:
-        q_ref, sums_ref, v_ref = refs
+        q_ref, sums_ref, _ = refs
     else:
         prev_ref, q_ref, sums_ref = refs
     i = lax.broadcasted_iota(jnp.int32, (64, W), 0)
@@ -331,20 +354,6 @@
                           in_specs=[VM, VM, VM], out_specs=[VM, VM], compiler_params=PARAMS, name="product_b")(slots, in_vmem(blocks), prev)
 
 
-def order_kernel(slot_ref, q_ref, out_ref):
-    def body(b, carry):
-        for u in range(16):
-            t = b * 16 + u
-            out_ref[pl.ds(t, 1), :] = q_ref[pl.ds(slot_ref[t], 1), :]
-        return carry
-
-    lax.fori_loop(0, T // 16, body, 0)
-
-
-def order(slot, q):
-    return pl.pallas_call(order_kernel, out_shape=keep((T, W)), in_specs=[SM, VM], out_specs=VM, compiler_params=PARAMS, name="order")(slot, q)
-
-
 CH = 4
 TC = T // CH
 
@@ -405,7 +414,7 @@
         input_output_aliases={5: 0}, compiler_params=PARAMS, name="final")(in_vmem(red), in_hbm(r_tiles), q_tiles, in_hbm(strips), in_hbm(rows), field)
 
 
-def per_device(rhs, sigma, tile_list, tile_owner, schur_blocks):
+def step(rhs, sigma, tile_list, tile_owner, schur_blocks):
     core = lax.axis_index("c")
     big = (in_hbm(rhs), in_hbm(sigma))
     packed, *ready = lax.optimization_barrier((pack(schur_blocks), rhs, sigma))
@@ -419,7 +428,7 @@
 
     rightward = [(i, i + 1) for i in range(ncol - 1)]
     leftward = [(i + 1, i) for i in range(ncol - 1)]
-    to_right, to_left, tile_list = lax.optimization_barrier((*edge_cols(*big, hup, hdn), tile_list))
+    to_right, to_left, tile_list, tile_owner = lax.optimization_barrier((*edge_cols(*big, hup, hdn), tile_list, tile_owner))
     hcl = lax.ppermute(to_right, COLS, rightward)
     hcr = lax.ppermute(to_left, COLS, leftward)
     row_at = lax.axis_index(ROWS)
@@ -442,8 +451,7 @@
     q, sums = product_second(q, theirs, part)
     q, sums, late_rhs, late_sigma = lax.optimization_barrier((q, sums, rhs, sigma))
     red = lax.all_to_all(sums, ALL, 0, 0, tiled=True)
-    q_tiles = order(slot, q)
-    field = dense(in_hbm(late_rhs), in_hbm(late_sigma))
+    field, q_tiles = dense(slot, q, in_hbm(late_rhs), in_hbm(late_sigma))
     return tuple(final(red, r_tiles, q_tiles, strips, rows, field))
 
 
@@ -451,4 +459,4 @@
     grid = Mesh(mesh.devices.reshape(4, 4, 4, 2), ("y", "z", "x", "c"))
     in_specs = (P(ROWS, COLS), P(ROWS, COLS), P(ALL), P(ALL, None), P(ALL, None, None))
     out_specs = (P(ROWS, COLS), P(ALL, None), P(ALL, None))
-    return jax.shard_map(per_device, mesh=grid, in_specs=in_specs, out_specs=out_specs, check_vma=False)
+    return jax.shard_map(step, mesh=grid, in_specs=in_specs, out_specs=out_specs, check_vma=False)

time: 83.2 us -> 83 us (level)
  Pallas kernels: 35.8 us -> 34.8 us
    pallas_call x3 -> x2, Pallas kernels: 22.8 us -> 21.7 us  [the longest x1 12.2 us: dense(): pl.pallas_call(dense_kernel, grid=(R // n,), out_shape=[sds((R, C)), keep...]
  transfers between devices with their start and end apart: 7 -> 7, of which waited for: 3 -> 2; matrix products, arithmetic and copies ran while one was open for 6% -> 6% of each run, Pallas kernels for 33% -> 32%
where the time goes in v5:
time: 83 us; the launch traced here: 82.3 us
  starting transfers between devices  36.7 us (44%)
  Pallas kernels  34.8 us (42%)
  waiting for transfers between devices  4.27 us (5%)
  matrix products  2.28 us (3%)
  local copies, waits for them, and re-layouts  2.17 us (3%)
  other arithmetic  1.21 us (1%)
  between operations  0.86 us (1%)
    pallas_call x1, Pallas kernels, dense(): pl.pallas_call(dense_kernel, grid=(R // n,), out_shape=[sds((R, C)), keep...  12.2 us
    all_to_all x1, starting transfers between devices, step(): mine = lax.all_to_all(packed, CHIPS, 0, 0, tiled=True)  12 us
    ppermute x1, starting transfers between devices, step(): hcl = lax.ppermute(to_right, COLS, rightward)  10.6 us
    pallas_call x1, Pallas kernels, rim(): pl.pallas_call(rim_kernel, out_shape=[pltpu.HBM(strips, F32), pltpu.HBM(r...  9.53 us
    all_to_all x1, starting transfers between devices, step(): red = lax.all_to_all(sums, ALL, 0, 0, tiled=True)  7.95 us
    pallas_call x1, Pallas kernels, final(): pl.pallas_call(final_kernel, out_shape=[sds((R, C)), sds((T, W)), sds((T,...  3.56 us
    pallas_call x1, Pallas kernels, product_second(): pl.pallas_call(kernel, out_shape=[keep((2 * NG * CAP, W)), keep((2 * NG,...  3.5 us
    pallas_call x1, Pallas kernels, product_first(): pl.pallas_call(kernel, out_shape=[keep((2 * NG * CAP, W)), keep((4, 8, W)...  2.99 us
  transfers between devices with their start and end apart: 7, of which 2 were waited for; matrix products, arithmetic and copies ran while one was open for 6% of the time, Pallas kernels for 32%

profile of v5, /device:TPU:1, one launch (start us, length us, event | category | flops | bytes accessed | tf_op | source)
XLA Modules:
  0.0 82.3 jit_solution(17796308663949186212)
XLA Ops:
  0.6 0.0 copy-start
  0.6 0.7 copy-done
  1.4 1.1 %pack.1 = bf16[64,72,128]{2,1,0:T(8,128)(2,1)} custom-call(bf16[1,128,128]{2,1,0:T(8,128)(2,1)S(1)} %copy-done), custom_call_target="tpu_custom_call" | custom-call | tf_op jit(solution)/shard_map/pack/pallas_call | solution.py:65
  2.5 12.0 %all-to-all-start = ((bf16[64,72,128]{2,1,0:T(8,128)(2,1)}), bf16[64,72,128]{2,1,0:T(8,128)(2,1)S(1)}, u32[]{:S(2)}, u32[]{:S(2)}) async-start(bf16[64,72,128]{2,1,0:T(8,128)(2,1)} %pack.1), calls=%async_computation | async-start | bytes 2359296 | tf_op jit(solution)/shard_map/all_to_all | solution.py:421
  14.5 1.0 %fusion.11 = (f32[2,2048]{1,0:T(2,128)S(1)}, f32[2,2048]{1,0:T(2,128)S(1)}, f32[2,2048]{1,0:T(2,128)S(1)}, f32[2,2048]{1,0:T(2,128)S(1)}) fusion(f32[768,2048]{1,0:T(8,128)} %xn_ref, f32[768,2048]{1,0:T(8,128)} %sn_ref), kind=kLoop, calls=%fused_computation.28 | loop fusion | bytes 131072 | tf_op jit(solution)/shard_map/slice | solution.py:425
  15.5 2.9 %collective-permute-start = (f32[4,2048]{1,0:T(4,128)S(1)}, f32[4,2048]{1,0:T(4,128)S(1)}, u32[]{:S(2)}, u32[]{:S(2)}) collective-permute-start(f32[4,2048]{1,0:T(4,128)S(1)} %pad_maximum_fusion), channel_id=1, source_target_pairs={{0,8},{8,16},{16,24},{24,32},{32,40},{40,48},{48,56},{56,64},{64,7... | collective-permute-start | bytes 98312 | tf_op jit(solution)/shard_map/ppermute | solution.py:426
  18.4 1.3 %collective-permute-start.1 = (f32[4,2048]{1,0:T(4,128)S(1)}, f32[4,2048]{1,0:T(4,128)S(1)}, u32[]{:S(2)}, u32[]{:S(2)}) collective-permute-start(f32[4,2048]{1,0:T(4,128)S(1)} %pad_maximum_fusion.1), channel_id=1, source_target_pairs={{8,0},{16,8},{24,16},{32,24},{40,32},{48,40},{56,48},{64,56},{72,6... | collective-permute-start | bytes 98312 | tf_op jit(solution)/shard_map/ppermute | solution.py:427
  19.7 0.1 add_convert_fusion.has_ref
  19.8 0.0 copy-start.1
  19.8 1.8 %collective-permute-done.hup = f32[4,2048]{1,0:T(4,128)S(1)} collective-permute-done((f32[4,2048]{1,0:T(4,128)S(1)}, f32[4,2048]{1,0:T(4,128)S(1)}, u32[]{:S(2)}, u32[]{:S(2)}) %collective-permute-start) | collective-permute-done | bytes 32800 | tf_op jit(solution)/shard_map/ppermute | solution.py:426
  21.6 2.4 %collective-permute-done.1.hdn = f32[4,2048]{1,0:T(4,128)S(1)} collective-permute-done((f32[4,2048]{1,0:T(4,128)S(1)}, f32[4,2048]{1,0:T(4,128)S(1)}, u32[]{:S(2)}, u32[]{:S(2)}) %collective-permute-start.1) | collective-permute-done | bytes 32800 | tf_op jit(solution)/shard_map/ppermute | solution.py:427
  24.1 1.9 %cols.1 = (f32[16,896]{1,0:T(8,128)S(1)}, f32[16,896]{1,0:T(8,128)S(1)}) custom-call(f32[768,2048]{1,0:T(8,128)} %xn_ref, f32[768,2048]{1,0:T(8,128)} %sn_ref, f32[768,2048]{1,0:T(8,128)} %xn_ref, f32[768,2048]{1,0:T(8,128)} %sn_ref, f32[4,2048]{1,0:T(4,128)S(1)} %collective-permute-done.hup, f32[4,2048]{1,0:T(4,128)S(1)} %collective-permute-done.1.hdn), custom_call_target="tpu_custom_call" | custom-call | tf_op jit(solution)/shard_map/cols/pallas_call | solution.py:132
  25.9 0.0 copy-done.1
  25.9 0.1 copy.12
  26.1 0.0 copy-start.2
  26.1 10.6 %collective-permute-start.2 = (f32[16,896]{1,0:T(8,128)S(1)}, f32[16,896]{1,0:T(8,128)S(1)}, u32[]{:S(2)}, u32[]{:S(2)}) collective-permute-start(f32[16,896]{1,0:T(8,128)S(1)} %get-tuple-element.35), channel_id=1, source_target_pairs={{0,1},{1,2},{2,3},{3,4},{4,5},{5,6},{6,7},{8,9},{9,10},{10,11},{11... | collective-permute-start | bytes 172040 | tf_op jit(solution)/shard_map/ppermute | solution.py:432
  36.6 1.9 %collective-permute-start.3 = (f32[16,896]{1,0:T(8,128)S(1)}, f32[16,896]{1,0:T(8,128)S(1)}, u32[]{:S(2)}, u32[]{:S(2)}) collective-permute-start(f32[16,896]{1,0:T(8,128)S(1)} %get-tuple-element.36), channel_id=1, source_target_pairs={{1,0},{2,1},{3,2},{4,3},{5,4},{6,5},{7,6},{9,8},{10,9},{11,10},{12... | collective-permute-start | bytes 172040 | tf_op jit(solution)/shard_map/ppermute | solution.py:433
  38.6 0.3 fusion.4
  39.0 0.1 broadcast_add_fusion
  39.0 0.3 copy.13
  39.4 0.6 fusion.3
  40.0 0.0 copy-done.2
  40.1 2.3 %fusion.cnt = f32[1568,128]{1,0:T(8,128)S(1)} fusion(s32[2048]{0:T(1024)S(1)} %select_select_fusion.run_ref), kind=kOutput, calls=%fused_computation.1 | convolution fusion | flops 825294848 | bytes 811008 | tf_op jit(solution)/shard_map/dot_general | solution.py:446
  42.4 0.0 collective-permute-done.2.hcl
  42.4 0.0 collective-permute-done.3.hcr
  42.4 9.5 %rim.1 = (f32[2,1536,128]{2,1,0:T(8,128)}, f32[3,8,2048]{2,1,0:T(8,128)}, f32[2048,128]{1,0:T(8,128)}, f32[4096,128]{1,0:T(8,128)S(1)}) custom-call(s32[4]{0:T(128)S(1)} %add_convert_fusion.has_ref, s32[2048]{0:T(1024)S(1)} %select_select_fusion.run_ref, s32[2048]{0:T(1024)S(1)} %multiply_add_fusion.slot_ref, f32[768,2048]{1,0:T(8,128)} %xn_ref, ...), custom_call_target="tpu_custom_call" | custom-call | tf_op jit(solution)/shard_map/rim/pallas_call | solution.py:267
  51.9 0.0 all-to-all-done.b
  51.9 0.1 collective-permute-start.4
  52.0 3.0 %product_a.1 = (f32[4096,128]{1,0:T(8,128)S(1)}, f32[4,8,128]{2,1,0:T(8,128)S(1)}) custom-call(f32[4096,128]{1,0:T(8,128)S(1)} %get-tuple-element.38.s, bf16[64,72,128]{2,1,0:T(8,128)(2,1)S(1)} %all-to-all-done.b), custom_call_target="tpu_custom_call", output_to_operand_aliasing={{0}: (0, {})} | custom-call | tf_op jit(solution)/shard_map/product_a/pallas_call | solution.py:344
  55.0 0.0 collective-permute-done.4.b
  55.0 3.5 %product_b.1 = (f32[4096,128]{1,0:T(8,128)S(1)}, f32[128,4,128]{2,1,0:T(4,128)}) custom-call(f32[4096,128]{1,0:T(8,128)S(1)} %get-tuple-element.40.s, bf16[64,72,128]{2,1,0:T(8,128)(2,1)S(1)} %collective-permute-done.4.b, f32[4,8,128]{2,1,0:T(8,128)S(1)} %get-tuple-element.41.p), custom_call_target="tpu_custom_call", output_to_operand_aliasing={{0}: (0, {})} | custom-call | tf_op jit(solution)/shard_map/product_b/pallas_call | solution.py:353
  58.5 7.9 %all-to-all-start.1 = ((f32[128,4,128]{2,1,0:T(4,128)}), f32[128,4,128]{2,1,0:T(4,128)S(1)}, u32[]{:S(2)}, u32[]{:S(2)}) async-start(f32[128,4,128]{2,1,0:T(4,128)} %get-tuple-element.44), calls=%async_computation.1 | async-start | bytes 524288 | tf_op jit(solution)/shard_map/all_to_all | solution.py:453
  66.5 12.2 %dense.1 = (f32[768,2048]{1,0:T(8,128)}, f32[2048,128]{1,0:T(8,128)S(1)}) custom-call(s32[2048]{0:T(1024)S(1)} %multiply_add_fusion.slot_ref, f32[4096,128]{1,0:T(8,128)S(1)} %get-tuple-element.46.q_ref, f32[768,2048]{1,0:T(8,128)} %xn_ref, f32[768,2048]{1,0:T(8,128)} %sn_ref, f32[768,2048]{1,0:T(8,128)} %xn_ref, f32[768,2048]{1,0:T(8,128)} %sn_ref, ...), custom_call_target="tpu_custom_call" | custom-call | tf_op jit(solution)/shard_map/dense/pallas_call | solution.py:108
  78.7 0.0 all-to-all-done.1.red_ref
  78.7 3.6 %final.1 = (f32[768,2048]{1,0:T(8,128)}, f32[2048,128]{1,0:T(8,128)}, f32[2048,128]{1,0:T(8,128)}) custom-call(f32[128,4,128]{2,1,0:T(4,128)S(1)} %all-to-all-done.1.red_ref, f32[2048,128]{1,0:T(8,128)} %get-tuple-element.45.r_hbm, f32[2048,128]{1,0:T(8,128)S(1)} %get-tuple-element.49.q_ref, ...), custom_call_target="tpu_custom_call", output_to_operand_aliasing={{0}: (5, {})} | custom-call | tf_op jit(solution)/shard_map/final/pallas_call | solution.py:409
  (7 shorter events, 0.1 us)
Async XLA Ops:
  0.6 0.8 copy-start
  2.5 49.4 %all-to-all-start = ((bf16[64,72,128]{2,1,0:T(8,128)(2,1)}), bf16[64,72,128]{2,1,0:T(8,128)(2,1)S(1)}, u32[]{:S(2)}, u32[]{:S(2)}) async-start(bf16[64,72,128]{2,1,0:T(8,128)(2,1)} %pack.1), calls=%async_computation | async-start | bytes 2359296 | tf_op jit(solution)/shard_map/all_to_all | solution.py:421
  15.5 6.2 %collective-permute-start = (f32[4,2048]{1,0:T(4,128)S(1)}, f32[4,2048]{1,0:T(4,128)S(1)}, u32[]{:S(2)}, u32[]{:S(2)}) collective-permute-start(f32[4,2048]{1,0:T(4,128)S(1)} %pad_maximum_fusion), channel_id=1, source_target_pairs={{0,8},{8,16},{16,24},{24,32},{32,40},{40,48},{48,56},{56,64},{64,7... | collective-permute-start | bytes 98312 | tf_op jit(solution)/shard_map/ppermute | solution.py:426
  18.4 5.7 %collective-permute-start.1 = (f32[4,2048]{1,0:T(4,128)S(1)}, f32[4,2048]{1,0:T(4,128)S(1)}, u32[]{:S(2)}, u32[]{:S(2)}) collective-permute-start(f32[4,2048]{1,0:T(4,128)S(1)} %pad_maximum_fusion.1), channel_id=1, source_target_pairs={{8,0},{16,8},{24,16},{32,24},{40,32},{48,40},{56,48},{64,56},{72,6... | collective-permute-start | bytes 98312 | tf_op jit(solution)/shard_map/ppermute | solution.py:427
  19.8 6.1 %copy-start.1 = (s32[2048,1]{0,1:T(1,128)S(1)}, s32[2048,1]{0,1:T(1,128)}, u32[]{:S(2)}) copy-start(s32[2048,1]{0,1:T(1,128)} %param.8) | copy-start | bytes 24580
  26.1 14.0 %copy-start.2 = (s32[2048]{0:T(1024)S(1)}, s32[2048]{0:T(1024)}, u32[]{:S(2)}) copy-start(s32[2048]{0:T(1024)} %param.7) | copy-start | bytes 24580
  26.1 16.3 %collective-permute-start.2 = (f32[16,896]{1,0:T(8,128)S(1)}, f32[16,896]{1,0:T(8,128)S(1)}, u32[]{:S(2)}, u32[]{:S(2)}) collective-permute-start(f32[16,896]{1,0:T(8,128)S(1)} %get-tuple-element.35), channel_id=1, source_target_pairs={{0,1},{1,2},{2,3},{3,4},{4,5},{5,6},{6,7},{8,9},{9,10},{10,11},{11... | collective-permute-start | bytes 172040 | tf_op jit(solution)/shard_map/ppermute | solution.py:432
  36.6 5.7 %collective-permute-start.3 = (f32[16,896]{1,0:T(8,128)S(1)}, f32[16,896]{1,0:T(8,128)S(1)}, u32[]{:S(2)}, u32[]{:S(2)}) collective-permute-start(f32[16,896]{1,0:T(8,128)S(1)} %get-tuple-element.36), channel_id=1, source_target_pairs={{1,0},{2,1},{3,2},{4,3},{5,4},{6,5},{7,6},{9,8},{10,9},{11,10},{12... | collective-permute-start | bytes 172040 | tf_op jit(solution)/shard_map/ppermute | solution.py:433
  51.9 3.1 %collective-permute-start.4 = (bf16[64,72,128]{2,1,0:T(8,128)(2,1)S(1)}, bf16[64,72,128]{2,1,0:T(8,128)(2,1)S(1)}, u32[]{:S(2)}, u32[]{:S(2)}) collective-permute-start(bf16[64,72,128]{2,1,0:T(8,128)(2,1)S(1)} %all-to-all-done.b), channel_id=1, source_target_pairs={{0,1},{1,0},{2,3},{3,2},{4,5},{5,4},{6,7},{7,6},{8,9},{9,8},{10,11... | collective-permute-start | bytes 3538952 | tf_op jit(solution)/shard_map/ppermute | solution.py:449
  58.5 20.2 %all-to-all-start.1 = ((f32[128,4,128]{2,1,0:T(4,128)}), f32[128,4,128]{2,1,0:T(4,128)S(1)}, u32[]{:S(2)}, u32[]{:S(2)}) async-start(f32[128,4,128]{2,1,0:T(4,128)} %get-tuple-element.44), calls=%async_computation.1 | async-start | bytes 524288 | tf_op jit(solution)/shard_map/all_to_all | solution.py:453

commit v6 on v5

--- a/solution.py
+++ b/solution.py
@@ -23,7 +23,6 @@
 VM = pl.BlockSpec(memory_space=pltpu.VMEM)
 SM = pl.BlockSpec(memory_space=pltpu.SMEM)
 ANY = pl.BlockSpec(memory_space=pl.ANY)
-ND = 12
 C1 = 0.6111111
 K1 = C1 + 2.75 * (1.0 - C1)
 K2 = 2.75 * C1
@@ -73,42 +72,67 @@
     return [jnp.where(lane == 0, prev[c - 1], prev[c]) + jnp.where(lane == W - 1, succ[(c + 1) % n], succ[c]) for c in range(n)]
 
 
-def dense_kernel(slot_ref, q_ref, x_ref, s_ref, xp_ref, sp_ref, xn_ref, sn_ref, out_ref, tiles_ref, g_ref, d_ref):
-    share = T // (R // (8 * ND))
-    first = pl.program_id(0) * share
+NC = 8
+NR = R // NC
+
+
+def dense_kernel(slot_ref, q_ref, x_hbm, s_hbm, out_hbm, tiles_ref, x, s, g, ins, outs):
+    nt = C // W
+    tiles = [slice(c * W, (c + 1) * W) for c in range(nt)]
+    chunks = [slice(k * NR, (k + 1) * NR) for k in range(NC)]
+    loads = [[pltpu.make_async_copy(src.at[p], dst.at[p], ins.at[n, k]) for n, (src, dst) in enumerate(((x_hbm, x), (s_hbm, s)))]
+             for k, p in enumerate(chunks)]
+    for pair in loads:
+        for c in pair:
+            c.start()
 
     def body(b, carry):
         for u in range(16):
-            t = first + b * 16 + u
+            t = b * 16 + u
             tiles_ref[pl.ds(t, 1), :] = q_ref[pl.ds(slot_ref[t], 1), :]
         return carry
 
-    lax.fori_loop(0, share // 16, body, 0)
-    tiles = [slice(c * W, (c + 1) * W) for c in range(C // W)]
-    n = 8 * ND
-    for c, lanes in enumerate(tiles):
-        dinv = 1.0 / (4.0 + s_ref[:, lanes])
-        d_ref[c] = dinv
-        g_ref[c, 8:8 + n] = dinv * x_ref[:, lanes]
-        g_ref[c, 7:8] = xp_ref[7:8, lanes] / (4.0 + sp_ref[7:8, lanes])
-        g_ref[c, 8 + n:9 + n] = xn_ref[0:1, lanes] / (4.0 + sn_ref[0:1, lanes])
-    for k in range(ND):
-        rows = slice(8 * k, 8 * k + 8)
-        side = sides([g_ref[c, 8 * k + 8:8 * k + 16] for c in range(C // W)])
+    lax.fori_loop(0, T // 16, body, 0)
+    for c in range(nt):
+        g[c, 0:8] = jnp.zeros((8, W), F32)
+        g[c, R + 8:R + 16] = jnp.zeros((8, W), F32)
+
+    def first(k):
+        for c in loads[k]:
+            c.wait()
+        p = chunks[k]
         for c, lanes in enumerate(tiles):
-            beside = (g_ref[c, 8 * k + 7:8 * k + 15] + g_ref[c, 8 * k + 9:8 * k + 17]) + side[c]
-            out_ref[rows, lanes] = d_ref[c, rows] * (K1 * x_ref[rows, lanes] + K2 * beside)
+            dinv = 1.0 / (4.0 + s[p, lanes])
+            s[p, lanes] = dinv
+            g[c, 8 + k * NR:8 + (k + 1) * NR] = dinv * x[p, lanes]
+
+    def second(k):
+        for j in range(k * NR // 8, (k + 1) * NR // 8):
+            rows = slice(8 * j, 8 * j + 8)
+            side = sides([g[c, 8 * j + 8:8 * j + 16] for c in range(nt)])
+            for c, lanes in enumerate(tiles):
+                beside = (g[c, 8 * j + 7:8 * j + 15] + g[c, 8 * j + 9:8 * j + 17]) + side[c]
+                x[rows, lanes] = s[rows, lanes] * (K1 * x[rows, lanes] + K2 * beside)
+        c = pltpu.make_async_copy(x.at[chunks[k]], out_hbm.at[chunks[k]], outs.at[k])
+        c.start()
+        return c
+
+    sent = []
+    for k in range(NC):
+        first(k)
+        if k:
+            sent.append(second(k - 1))
+    sent.append(second(NC - 1))
+    for c in sent:
+        c.wait()
 
 
 def dense(slot, q, rhs, sigma):
-    n = 8 * ND
-    main = pl.BlockSpec((n, C), lambda i: (i, 0))
-    prev = pl.BlockSpec((8, C), lambda i: (jnp.maximum(ND * i - 1, 0), 0))
-    succ = pl.BlockSpec((8, C), lambda i: (jnp.minimum(ND * i + ND, R // 8 - 1), 0))
     return pl.pallas_call(
-        dense_kernel, grid=(R // n,), out_shape=[sds((R, C)), keep((T, W))], in_specs=[SM, VM, main, main, prev, prev, succ, succ], out_specs=[main, VM],
-        scratch_shapes=[pltpu.VMEM((C // W, n + 16, W), F32), pltpu.VMEM((C // W, n, W), F32)],
-        compiler_params=PARAMS, name="dense")(slot, q, rhs, sigma, rhs, sigma, rhs, sigma)
+        dense_kernel, out_shape=[sds((R, C)), keep((T, W))], in_specs=[SM, VM, ANY, ANY], out_specs=[ANY, VM],
+        scratch_shapes=[pltpu.VMEM((R, C), F32), pltpu.VMEM((R, C), F32), pltpu.VMEM((C // W, R + 16, W), F32),
+                        pltpu.SemaphoreType.DMA((2, NC)), pltpu.SemaphoreType.DMA((NC,))],
+        compiler_params=pltpu.CompilerParams(vmem_limit_bytes=32 << 20), name="dense")(slot, q, rhs, sigma)
 
 
 def cols_kernel(xl, sl, xr, sr, hup, hdn, right_out, left_out, buf):

time: 83 us -> 81.8 us (0.986)
  Pallas kernels: 34.8 us -> 30.9 us
  waiting for transfers between devices: 4.27 us -> 6.9 us
    pallas_call x1, Pallas kernels: 12.2 us -> 8.37 us  [dense(): pl.pallas_call(dense_kernel, out_shape=[sds((R, C)), keep((T, W))], in_sp...]
    all_to_all x1, waiting for transfers between devices: 0.01 us -> 2.63 us  [step(): red = lax.all_to_all(sums, ALL, 0, 0, tiled=True)]
  transfers between devices with their start and end apart: 7 -> 7, of which waited for: 2 -> 3; matrix products, arithmetic and copies ran while one was open for 6% -> 6% of each run, Pallas kernels for 32% -> 28%
where the time goes in v6:
time: 81.8 us; the launch traced here: 81.2 us
  starting transfers between devices  36.7 us (45%)
  Pallas kernels  30.9 us (38%)
  waiting for transfers between devices  6.9 us (8%)
  matrix products  2.28 us (3%)
  local copies, waits for them, and re-layouts  2.17 us (3%)
  other arithmetic  1.21 us (1%)
  between operations  1.02 us (1%)
    all_to_all x1, starting transfers between devices, step(): mine = lax.all_to_all(packed, CHIPS, 0, 0, tiled=True)  12 us
    ppermute x1, starting transfers between devices, step(): hcl = lax.ppermute(to_right, COLS, rightward)  10.6 us
    pallas_call x1, Pallas kernels, rim(): pl.pallas_call(rim_kernel, out_shape=[pltpu.HBM(strips, F32), pltpu.HBM(r...  9.53 us
    pallas_call x1, Pallas kernels, dense(): pl.pallas_call(dense_kernel, out_shape=[sds((R, C)), keep((T, W))], in_sp...  8.37 us
    all_to_all x1, starting transfers between devices, step(): red = lax.all_to_all(sums, ALL, 0, 0, tiled=True)  7.95 us
    pallas_call x1, Pallas kernels, final(): pl.pallas_call(final_kernel, out_shape=[sds((R, C)), sds((T, W)), sds((T,...  3.55 us
    pallas_call x1, Pallas kernels, product_second(): pl.pallas_call(kernel, out_shape=[keep((2 * NG * CAP, W)), keep((2 * NG,...  3.5 us
    pallas_call x1, Pallas kernels, product_first(): pl.pallas_call(kernel, out_shape=[keep((2 * NG * CAP, W)), keep((4, 8, W)...  2.99 us
  transfers between devices with their start and end apart: 7, of which 3 were waited for; matrix products, arithmetic and copies ran while one was open for 6% of the time, Pallas kernels for 28%

profile of v6, /device:TPU:1, one launch (start us, length us, event | category | flops | bytes accessed | tf_op | source)
XLA Modules:
  0.0 81.2 jit_solution(11655883223436710290)
XLA Ops:
  0.6 0.0 copy-start
  0.6 0.7 copy-done
  1.4 1.1 %pack.1 = bf16[64,72,128]{2,1,0:T(8,128)(2,1)} custom-call(bf16[1,128,128]{2,1,0:T(8,128)(2,1)S(1)} %copy-done), custom_call_target="tpu_custom_call" | custom-call | tf_op jit(solution)/shard_map/pack/pallas_call | solution.py:64
  2.5 12.0 %all-to-all-start = ((bf16[64,72,128]{2,1,0:T(8,128)(2,1)}), bf16[64,72,128]{2,1,0:T(8,128)(2,1)S(1)}, u32[]{:S(2)}, u32[]{:S(2)}) async-start(bf16[64,72,128]{2,1,0:T(8,128)(2,1)} %pack.1), calls=%async_computation | async-start | bytes 2359296 | tf_op jit(solution)/shard_map/all_to_all | solution.py:445
  14.5 1.0 %fusion.11 = (f32[2,2048]{1,0:T(2,128)S(1)}, f32[2,2048]{1,0:T(2,128)S(1)}, f32[2,2048]{1,0:T(2,128)S(1)}, f32[2,2048]{1,0:T(2,128)S(1)}) fusion(f32[768,2048]{1,0:T(8,128)} %x_hbm, f32[768,2048]{1,0:T(8,128)} %s_hbm), kind=kLoop, calls=%fused_computation.28 | loop fusion | bytes 131072 | tf_op jit(solution)/shard_map/slice | solution.py:449
  15.5 2.9 %collective-permute-start = (f32[4,2048]{1,0:T(4,128)S(1)}, f32[4,2048]{1,0:T(4,128)S(1)}, u32[]{:S(2)}, u32[]{:S(2)}) collective-permute-start(f32[4,2048]{1,0:T(4,128)S(1)} %pad_maximum_fusion), channel_id=1, source_target_pairs={{0,8},{8,16},{16,24},{24,32},{32,40},{40,48},{48,56},{56,64},{64,7... | collective-permute-start | bytes 98312 | tf_op jit(solution)/shard_map/ppermute | solution.py:450
  18.4 1.3 %collective-permute-start.1 = (f32[4,2048]{1,0:T(4,128)S(1)}, f32[4,2048]{1,0:T(4,128)S(1)}, u32[]{:S(2)}, u32[]{:S(2)}) collective-permute-start(f32[4,2048]{1,0:T(4,128)S(1)} %pad_maximum_fusion.1), channel_id=1, source_target_pairs={{8,0},{16,8},{24,16},{32,24},{40,32},{48,40},{56,48},{64,56},{72,6... | collective-permute-start | bytes 98312 | tf_op jit(solution)/shard_map/ppermute | solution.py:451
  19.7 0.1 add_convert_fusion.has_ref
  19.8 0.0 copy-start.1
  19.8 1.8 %collective-permute-done.hup = f32[4,2048]{1,0:T(4,128)S(1)} collective-permute-done((f32[4,2048]{1,0:T(4,128)S(1)}, f32[4,2048]{1,0:T(4,128)S(1)}, u32[]{:S(2)}, u32[]{:S(2)}) %collective-permute-start) | collective-permute-done | bytes 32800 | tf_op jit(solution)/shard_map/ppermute | solution.py:450
  21.6 2.4 %collective-permute-done.1.hdn = f32[4,2048]{1,0:T(4,128)S(1)} collective-permute-done((f32[4,2048]{1,0:T(4,128)S(1)}, f32[4,2048]{1,0:T(4,128)S(1)}, u32[]{:S(2)}, u32[]{:S(2)}) %collective-permute-start.1) | collective-permute-done | bytes 32800 | tf_op jit(solution)/shard_map/ppermute | solution.py:451
  24.1 1.9 %cols.1 = (f32[16,896]{1,0:T(8,128)S(1)}, f32[16,896]{1,0:T(8,128)S(1)}) custom-call(f32[768,2048]{1,0:T(8,128)} %x_hbm, f32[768,2048]{1,0:T(8,128)} %s_hbm, f32[768,2048]{1,0:T(8,128)} %x_hbm, f32[768,2048]{1,0:T(8,128)} %s_hbm, f32[4,2048]{1,0:T(4,128)S(1)} %collective-permute-done.hup, f32[4,2048]{1,0:T(4,128)S(1)} %collective-permute-done.1.hdn), custom_call_target="tpu_custom_call" | custom-call | tf_op jit(solution)/shard_map/cols/pallas_call | solution.py:156
  25.9 0.0 copy-done.1
  25.9 0.1 copy.12
  26.1 0.0 copy-start.2
  26.1 10.6 %collective-permute-start.2 = (f32[16,896]{1,0:T(8,128)S(1)}, f32[16,896]{1,0:T(8,128)S(1)}, u32[]{:S(2)}, u32[]{:S(2)}) collective-permute-start(f32[16,896]{1,0:T(8,128)S(1)} %get-tuple-element.35), channel_id=1, source_target_pairs={{0,1},{1,2},{2,3},{3,4},{4,5},{5,6},{6,7},{8,9},{9,10},{10,11},{11... | collective-permute-start | bytes 172040 | tf_op jit(solution)/shard_map/ppermute | solution.py:456
  36.6 1.9 %collective-permute-start.3 = (f32[16,896]{1,0:T(8,128)S(1)}, f32[16,896]{1,0:T(8,128)S(1)}, u32[]{:S(2)}, u32[]{:S(2)}) collective-permute-start(f32[16,896]{1,0:T(8,128)S(1)} %get-tuple-element.36), channel_id=1, source_target_pairs={{1,0},{2,1},{3,2},{4,3},{5,4},{6,5},{7,6},{9,8},{10,9},{11,10},{12... | collective-permute-start | bytes 172040 | tf_op jit(solution)/shard_map/ppermute | solution.py:457
  38.6 0.3 fusion.4
  39.0 0.1 broadcast_add_fusion
  39.0 0.3 copy.13
  39.4 0.6 fusion.3
  40.0 0.0 copy-done.2
  40.1 2.3 %fusion.cnt = f32[1568,128]{1,0:T(8,128)S(1)} fusion(s32[2048]{0:T(1024)S(1)} %select_select_fusion.run_ref), kind=kOutput, calls=%fused_computation.1 | convolution fusion | flops 825294848 | bytes 811008 | tf_op jit(solution)/shard_map/dot_general | solution.py:470
  42.4 0.0 collective-permute-done.2.hcl
  42.4 0.0 collective-permute-done.3.hcr
  42.4 9.5 %rim.1 = (f32[2,1536,128]{2,1,0:T(8,128)}, f32[3,8,2048]{2,1,0:T(8,128)}, f32[2048,128]{1,0:T(8,128)}, f32[4096,128]{1,0:T(8,128)S(1)}) custom-call(s32[4]{0:T(128)S(1)} %add_convert_fusion.has_ref, s32[2048]{0:T(1024)S(1)} %select_select_fusion.run_ref, s32[2048]{0:T(1024)S(1)} %multiply_add_fusion.slot_ref, f32[768,2048]{1,0:T(8,128)} %x_hbm, ...), custom_call_target="tpu_custom_call" | custom-call | tf_op jit(solution)/shard_map/rim/pallas_call | solution.py:291
  51.9 0.0 all-to-all-done.b
  51.9 0.1 collective-permute-start.4
  52.0 3.0 %product_a.1 = (f32[4096,128]{1,0:T(8,128)S(1)}, f32[4,8,128]{2,1,0:T(8,128)S(1)}) custom-call(f32[4096,128]{1,0:T(8,128)S(1)} %get-tuple-element.38.s, bf16[64,72,128]{2,1,0:T(8,128)(2,1)S(1)} %all-to-all-done.b), custom_call_target="tpu_custom_call", output_to_operand_aliasing={{0}: (0, {})} | custom-call | tf_op jit(solution)/shard_map/product_a/pallas_call | solution.py:368
  55.0 0.0 collective-permute-done.4.b
  55.0 3.5 %product_b.1 = (f32[4096,128]{1,0:T(8,128)S(1)}, f32[128,4,128]{2,1,0:T(4,128)}) custom-call(f32[4096,128]{1,0:T(8,128)S(1)} %get-tuple-element.40.s, bf16[64,72,128]{2,1,0:T(8,128)(2,1)S(1)} %collective-permute-done.4.b, f32[4,8,128]{2,1,0:T(8,128)S(1)} %get-tuple-element.41.p), custom_call_target="tpu_custom_call", output_to_operand_aliasing={{0}: (0, {})} | custom-call | tf_op jit(solution)/shard_map/product_b/pallas_call | solution.py:377
  58.5 7.9 %all-to-all-start.1 = ((f32[128,4,128]{2,1,0:T(4,128)}), f32[128,4,128]{2,1,0:T(4,128)S(1)}, u32[]{:S(2)}, u32[]{:S(2)}) async-start(f32[128,4,128]{2,1,0:T(4,128)} %get-tuple-element.44), calls=%async_computation.1 | async-start | bytes 524288 | tf_op jit(solution)/shard_map/all_to_all | solution.py:477
  66.5 8.4 %dense.1 = (f32[768,2048]{1,0:T(8,128)}, f32[2048,128]{1,0:T(8,128)S(1)}) custom-call(s32[2048]{0:T(1024)S(1)} %multiply_add_fusion.slot_ref, f32[4096,128]{1,0:T(8,128)S(1)} %get-tuple-element.46.q_ref, f32[768,2048]{1,0:T(8,128)} %x_hbm, f32[768,2048]{1,0:T(8,128)} %s_hbm), custom_call_target="tpu_custom_call" | custom-call | tf_op jit(solution)/shard_map/dense/pallas_call | solution.py:131
  74.9 2.6 %all-to-all-done.1.red_ref = f32[128,4,128]{2,1,0:T(4,128)S(1)} async-done(((f32[128,4,128]{2,1,0:T(4,128)}), f32[128,4,128]{2,1,0:T(4,128)S(1)}, u32[]{:S(2)}, u32[]{:S(2)}) %all-to-all-start.1) | async-done | bytes 262176 | tf_op jit(solution)/shard_map/all_to_all | solution.py:477
  77.5 3.6 %final.1 = (f32[768,2048]{1,0:T(8,128)}, f32[2048,128]{1,0:T(8,128)}, f32[2048,128]{1,0:T(8,128)}) custom-call(f32[128,4,128]{2,1,0:T(4,128)S(1)} %all-to-all-done.1.red_ref, f32[2048,128]{1,0:T(8,128)} %get-tuple-element.45.r_hbm, f32[2048,128]{1,0:T(8,128)S(1)} %get-tuple-element.49.q_ref, ...), custom_call_target="tpu_custom_call", output_to_operand_aliasing={{0}: (5, {})} | custom-call | tf_op jit(solution)/shard_map/final/pallas_call | solution.py:433
  (7 shorter events, 0.1 us)
Async XLA Ops:
  0.6 0.8 copy-start
  2.5 49.4 %all-to-all-start = ((bf16[64,72,128]{2,1,0:T(8,128)(2,1)}), bf16[64,72,128]{2,1,0:T(8,128)(2,1)S(1)}, u32[]{:S(2)}, u32[]{:S(2)}) async-start(bf16[64,72,128]{2,1,0:T(8,128)(2,1)} %pack.1), calls=%async_computation | async-start | bytes 2359296 | tf_op jit(solution)/shard_map/all_to_all | solution.py:445
  15.5 6.2 %collective-permute-start = (f32[4,2048]{1,0:T(4,128)S(1)}, f32[4,2048]{1,0:T(4,128)S(1)}, u32[]{:S(2)}, u32[]{:S(2)}) collective-permute-start(f32[4,2048]{1,0:T(4,128)S(1)} %pad_maximum_fusion), channel_id=1, source_target_pairs={{0,8},{8,16},{16,24},{24,32},{32,40},{40,48},{48,56},{56,64},{64,7... | collective-permute-start | bytes 98312 | tf_op jit(solution)/shard_map/ppermute | solution.py:450
  18.4 5.7 %collective-permute-start.1 = (f32[4,2048]{1,0:T(4,128)S(1)}, f32[4,2048]{1,0:T(4,128)S(1)}, u32[]{:S(2)}, u32[]{:S(2)}) collective-permute-start(f32[4,2048]{1,0:T(4,128)S(1)} %pad_maximum_fusion.1), channel_id=1, source_target_pairs={{8,0},{16,8},{24,16},{32,24},{40,32},{48,40},{56,48},{64,56},{72,6... | collective-permute-start | bytes 98312 | tf_op jit(solution)/shard_map/ppermute | solution.py:451
  19.8 6.1 %copy-start.1 = (s32[2048,1]{0,1:T(1,128)S(1)}, s32[2048,1]{0,1:T(1,128)}, u32[]{:S(2)}) copy-start(s32[2048,1]{0,1:T(1,128)} %param.8) | copy-start | bytes 24580
  26.1 14.0 %copy-start.2 = (s32[2048]{0:T(1024)S(1)}, s32[2048]{0:T(1024)}, u32[]{:S(2)}) copy-start(s32[2048]{0:T(1024)} %param.7) | copy-start | bytes 24580
  26.1 16.3 %collective-permute-start.2 = (f32[16,896]{1,0:T(8,128)S(1)}, f32[16,896]{1,0:T(8,128)S(1)}, u32[]{:S(2)}, u32[]{:S(2)}) collective-permute-start(f32[16,896]{1,0:T(8,128)S(1)} %get-tuple-element.35), channel_id=1, source_target_pairs={{0,1},{1,2},{2,3},{3,4},{4,5},{5,6},{6,7},{8,9},{9,10},{10,11},{11... | collective-permute-start | bytes 172040 | tf_op jit(solution)/shard_map/ppermute | solution.py:456
  36.6 5.7 %collective-permute-start.3 = (f32[16,896]{1,0:T(8,128)S(1)}, f32[16,896]{1,0:T(8,128)S(1)}, u32[]{:S(2)}, u32[]{:S(2)}) collective-permute-start(f32[16,896]{1,0:T(8,128)S(1)} %get-tuple-element.36), channel_id=1, source_target_pairs={{1,0},{2,1},{3,2},{4,3},{5,4},{6,5},{7,6},{9,8},{10,9},{11,10},{12... | collective-permute-start | bytes 172040 | tf_op jit(solution)/shard_map/ppermute | solution.py:457
  51.9 3.1 %collective-permute-start.4 = (bf16[64,72,128]{2,1,0:T(8,128)(2,1)S(1)}, bf16[64,72,128]{2,1,0:T(8,128)(2,1)S(1)}, u32[]{:S(2)}, u32[]{:S(2)}) collective-permute-start(bf16[64,72,128]{2,1,0:T(8,128)(2,1)S(1)} %all-to-all-done.b), channel_id=1, source_target_pairs={{0,1},{1,0},{2,3},{3,2},{4,5},{5,4},{6,7},{7,6},{8,9},{9,8},{10,11... | collective-permute-start | bytes 3538952 | tf_op jit(solution)/shard_map/ppermute | solution.py:473
  58.5 19.0 %all-to-all-start.1 = ((f32[128,4,128]{2,1,0:T(4,128)}), f32[128,4,128]{2,1,0:T(4,128)S(1)}, u32[]{:S(2)}, u32[]{:S(2)}) async-start(f32[128,4,128]{2,1,0:T(4,128)} %get-tuple-element.44), calls=%async_computation.1 | async-start | bytes 524288 | tf_op jit(solution)/shard_map/all_to_all | solution.py:477

commit v7 on v6

--- a/solution.py
+++ b/solution.py
@@ -45,23 +45,34 @@
     return pltpu.with_memory_space_constraint(x, pltpu.VMEM)
 
 
-def pack_kernel(s_ref, out_ref):
+def head_kernel(s_ref, rhs, sigma, out_ref, tail_ref, head_ref, rows, sems):
+    ends = (slice(R - 8, R), slice(0, 8))
+    loads = [pltpu.make_async_copy(src.at[p], rows.at[2 * k + n], sems.at[2 * k + n]) for k, p in enumerate(ends) for n, src in enumerate((rhs, sigma))]
+    for c in loads:
+        c.start()
     s = s_ref[0].astype(F32)
     top, bot = s[:64], s[64:]
     i = lax.broadcasted_iota(jnp.int32, (64, W), 0)
     j = lax.broadcasted_iota(jnp.int32, (64, W), 1)
     d = j - i
     body = jnp.where((d >= 0) & (d < 64), top, bot)
-    cross = jnp.where(d == 64, top, 0.0)
-    half = jnp.sum(cross, axis=0, keepdims=True)
+    half = jnp.sum(jnp.where(d == 64, top, 0.0), axis=0, keepdims=True)
     row = half + pltpu.roll(half, 64, axis=1)
     full = jnp.concatenate([body, jnp.broadcast_to(row, (8, W))], axis=0).astype(BF16)
     for k in range(NG):
         out_ref[k] = full
-
-
-def pack(blocks):
-    return pl.pallas_call(pack_kernel, out_shape=sds((NG, PR, W), BF16), in_specs=[VM], out_specs=VM, compiler_params=PARAMS, name="pack")(blocks)
+    for c in loads:
+        c.wait()
+    tail_ref[0:2] = rows[0, 6:8]
+    tail_ref[2:4] = rows[1, 6:8]
+    head_ref[0:2] = rows[2, 0:2]
+    head_ref[2:4] = rows[3, 0:2]
+
+
+def start(blocks, rhs, sigma):
+    return pl.pallas_call(
+        head_kernel, out_shape=[keep((NG, PR, W), BF16), keep((4, C)), keep((4, C))], in_specs=[VM, ANY, ANY], out_specs=[VM, VM, VM],
+        scratch_shapes=[pltpu.VMEM((4, 8, C), F32), pltpu.SemaphoreType.DMA((4,))], compiler_params=PARAMS, name="head")(in_hbm(blocks), rhs, sigma)
 
 
 def sides(tiles):
@@ -157,18 +168,8 @@
                           scratch_shapes=[pltpu.VMEM((FC, W), F32)], compiler_params=PARAMS, name="cols")(rhs, sigma, rhs, sigma, hup, hdn)
 
 
-def rim_kernel(has_ref, run_ref, slot_ref, rhs, sigma, hup, hdn, hcl, hcr, cnt, strips_out, rows_out, tiles_out, slots_ref,
-               r_out, strips, rows_buf, tiles, sems, ins, xl, sl, xr, sr, xt, st, xb, sb, X, D, G, S, H, D2, G2, S2):
-    wide, low, high = slice(C - 2 * W, C), slice(0, 16), slice(R - 16, R)
-    loads = [
-        pltpu.make_async_copy(src.at[where], dst, ins.at[k])
-        for k, (src, where, dst) in enumerate((
-            (rhs, (slice(None), slice(0, 2 * W)), xl), (sigma, (slice(None), slice(0, 2 * W)), sl),
-            (rhs, (slice(None), wide), xr), (sigma, (slice(None), wide), sr),
-            (rhs, (low, slice(None)), xt), (sigma, (low, slice(None)), st), (rhs, (high, slice(None)), xb), (sigma, (high, slice(None)), sb)))
-    ]
-    for c in loads:
-        c.start()
+def rim_kernel(has_ref, run_ref, slot_ref, xl, sl, xr, sr, xt, st, xb, sb, hup, hdn, hcl, hcr, cnt, strips_out, rows_out, tiles_out, slots_ref,
+               r_out, strips, rows_buf, tiles, sems, X, D, G, S, H, D2, G2, S2):
     slots_ref[...] = jnp.zeros_like(slots_ref)
     up, down, left, right = (has_ref[k] for k in range(4))
     lane = lax.broadcasted_iota(jnp.int32, (1, W), 1)
@@ -225,14 +226,8 @@
             strips[0, at] = v
             strips[1, at] = cnt[at] * res
 
-    loads[0].wait()
-    loads[1].wait()
     strip(xl, sl, 0, hcl, 1, W - 2, left, 0)
-    loads[2].wait()
-    loads[3].wait()
     strip(xr, sr, C - 2 * W, hcr, 0, 0, right, R)
-    for c in loads[4:]:
-        c.wait()
     copies = [pltpu.make_async_copy(strips, strips_out, sems.at[0]), pltpu.make_async_copy(rows_buf, rows_out, sems.at[1])]
     copies[0].start()
 
@@ -286,16 +281,30 @@
         c.wait()
 
 
-def rim(has, run, slot, rhs, sigma, hup, hdn, hcl, hcr, cnt):
+def near_kernel(rhs, sigma, *refs):
+    outs, sems = refs[:8], refs[8]
+    places = ((slice(None), slice(0, 2 * W)), (slice(None), slice(C - 2 * W, C)), (slice(0, 16), slice(None)), (slice(R - 16, R), slice(None)))
+    copies = [pltpu.make_async_copy(src.at[p], outs[2 * k + n], sems.at[2 * k + n]) for k, p in enumerate(places) for n, src in enumerate((rhs, sigma))]
+    for c in copies:
+        c.start()
+    for c in copies:
+        c.wait()
+
+
+def near(rhs, sigma):
+    return pl.pallas_call(near_kernel, out_shape=[keep((R, 2 * W))] * 4 + [keep((16, C))] * 4, in_specs=[ANY, ANY], out_specs=[VM] * 8,
+                          scratch_shapes=[pltpu.SemaphoreType.DMA((8,))], compiler_params=PARAMS, name="near")(rhs, sigma)
+
+
+def rim(has, run, slot, parts, hup, hdn, hcl, hcr, cnt):
     strips, rows, tiles = (2, 2 * R, W), (3, 8, C), (T, W)
     return pl.pallas_call(
         rim_kernel, out_shape=[pltpu.HBM(strips, F32), pltpu.HBM(rows, F32), pltpu.HBM(tiles, F32), keep((2 * NG * CAP, W))],
-        in_specs=[SM, SM, SM, ANY, ANY, VM, VM, VM, VM, VM],
+        in_specs=[SM, SM, SM] + [VM] * 13,
         out_specs=[ANY, ANY, ANY, VM],
-        scratch_shapes=[pltpu.VMEM((RIM, W), F32), pltpu.VMEM(strips, F32), pltpu.VMEM(rows, F32), pltpu.VMEM(tiles, F32), pltpu.SemaphoreType.DMA((6,)),
-                        pltpu.SemaphoreType.DMA((8,))]
-        + [pltpu.VMEM((R, 2 * W), F32)] * 4 + [pltpu.VMEM((16, C), F32)] * 4 + [pltpu.VMEM((2, FR, W), F32)] * 4 + [pltpu.VMEM((2, FC, W), F32)] + [pltpu.VMEM((C // W, 32, W), F32)] * 3,
-        compiler_params=PARAMS, name="rim")(has, run, slot, rhs, sigma, hup, hdn, in_vmem(hcl), in_vmem(hcr), in_vmem(cnt))
+        scratch_shapes=[pltpu.VMEM((RIM, W), F32), pltpu.VMEM(strips, F32), pltpu.VMEM(rows, F32), pltpu.VMEM(tiles, F32), pltpu.SemaphoreType.DMA((6,))]
+        + [pltpu.VMEM((2, FR, W), F32)] * 4 + [pltpu.VMEM((2, FC, W), F32)] + [pltpu.VMEM((C // W, 32, W), F32)] * 3,
+        compiler_params=PARAMS, name="rim")(has, run, slot, *parts, hup, hdn, in_vmem(hcl), in_vmem(hcr), in_vmem(cnt))
 
 
 def product_kernel(first, slots_ref, blk_ref, *refs):
@@ -324,8 +333,7 @@
         u = jnp.concatenate([b * mask_top, b * mask_bot], axis=0)
         cross = blk_ref[g, 64:72, :].astype(F32)
         swapped = pltpu.roll(half.astype(F32), 64, axis=1)
-        q = jnp.dot(half, u, preferred_element_type=F32)
-        q = q + lax.dot_general(half, u, (((1,), (1,)), ((), ())), preferred_element_type=F32)
+        q = jnp.dot(half, u + u.T, preferred_element_type=F32)
         q = q + (swapped.reshape(CAP // 8, 8, W) * cross[None]).reshape(CAP, W)
         q = q.astype(BF16).astype(F32)
         q_ref[rows, :] = q
@@ -441,12 +449,11 @@
 def step(rhs, sigma, tile_list, tile_owner, schur_blocks):
     core = lax.axis_index("c")
     big = (in_hbm(rhs), in_hbm(sigma))
-    packed, *ready = lax.optimization_barrier((pack(schur_blocks), rhs, sigma))
+    packed, tail, head = start(schur_blocks, *big)
     mine = lax.all_to_all(packed, CHIPS, 0, 0, tiled=True)
     nrow, ncol = 16, 8
     up = [(i, i + 1) for i in range(nrow - 1)]
     down = [(i + 1, i) for i in range(nrow - 1)]
-    tail, head = jnp.concatenate([ready[0][-2:], ready[1][-2:]]), jnp.concatenate([ready[0][:2], ready[1][:2]])
     hup = lax.ppermute(tail, ROWS, up)
     hdn = lax.ppermute(head, ROWS, down)
 
@@ -468,7 +475,9 @@
     slot = (((owner & 1) ^ core) * NG + (owner >> 1)) * CAP + rank
     hits = (jnp.arange(RIM, dtype=jnp.int32)[:, None] == run[None, :]).astype(BF16)
     cnt = jnp.dot(hits, jnp.ones((T, W), BF16), preferred_element_type=F32)
-    strips, rows, r_tiles, slots = rim(has, run, slot, *big, hup, hdn, hcl, hcr, cnt)
+    cnt, slot, *here = lax.optimization_barrier((cnt, slot, rhs, sigma))
+    parts = near(*(in_hbm(v) for v in here))
+    strips, rows, r_tiles, slots = rim(has, run, slot, parts, hup, hdn, hcl, hcr, cnt)
     mine, slots = lax.optimization_barrier((mine, slots))
     theirs = lax.ppermute(mine, "c", [(0, 1), (1, 0)])
     q, part = product_first(slots, mine)

time: 81.8 us -> 82.4 us (level)
  local copies, waits for them, and re-layouts: 2.17 us -> 0.46 us
  waiting for transfers between devices: 6.9 us -> 8.13 us
  Pallas kernels: 30.9 us -> 31.9 us
    pallas_call x1 -> x2, Pallas kernels: 1.12 us -> 4.81 us  [the longest x1 2.74 us: start(): pl.pallas_call(head_kernel, out_shape=[keep((NG, PR, W), BF16), keep((4,...]
    ppermute x1, waiting for transfers between devices: 2.43 us -> 4.97 us  [step(): hdn = lax.ppermute(head, ROWS, down)]
    ppermute x1, waiting for transfers between devices: 1.83 us -> 0.01 us  [step(): hup = lax.ppermute(tail, ROWS, up)]
    pallas_call x1, Pallas kernels: 9.53 us -> 8.15 us  [rim(): pl.pallas_call(rim_kernel, out_shape=[pltpu.HBM(strips, F32), pltpu.HBM(r...]
    slice x1 -> x0, local copies, waits for them, and re-layouts: 0.96 us -> none  [step(): ready[0][:2]]
  transfers between devices with their start and end apart: 7 -> 7, of which waited for: 3 -> 3; matrix products, arithmetic and copies ran while one was open for 6% -> 5% of each run, Pallas kernels for 28% -> 28%
where the time goes in v7:
time: 82.4 us; the launch traced here: 81.8 us
  starting transfers between devices  36.9 us (45%)
  Pallas kernels  31.9 us (39%)
  waiting for transfers between devices  8.13 us (10%)
  matrix products  2.28 us (3%)
  other arithmetic  1.18 us (1%)
  between operations  1 us (1%)
    all_to_all x1, starting transfers between devices, step(): mine = lax.all_to_all(packed, CHIPS, 0, 0, tiled=True)  12 us
    ppermute x1, starting transfers between devices, step(): hcl = lax.ppermute(to_right, COLS, rightward)  10.7 us
    pallas_call x1, Pallas kernels, dense(): pl.pallas_call(dense_kernel, out_shape=[sds((R, C)), keep((T, W))], in_sp...  8.37 us
    pallas_call x1, Pallas kernels, rim(): pl.pallas_call(rim_kernel, out_shape=[pltpu.HBM(strips, F32), pltpu.HBM(r...  8.15 us
    all_to_all x1, starting transfers between devices, step(): red = lax.all_to_all(sums, ALL, 0, 0, tiled=True)  7.99 us
    ppermute x1, waiting for transfers between devices, step(): hdn = lax.ppermute(head, ROWS, down)  4.97 us
    pallas_call x1, Pallas kernels, final(): pl.pallas_call(final_kernel, out_shape=[sds((R, C)), sds((T, W)), sds((T,...  3.55 us
    ppermute x1, starting transfers between devices, step(): hup = lax.ppermute(tail, ROWS, up)  2.92 us
  transfers between devices with their start and end apart: 7, of which 3 were waited for; matrix products, arithmetic and copies ran while one was open for 5% of the time, Pallas kernels for 28%

profile of v7, /device:TPU:1, one launch (start us, length us, event | category | flops | bytes accessed | tf_op | source)
XLA Modules:
  0.0 81.8 jit_solution(13154656915813053529)
XLA Ops:
  0.6 2.7 %head.1 = (bf16[64,72,128]{2,1,0:T(8,128)(2,1)}, f32[4,2048]{1,0:T(4,128)S(1)}, f32[4,2048]{1,0:T(4,128)S(1)}) custom-call(bf16[1,128,128]{2,1,0:T(8,128)(2,1)} %s_ref.1, f32[768,2048]{1,0:T(8,128)} %x_hbm, f32[768,2048]{1,0:T(8,128)} %s_hbm), custom_call_target="tpu_custom_call" | custom-call | tf_op jit(solution)/shard_map/head/pallas_call | solution.py:73
  3.4 12.0 %all-to-all-start = ((bf16[64,72,128]{2,1,0:T(8,128)(2,1)}), bf16[64,72,128]{2,1,0:T(8,128)(2,1)S(1)}, u32[]{:S(2)}, u32[]{:S(2)}) async-start(bf16[64,72,128]{2,1,0:T(8,128)(2,1)} %get-tuple-element.40), calls=%async_computation | async-start | bytes 2359296 | tf_op jit(solution)/shard_map/all_to_all | solution.py:453
  15.4 2.9 %collective-permute-start = (f32[4,2048]{1,0:T(4,128)S(1)}, f32[4,2048]{1,0:T(4,128)S(1)}, u32[]{:S(2)}, u32[]{:S(2)}) collective-permute-start(f32[4,2048]{1,0:T(4,128)S(1)} %get-tuple-element.41), channel_id=1, source_target_pairs={{0,8},{8,16},{16,24},{24,32},{32,40},{40,48},{48,56},{56,64},{64,7... | collective-permute-start | bytes 98312 | tf_op jit(solution)/shard_map/ppermute | solution.py:457
  18.3 1.3 %collective-permute-start.1 = (f32[4,2048]{1,0:T(4,128)S(1)}, f32[4,2048]{1,0:T(4,128)S(1)}, u32[]{:S(2)}, u32[]{:S(2)}) collective-permute-start(f32[4,2048]{1,0:T(4,128)S(1)} %get-tuple-element.42), channel_id=1, source_target_pairs={{8,0},{16,8},{24,16},{32,24},{40,32},{48,40},{56,48},{64,56},{72,6... | collective-permute-start | bytes 98312 | tf_op jit(solution)/shard_map/ppermute | solution.py:458
  19.6 0.1 add_convert_fusion.has_ref
  19.7 0.0 copy-start
  19.7 0.0 collective-permute-done.hup
  19.7 5.0 %collective-permute-done.1.hdn = f32[4,2048]{1,0:T(4,128)S(1)} collective-permute-done((f32[4,2048]{1,0:T(4,128)S(1)}, f32[4,2048]{1,0:T(4,128)S(1)}, u32[]{:S(2)}, u32[]{:S(2)}) %collective-permute-start.1) | collective-permute-done | bytes 32800 | tf_op jit(solution)/shard_map/ppermute | solution.py:458
  24.6 1.9 %cols.1 = (f32[16,896]{1,0:T(8,128)S(1)}, f32[16,896]{1,0:T(8,128)S(1)}) custom-call(f32[768,2048]{1,0:T(8,128)} %x_hbm, f32[768,2048]{1,0:T(8,128)} %s_hbm, f32[768,2048]{1,0:T(8,128)} %x_hbm, f32[768,2048]{1,0:T(8,128)} %s_hbm, f32[4,2048]{1,0:T(4,128)S(1)} %collective-permute-done.hup, f32[4,2048]{1,0:T(4,128)S(1)} %collective-permute-done.1.hdn), custom_call_target="tpu_custom_call" | custom-call | tf_op jit(solution)/shard_map/cols/pallas_call | solution.py:167
  26.5 0.0 copy-done
  26.5 0.1 copy.12
  26.6 0.0 copy-start.1
  26.6 10.7 %collective-permute-start.2 = (f32[16,896]{1,0:T(8,128)S(1)}, f32[16,896]{1,0:T(8,128)S(1)}, u32[]{:S(2)}, u32[]{:S(2)}) collective-permute-start(f32[16,896]{1,0:T(8,128)S(1)} %get-tuple-element.58), channel_id=1, source_target_pairs={{0,1},{1,2},{2,3},{3,4},{4,5},{5,6},{6,7},{8,9},{9,10},{10,11},{11... | collective-permute-start | bytes 172040 | tf_op jit(solution)/shard_map/ppermute | solution.py:463
  37.4 1.9 %collective-permute-start.3 = (f32[16,896]{1,0:T(8,128)S(1)}, f32[16,896]{1,0:T(8,128)S(1)}, u32[]{:S(2)}, u32[]{:S(2)}) collective-permute-start(f32[16,896]{1,0:T(8,128)S(1)} %get-tuple-element.59), channel_id=1, source_target_pairs={{1,0},{2,1},{3,2},{4,3},{5,4},{6,5},{7,6},{9,8},{10,9},{11,10},{12... | collective-permute-start | bytes 172040 | tf_op jit(solution)/shard_map/ppermute | solution.py:464
  39.3 0.3 fusion.4
  39.7 0.1 broadcast_add_fusion
  39.8 0.3 copy.13
  40.1 0.6 fusion.3
  40.8 0.0 copy-done.1
  40.8 2.3 %fusion.cnt = f32[1568,128]{1,0:T(8,128)S(1)} fusion(s32[2048]{0:T(1024)S(1)} %select_select_fusion.run_ref), kind=kOutput, calls=%fused_computation.1 | convolution fusion | flops 825294848 | bytes 811008 | tf_op jit(solution)/shard_map/dot_general | solution.py:477
  43.1 2.1 %near.1 = (f32[768,256]{1,0:T(8,128)S(1)}, f32[768,256]{1,0:T(8,128)S(1)}, f32[768,256]{1,0:T(8,128)S(1)}, f32[768,256]{1,0:T(8,128)S(1)}, f32[16,2048]{1,0:T(8,...) custom-call(f32[768,2048]{1,0:T(8,128)} %x_hbm, f32[768,2048]{1,0:T(8,128)} %s_hbm), custom_call_target="tpu_custom_call" | custom-call | tf_op jit(solution)/shard_map/near/pallas_call | solution.py:295
  45.2 0.0 collective-permute-done.2.hcl
  45.2 0.0 collective-permute-done.3.hcr
  45.2 8.2 %rim.1 = (f32[2,1536,128]{2,1,0:T(8,128)}, f32[3,8,2048]{2,1,0:T(8,128)}, f32[2048,128]{1,0:T(8,128)}, f32[4096,128]{1,0:T(8,128)S(1)}) custom-call(s32[4]{0:T(128)S(1)} %add_convert_fusion.has_ref, s32[2048]{0:T(1024)S(1)} %select_select_fusion.run_ref, s32[2048]{0:T(1024)S(1)} %multiply_add_fusion.slot_ref, f32[768,256]{1,0:T(8,128)S(1)} %get-tuple-element.50.xl, ...), custom_call_target="tpu_custom_call" | custom-call | tf_op jit(solution)/shard_map/rim/pallas_call | solution.py:301
  53.4 0.0 all-to-all-done.b
  53.4 0.1 collective-permute-start.4
  53.5 2.3 %product_a.1 = (f32[4096,128]{1,0:T(8,128)S(1)}, f32[4,8,128]{2,1,0:T(8,128)S(1)}) custom-call(f32[4096,128]{1,0:T(8,128)S(1)} %get-tuple-element.62.s, bf16[64,72,128]{2,1,0:T(8,128)(2,1)S(1)} %all-to-all-done.b), custom_call_target="tpu_custom_call", output_to_operand_aliasing={{0}: (0, {})} | custom-call | tf_op jit(solution)/shard_map/product_a/pallas_call | solution.py:376
  55.8 0.5 collective-permute-done.4.b
  56.3 2.8 %product_b.1 = (f32[4096,128]{1,0:T(8,128)S(1)}, f32[128,4,128]{2,1,0:T(4,128)}) custom-call(f32[4096,128]{1,0:T(8,128)S(1)} %get-tuple-element.64.s, bf16[64,72,128]{2,1,0:T(8,128)(2,1)S(1)} %collective-permute-done.4.b, f32[4,8,128]{2,1,0:T(8,128)S(1)} %get-tuple-element.65.p), custom_call_target="tpu_custom_call", output_to_operand_aliasing={{0}: (0, {})} | custom-call | tf_op jit(solution)/shard_map/product_b/pallas_call | solution.py:385
  59.1 8.0 %all-to-all-start.1 = ((f32[128,4,128]{2,1,0:T(4,128)}), f32[128,4,128]{2,1,0:T(4,128)S(1)}, u32[]{:S(2)}, u32[]{:S(2)}) async-start(f32[128,4,128]{2,1,0:T(4,128)} %get-tuple-element.68), calls=%async_computation.1 | async-start | bytes 524288 | tf_op jit(solution)/shard_map/all_to_all | solution.py:486
  67.1 8.4 %dense.1 = (f32[768,2048]{1,0:T(8,128)}, f32[2048,128]{1,0:T(8,128)S(1)}) custom-call(s32[2048]{0:T(1024)S(1)} %multiply_add_fusion.slot_ref, f32[4096,128]{1,0:T(8,128)S(1)} %get-tuple-element.70.q_ref, f32[768,2048]{1,0:T(8,128)} %x_hbm, f32[768,2048]{1,0:T(8,128)} %s_hbm), custom_call_target="tpu_custom_call" | custom-call | tf_op jit(solution)/shard_map/dense/pallas_call | solution.py:142
  75.5 2.6 %all-to-all-done.1.red_ref = f32[128,4,128]{2,1,0:T(4,128)S(1)} async-done(((f32[128,4,128]{2,1,0:T(4,128)}), f32[128,4,128]{2,1,0:T(4,128)S(1)}, u32[]{:S(2)}, u32[]{:S(2)}) %all-to-all-start.1) | async-done | bytes 262176 | tf_op jit(solution)/shard_map/all_to_all | solution.py:486
  78.1 3.6 %final.1 = (f32[768,2048]{1,0:T(8,128)}, f32[2048,128]{1,0:T(8,128)}, f32[2048,128]{1,0:T(8,128)}) custom-call(f32[128,4,128]{2,1,0:T(4,128)S(1)} %all-to-all-done.1.red_ref, f32[2048,128]{1,0:T(8,128)} %get-tuple-element.69.r_hbm, f32[2048,128]{1,0:T(8,128)S(1)} %get-tuple-element.73.q_ref, ...), custom_call_target="tpu_custom_call", output_to_operand_aliasing={{0}: (5, {})} | custom-call | tf_op jit(solution)/shard_map/final/pallas_call | solution.py:441
  (5 shorter events, 0.1 us)
Async XLA Ops:
  3.4 50.0 %all-to-all-start = ((bf16[64,72,128]{2,1,0:T(8,128)(2,1)}), bf16[64,72,128]{2,1,0:T(8,128)(2,1)S(1)}, u32[]{:S(2)}, u32[]{:S(2)}) async-start(bf16[64,72,128]{2,1,0:T(8,128)(2,1)} %get-tuple-element.40), calls=%async_computation | async-start | bytes 2359296 | tf_op jit(solution)/shard_map/all_to_all | solution.py:453
  15.4 4.3 %collective-permute-start = (f32[4,2048]{1,0:T(4,128)S(1)}, f32[4,2048]{1,0:T(4,128)S(1)}, u32[]{:S(2)}, u32[]{:S(2)}) collective-permute-start(f32[4,2048]{1,0:T(4,128)S(1)} %get-tuple-element.41), channel_id=1, source_target_pairs={{0,8},{8,16},{16,24},{24,32},{32,40},{40,48},{48,56},{56,64},{64,7... | collective-permute-start | bytes 98312 | tf_op jit(solution)/shard_map/ppermute | solution.py:457
  18.3 6.4 %collective-permute-start.1 = (f32[4,2048]{1,0:T(4,128)S(1)}, f32[4,2048]{1,0:T(4,128)S(1)}, u32[]{:S(2)}, u32[]{:S(2)}) collective-permute-start(f32[4,2048]{1,0:T(4,128)S(1)} %get-tuple-element.42), channel_id=1, source_target_pairs={{8,0},{16,8},{24,16},{32,24},{40,32},{48,40},{56,48},{64,56},{72,6... | collective-permute-start | bytes 98312 | tf_op jit(solution)/shard_map/ppermute | solution.py:458
  19.7 6.8 %copy-start = (s32[2048,1]{0,1:T(1,128)S(1)}, s32[2048,1]{0,1:T(1,128)}, u32[]{:S(2)}) copy-start(s32[2048,1]{0,1:T(1,128)} %param.8) | copy-start | bytes 24580
  26.6 14.2 %copy-start.1 = (s32[2048]{0:T(1024)S(1)}, s32[2048]{0:T(1024)}, u32[]{:S(2)}) copy-start(s32[2048]{0:T(1024)} %param.7) | copy-start | bytes 24580
  26.6 18.5 %collective-permute-start.2 = (f32[16,896]{1,0:T(8,128)S(1)}, f32[16,896]{1,0:T(8,128)S(1)}, u32[]{:S(2)}, u32[]{:S(2)}) collective-permute-start(f32[16,896]{1,0:T(8,128)S(1)} %get-tuple-element.58), channel_id=1, source_target_pairs={{0,1},{1,2},{2,3},{3,4},{4,5},{5,6},{6,7},{8,9},{9,10},{10,11},{11... | collective-permute-start | bytes 172040 | tf_op jit(solution)/shard_map/ppermute | solution.py:463
  37.4 7.8 %collective-permute-start.3 = (f32[16,896]{1,0:T(8,128)S(1)}, f32[16,896]{1,0:T(8,128)S(1)}, u32[]{:S(2)}, u32[]{:S(2)}) collective-permute-start(f32[16,896]{1,0:T(8,128)S(1)} %get-tuple-element.59), channel_id=1, source_target_pairs={{1,0},{2,1},{3,2},{4,3},{5,4},{6,5},{7,6},{9,8},{10,9},{11,10},{12... | collective-permute-start | bytes 172040 | tf_op jit(solution)/shard_map/ppermute | solution.py:464
  53.4 2.9 %collective-permute-start.4 = (bf16[64,72,128]{2,1,0:T(8,128)(2,1)S(1)}, bf16[64,72,128]{2,1,0:T(8,128)(2,1)S(1)}, u32[]{:S(2)}, u32[]{:S(2)}) collective-permute-start(bf16[64,72,128]{2,1,0:T(8,128)(2,1)S(1)} %all-to-all-done.b), channel_id=1, source_target_pairs={{0,1},{1,0},{2,3},{3,2},{4,5},{5,4},{6,7},{7,6},{8,9},{9,8},{10,11... | collective-permute-start | bytes 3538952 | tf_op jit(solution)/shard_map/ppermute | solution.py:482
  59.1 19.0 %all-to-all-start.1 = ((f32[128,4,128]{2,1,0:T(4,128)}), f32[128,4,128]{2,1,0:T(4,128)S(1)}, u32[]{:S(2)}, u32[]{:S(2)}) async-start(f32[128,4,128]{2,1,0:T(4,128)} %get-tuple-element.68), calls=%async_computation.1 | async-start | bytes 524288 | tf_op jit(solution)/shard_map/all_to_all | solution.py:486
